TPU v7x, 512 devices: a whole 4x8x8 slice. The times are simulated.
512 devices in a mesh: pole: 8 (over y_hi, core), sep: 64 (over y_lo, z, x).
Axes of the slice: x: 4, y: 8 (y_hi: 4, y_lo: 2; y = y_hi * 2 + y_lo), z: 8, core: 2. Of those that a mesh axis runs over, the one named last changes fastest.
Arguments:
- diag_inverse: bfloat16 [8, 512, 2, 256, 256], P('pole', 'sep'), may hold values from -6 to 6
- coupling: bfloat16 [8, 512, 2, 256, 256], P('pole', 'sep'), may hold values from -0.25 to 0.25
- ancestor_inverse: bfloat16 [8, 64, 2, 256, 256], P('pole', 'sep'), may hold values from -6 to 6
- pole_weight: float32 [8, 2], P('pole'), may hold values from -1 to 1
- ancestor_bit: int32 [512], P('sep'), may hold values from 0 to 3
- tile_blocks: int32 [64, 6], P('sep'), may hold values from 0 to 511, as said below
- tile_count: int32 [64], P('sep'), may hold values from 1 to 6
- orbital_values: bfloat16 [64, 6, 2048, 256], P('sep', None, 'pole'), may hold values from -0.375 to 0.375
Outputs:
- density_grid: float32 [64, 2048], P('sep', 'pole')
Inputs may be any that keep to these rules, and one draw needn't show every extreme that they name: `tile_blocks`: entry (t, s) names a block owned by device t - 1, t or t + 1 of sep, block b being owned by device b // 8.
All inputs are finite; a program needn't handle non-finite values.
Results may differ from a plain program's by a relative error of at most 0.0035.
Values may be sent and summed in bfloat16 or wider, within the bound.
No kernel may reach another device: no remote copies, remote signals or barrier semaphores. Data moves between devices by JAX's collectives and lax.ppermute only.
A program may use at most 64 MiB of HBM per device.

v0:
```python
import jax
import jax.numpy as jnp
from jax import lax
from jax.sharding import PartitionSpec as P

LEVELS = 4


def from_partner(x, axis, distance):
    return lax.ppermute(x, axis, [(i, i ^ 1 << distance) for i in range(lax.axis_size(axis))])


def padded(x, sides, width):
    for axis, dim in sides:
        devices, length = (lax.axis_size(axis), x.shape[dim])
        up = [(i, (i + 1) % devices) for i in range(devices - 1)]
        down = [(j, i) for i, j in up]
        last = lax.slice_in_dim(x, length - width, length, axis=dim)
        initial = lax.slice_in_dim(x, 0, width, axis=dim)
        before = lax.ppermute(last, axis, up)
        after = lax.ppermute(initial, axis, down)
        x = jnp.concatenate([before, x, after], axis=dim)
    return x


def matmul(left, right):
    return jnp.einsum("bij,bjk->bik", left, right, preferred_element_type=jnp.float32)


def matmul_t(left, right):
    return jnp.einsum("bij,bkj->bik", left, right, preferred_element_type=jnp.float32)


def shards(
    diag_inverse,
    coupling,
    ancestor_inverse,
    pole_weight,
    ancestor_bit,
    tile_blocks,
    tile_count,
    orbital_values,
):
    diag = diag_inverse[0]
    link = coupling[0]
    own_upper = ancestor_inverse[0]
    nblocks = diag.shape[0]
    chosen = jnp.zeros(diag.shape, jnp.bfloat16)
    for level in range(LEVELS):
        partner = from_partner(own_upper, "sep", level)
        chosen = jnp.where((ancestor_bit == level)[:, None, None, None], partner, chosen)
    lr, li = (link[:, 0], link[:, 1])
    gr, gi = (chosen[:, 0], chosen[:, 1])
    mr = (matmul(lr, gr) - matmul(li, gi)).astype(jnp.bfloat16)
    mi = (matmul(lr, gi) + matmul(li, gr)).astype(jnp.bfloat16)
    green_real = diag[:, 0].astype(jnp.float32) + matmul_t(mr, lr) - matmul_t(mi, li)
    green_imag = diag[:, 1].astype(jnp.float32) + matmul_t(mr, li) + matmul_t(mi, lr)
    weight = pole_weight[0]
    term = weight[0] * green_imag + weight[1] * green_real
    total = lax.psum(term, "pole").astype(jnp.bfloat16)
    near = padded(total, (("sep", 0),), nblocks)
    device = lax.axis_index("sep")
    local = tile_blocks[0] - (device - 1) * nblocks
    blocks = jnp.take(near, local, axis=0)
    values = orbital_values[0]
    inner = jnp.einsum("spw,swv->spv", values, blocks, preferred_element_type=jnp.float32)
    contribution = jnp.sum(values.astype(jnp.float32) * inner, axis=-1)
    live = (jnp.arange(values.shape[0], dtype=jnp.int32) < tile_count[0])[:, None]
    result = jnp.sum(jnp.where(live, contribution, jnp.float32(0.0)), axis=0)
    return result[None, :]


def solution(mesh):
    placed = (
        P("pole", "sep", None, None, None),
        P("pole", "sep", None, None, None),
        P("pole", "sep", None, None, None),
        P("pole", None),
        P("sep"),
        P("sep", None),
        P("sep"),
        P("sep", None, "pole", None),
    )
    return jax.shard_map(
        shards, mesh=mesh, in_specs=placed, out_specs=P("sep", "pole"), check_vma=False
    )
```

profile of v0, /device:TPU:223, one launch (start us, length us, event | category | flops | bytes accessed | tf_op | source)
XLA Modules:
  0.0 144.1 jit_solution(15881584173617389905)
XLA Ops:
  0.0 1.9 %collective-permute-start = (bf16[1,2,256,256]{3,2,1,0:T(8,128)(2,1)}, bf16[1,2,256,256]{3,2,1,0:T(8,128)(2,1)S(1)}, u32[]{:S(2)}, u32[]{:S(2)}) collective-permute-start(bf16[1,2,256,256]{3,2,1,0:T(8,128)(2,1)} %bitcast.78), channel_id=1, source_target_pairs={{0,8},{1,9},{2,10},{3,11},{4,12},{5,13},{6,14},{7,15},{8,0},{9,1},... | collective-permute-start | bytes 786440 | tf_op jit(solution)/shard_map/ppermute | solution.py:10
  1.9 1.9 %collective-permute-start.1 = (bf16[1,2,256,256]{3,2,1,0:T(8,128)(2,1)}, bf16[1,2,256,256]{3,2,1,0:T(8,128)(2,1)S(1)}, u32[]{:S(2)}, u32[]{:S(2)}) collective-permute-start(bf16[1,2,256,256]{3,2,1,0:T(8,128)(2,1)} %bitcast.79), channel_id=1, source_target_pairs={{0,4},{1,5},{2,6},{3,7},{4,0},{5,1},{6,2},{7,3},{8,12},{9,13},{10,... | collective-permute-start | bytes 786440 | tf_op jit(solution)/shard_map/ppermute | solution.py:10
  3.8 3.0 %collective-permute-start.2 = (bf16[1,2,256,256]{3,2,1,0:T(8,128)(2,1)}, bf16[1,2,256,256]{3,2,1,0:T(8,128)(2,1)S(1)}, u32[]{:S(2)}, u32[]{:S(2)}) collective-permute-start(bf16[1,2,256,256]{3,2,1,0:T(8,128)(2,1)} %bitcast.80), channel_id=1, source_target_pairs={{0,2},{1,3},{2,0},{3,1},{4,6},{5,7},{6,4},{7,5},{8,10},{9,11},{10,... | collective-permute-start | bytes 786440 | tf_op jit(solution)/shard_map/ppermute | solution.py:10
  6.9 1.9 %collective-permute-start.3 = (bf16[1,2,256,256]{3,2,1,0:T(8,128)(2,1)}, bf16[1,2,256,256]{3,2,1,0:T(8,128)(2,1)S(1)}, u32[]{:S(2)}, u32[]{:S(2)}) collective-permute-start(bf16[1,2,256,256]{3,2,1,0:T(8,128)(2,1)} %bitcast.81), channel_id=1, source_target_pairs={{0,1},{1,0},{2,3},{3,2},{4,5},{5,4},{6,7},{7,6},{8,9},{9,8},{10,11... | collective-permute-start | bytes 786440 | tf_op jit(solution)/shard_map/ppermute | solution.py:10
  8.8 1.4 fusion.17
  10.2 0.0 copy-start.2
  10.2 1.9 %copy.45 = bf16[1,8,2,256,256]{4,3,1,2,0:T(8,128)(2,1)S(1)} copy(bf16[1,8,2,256,256]{4,3,2,1,0:T(8,128)(2,1)} %param.9) | data formatting | bytes 4194304 | tf_op args[1]
  12.1 0.3 copy-done.2
  12.4 0.0 copy-start.5
  12.4 1.5 %copy.46 = bf16[1,8,2,256,256]{4,3,1,2,0:T(8,128)(2,1)} copy(bf16[1,8,2,256,256]{4,3,2,1,0:T(8,128)(2,1)S(1)} %copy-done.2) | data formatting | bytes 4194304 | tf_op args[0]
  13.9 0.0 copy-done.5
  13.9 2.0 %collective-permute-done = bf16[1,2,256,256]{3,2,1,0:T(8,128)(2,1)S(1)} collective-permute-done((bf16[1,2,256,256]{3,2,1,0:T(8,128)(2,1)}, bf16[1,2,256,256]{3,2,1,0:T(8,128)(2,1)S(1)}, u32[]{:S(2)}, u32[]{:S(2)}) %collective-permute-start) | collective-permute-done | bytes 262176 | tf_op jit(solution)/shard_map/ppermute | solution.py:10
  16.0 0.1 copy.24
  16.1 0.6 collective-permute-done.1
  16.7 0.1 copy.25
  16.9 0.0 collective-permute-done.2
  16.9 0.1 copy.26
  17.0 1.0 collective-permute-done.3
  18.1 0.1 copy.27
  18.2 0.6 select_select_fusion
  18.8 0.5 fusion.7
  19.3 0.5 fusion.6
  19.8 0.5 subtract_convert_fusion
  20.3 0.5 fusion.13
  20.8 0.5 fusion.11
  21.3 0.5 add_convert_fusion
  21.8 0.0 copy-start
  21.8 0.5 fusion.12
  22.3 1.1 copy-done
  23.4 3.5 %fusion.2 = f32[8,256,256]{2,1,0:T(8,128)} fusion(f32[8,256,256]{2,1,0:T(8,128)S(1)} %fusion.11, f32[8,256,256]{2,1,0:T(8,128)S(1)} %fusion.12, f32[8,256,256]{2,1,0:T(8,128)S(1)} %fusion.13, bf16[8,256,256]{2,1,0:T(8,128)(2,1)S(1)} %add_convert_fusion, bf16[8,2,256,256]{3,2,0,1:T(8,128)(2,1)S(1)} %bitcast.73, f32[]{:T(128)} %bitcast.16, f32[]{:T(128)} %bitcast.3, ...), kind=kOutput, calls=%fused_computation.5 | convolution fusion | flops 273154048 | bytes 12582920 | tf_op jit(solution)/shard_map/bij,bkj->bik/dot_general | solution.py:31
  26.9 0.0 copy-start.4
  26.9 0.0 copy-start.6
  26.9 72.2 %all-reduce.1 = bf16[8,256,256]{2,1,0:T(8,128)(2,1)S(1)} all-reduce(f32[8,256,256]{2,1,0:T(8,128)} %fusion.2), channel_id=1, replica_groups=mesh['pole'=8,'sep'=64] {'pole'}, use_global_device_ids=true, to_apply=%region_0.1 | all-reduce | flops 524288 | bytes 3145728 | tf_op jit(solution)/shard_map/psum | solution.py:60
  99.2 0.0 copy-start.1
  99.2 9.5 %collective-permute-start.4 = (bf16[8,256,256]{2,1,0:T(8,128)(2,1)S(1)}, bf16[8,256,256]{2,1,0:T(8,128)(2,1)S(1)}, u32[]{:S(2)}, u32[]{:S(2)}) collective-permute-start(bf16[8,256,256]{2,1,0:T(8,128)(2,1)S(1)} %all-reduce.1), channel_id=1, source_target_pairs={{0,1},{1,2},{2,3},{3,4},{4,5},{5,6},{6,7},{7,8},{8,9},{9,10},{10,1... | collective-permute-start | bytes 3145736 | tf_op jit(solution)/shard_map/ppermute | solution.py:20
  108.7 1.9 %collective-permute-start.5 = (bf16[8,256,256]{2,1,0:T(8,128)(2,1)S(1)}, bf16[8,256,256]{2,1,0:T(8,128)(2,1)}, u32[]{:S(2)}, u32[]{:S(2)}) collective-permute-start(bf16[8,256,256]{2,1,0:T(8,128)(2,1)S(1)} %all-reduce.1), channel_id=1, source_target_pairs={{1,0},{2,1},{3,2},{4,3},{5,4},{6,5},{7,6},{8,7},{9,8},{10,9},{11,1... | collective-permute-start | bytes 3145736 | tf_op jit(solution)/shard_map/ppermute | solution.py:21
  110.6 0.0 copy-done.4
  110.6 1.2 copy.22
  112.5 0.0 copy-done.6
  112.5 17.7 %collective-permute-done.4 = bf16[8,256,256]{2,1,0:T(8,128)(2,1)S(1)} collective-permute-done((bf16[8,256,256]{2,1,0:T(8,128)(2,1)S(1)}, bf16[8,256,256]{2,1,0:T(8,128)(2,1)S(1)}, u32[]{:S(2)}, u32[]{:S(2)}) %collective-permute-start.4) | collective-permute-done | bytes 1048608 | tf_op jit(solution)/shard_map/ppermute | solution.py:20
  130.2 0.0 copy-done.1
  130.2 0.0 copy-start.3
  130.2 1.0 copy-done.3
  131.2 6.5 %collective-permute-done.5 = bf16[8,256,256]{2,1,0:T(8,128)(2,1)} collective-permute-done((bf16[8,256,256]{2,1,0:T(8,128)(2,1)S(1)}, bf16[8,256,256]{2,1,0:T(8,128)(2,1)}, u32[]{:S(2)}, u32[]{:S(2)}) %collective-permute-start.5) | collective-permute-done | bytes 1048608 | tf_op jit(solution)/shard_map/ppermute | solution.py:21
  137.8 2.0 %pad_maximum_fusion = bf16[24,256,256]{2,1,0:T(8,128)(2,1)S(1)} fusion(bf16[8,256,256]{2,1,0:T(8,128)(2,1)} %collective-permute-done.5, bf16[8,256,256]{2,1,0:T(8,128)(2,1)} %copy-done.1, bf16[8,256,256]{2,1,0:T(8,128)(2,1)} %copy-done.3), kind=kLoop, calls=%fused_computation.1 | loop fusion | flops 3145728 | bytes 6291456 | tf_op jit(solution)/shard_map/concatenate | solution.py:22
  139.8 1.5 %gather_fusion = bf16[6,256,256]{2,1,0:T(8,128)(2,1)} fusion(bf16[24,256,256]{2,1,0:T(8,128)(2,1)S(1)} %pad_maximum_fusion, s32[1024]{0:T(1024)S(1)} %pad_clamp_fusion), kind=kCustom, calls=%fused_computation | custom fusion | bytes 1572888 | tf_op jit(solution)/shard_map/jit(_take)/gather | solution.py:64
  141.3 2.1 %fusion.5 = f32[6,256]{1,0:T(8,128)S(1)} fusion(bf16[1,6,256,256]{3,2,1,0:T(8,128)(2,1)} %param.15, bf16[1,6,256,256]{2,3,1,0:T(8,128)(2,1)} %copy.22, bf16[6,256,256]{2,1,0:T(8,128)(2,1)} %gather_fusion, pred[6]{0:T(512)(128)(4,1)S(1)} %compare_and_fusion), kind=kOutput, calls=%fused_computation.15 | convolution fusion | flops 202897920 | bytes 2365446 | tf_op jit(solution)/shard_map/spw,swv->spv/dot_general | solution.py:66
  143.4 0.6 select_reduce_fusion
  (5 shorter events, 0.0 us)
Async XLA Ops:
  0.0 16.0 %collective-permute-start = (bf16[1,2,256,256]{3,2,1,0:T(8,128)(2,1)}, bf16[1,2,256,256]{3,2,1,0:T(8,128)(2,1)S(1)}, u32[]{:S(2)}, u32[]{:S(2)}) collective-permute-start(bf16[1,2,256,256]{3,2,1,0:T(8,128)(2,1)} %bitcast.78), channel_id=1, source_target_pairs={{0,8},{1,9},{2,10},{3,11},{4,12},{5,13},{6,14},{7,15},{8,0},{9,1},... | collective-permute-start | bytes 786440 | tf_op jit(solution)/shard_map/ppermute | solution.py:10
  1.9 14.8 %collective-permute-start.1 = (bf16[1,2,256,256]{3,2,1,0:T(8,128)(2,1)}, bf16[1,2,256,256]{3,2,1,0:T(8,128)(2,1)S(1)}, u32[]{:S(2)}, u32[]{:S(2)}) collective-permute-start(bf16[1,2,256,256]{3,2,1,0:T(8,128)(2,1)} %bitcast.79), channel_id=1, source_target_pairs={{0,4},{1,5},{2,6},{3,7},{4,0},{5,1},{6,2},{7,3},{8,12},{9,13},{10,... | collective-permute-start | bytes 786440 | tf_op jit(solution)/shard_map/ppermute | solution.py:10
  3.8 13.0 %collective-permute-start.2 = (bf16[1,2,256,256]{3,2,1,0:T(8,128)(2,1)}, bf16[1,2,256,256]{3,2,1,0:T(8,128)(2,1)S(1)}, u32[]{:S(2)}, u32[]{:S(2)}) collective-permute-start(bf16[1,2,256,256]{3,2,1,0:T(8,128)(2,1)} %bitcast.80), channel_id=1, source_target_pairs={{0,2},{1,3},{2,0},{3,1},{4,6},{5,7},{6,4},{7,5},{8,10},{9,11},{10,... | collective-permute-start | bytes 786440 | tf_op jit(solution)/shard_map/ppermute | solution.py:10
  6.9 11.2 %collective-permute-start.3 = (bf16[1,2,256,256]{3,2,1,0:T(8,128)(2,1)}, bf16[1,2,256,256]{3,2,1,0:T(8,128)(2,1)S(1)}, u32[]{:S(2)}, u32[]{:S(2)}) collective-permute-start(bf16[1,2,256,256]{3,2,1,0:T(8,128)(2,1)} %bitcast.81), channel_id=1, source_target_pairs={{0,1},{1,0},{2,3},{3,2},{4,5},{5,4},{6,7},{7,6},{8,9},{9,8},{10,11... | collective-permute-start | bytes 786440 | tf_op jit(solution)/shard_map/ppermute | solution.py:10
  10.2 2.2 %copy-start.2 = (bf16[1,8,2,256,256]{4,3,2,1,0:T(8,128)(2,1)S(1)}, bf16[1,8,2,256,256]{4,3,2,1,0:T(8,128)(2,1)}, u32[]{:S(2)}) copy-start(bf16[1,8,2,256,256]{4,3,2,1,0:T(8,128)(2,1)} %param.8) | copy-start | bytes 6291460
  12.4 1.5 %copy-start.5 = (s32[8]{0:T(128)S(1)}, s32[8]{0:T(128)}, u32[]{:S(2)}) copy-start(s32[8]{0:T(128)} %param.12) | copy-start | bytes 100
  21.8 1.6 %copy-start = (bf16[1,8,2,256,256]{4,3,1,2,0:T(8,128)(2,1)S(1)}, bf16[1,8,2,256,256]{4,3,1,2,0:T(8,128)(2,1)}, u32[]{:S(2)}) copy-start(bf16[1,8,2,256,256]{4,3,1,2,0:T(8,128)(2,1)} %copy.46) | copy-start | bytes 6291460
  26.9 83.7 %copy-start.4 = (bf16[1,6,256,256]{3,2,1,0:T(8,128)(2,1)S(1)}, bf16[1,6,256,256]{3,2,1,0:T(8,128)(2,1)}, u32[]{:S(2)}) copy-start(bf16[1,6,256,256]{3,2,1,0:T(8,128)(2,1)} %param.15) | copy-start | bytes 2359300
  26.9 85.5 %copy-start.6 = (s32[1,6]{1,0:T(1,128)S(1)}, s32[1,6]{1,0:T(1,128)}, u32[]{:S(2)}) copy-start(s32[1,6]{1,0:T(1,128)} %param.13) | copy-start | bytes 76
  99.2 31.1 %copy-start.1 = (bf16[8,256,256]{2,1,0:T(8,128)(2,1)}, bf16[8,256,256]{2,1,0:T(8,128)(2,1)S(1)}, u32[]{:S(2)}) copy-start(bf16[8,256,256]{2,1,0:T(8,128)(2,1)S(1)} %all-reduce.1) | copy-start | bytes 3145732
  99.2 31.0 %collective-permute-start.4 = (bf16[8,256,256]{2,1,0:T(8,128)(2,1)S(1)}, bf16[8,256,256]{2,1,0:T(8,128)(2,1)S(1)}, u32[]{:S(2)}, u32[]{:S(2)}) collective-permute-start(bf16[8,256,256]{2,1,0:T(8,128)(2,1)S(1)} %all-reduce.1), channel_id=1, source_target_pairs={{0,1},{1,2},{2,3},{3,4},{4,5},{5,6},{6,7},{7,8},{8,9},{9,10},{10,1... | collective-permute-start | bytes 3145736 | tf_op jit(solution)/shard_map/ppermute | solution.py:20
  108.7 29.1 %collective-permute-start.5 = (bf16[8,256,256]{2,1,0:T(8,128)(2,1)S(1)}, bf16[8,256,256]{2,1,0:T(8,128)(2,1)}, u32[]{:S(2)}, u32[]{:S(2)}) collective-permute-start(bf16[8,256,256]{2,1,0:T(8,128)(2,1)S(1)} %all-reduce.1), channel_id=1, source_target_pairs={{1,0},{2,1},{3,2},{4,3},{5,4},{6,5},{7,6},{8,7},{9,8},{10,9},{11,1... | collective-permute-start | bytes 3145736 | tf_op jit(solution)/shard_map/ppermute | solution.py:21
  130.2 1.0 copy-start.3
where the time goes:
time: 144 us
  blocking collectives  72.2 us (50%)
  waiting for transfers between devices  28 us (19%)
  starting transfers between devices  20.2 us (14%)
  local copies, waits for them, and re-layouts  10.4 us (7%)
  matrix products  9.08 us (6%)
  other arithmetic  3.33 us (2%)
    psum x1, blocking collectives, shards(): total = lax.psum(term, 'pole').astype(jnp.bfloat16)  72.2 us
    ppermute x1, waiting for transfers between devices, padded(): before = lax.ppermute(last, axis, up)  17.7 us
    ppermute x1, starting transfers between devices, padded(): before = lax.ppermute(last, axis, up)  9.49 us
    ppermute x4, starting transfers between devices, from_partner(): lax.ppermute(x, axis, [(i, i ^ 1 << distance) for i in range(lax.axis_siz...  8.78 us
    unnamed x17, local copies, waits for them, and re-layouts  6.97 us
    ppermute x1, waiting for transfers between devices, padded(): after = lax.ppermute(initial, axis, down)  6.52 us
    dot_general x4, matrix products, matmul_t(): jnp.einsum('bij,bkj->bik', left, right, preferred_element_type=jnp.float32)  5.04 us
    ppermute x4, waiting for transfers between devices, from_partner(): lax.ppermute(x, axis, [(i, i ^ 1 << distance) for i in range(lax.axis_siz...  3.72 us
  transfers between devices with their start and end apart: 6, of which 5 were waited for; matrix products, arithmetic and copies ran while one was open for 4% of the time, Pallas kernels for 0%

commit v1 on v0

v1 whole, which is shorter than its diff:
```python
import jax
import jax.numpy as jnp
from jax import lax
from jax.experimental import pallas as pl
from jax.experimental.pallas import tpu as pltpu
from jax.sharding import Mesh, PartitionSpec as P

LEVELS = 4
HALF = 128
F32 = jnp.float32
BF16 = jnp.bfloat16
SMEM = pl.BlockSpec(memory_space=pltpu.SMEM)
VMEM = pl.BlockSpec(memory_space=pltpu.VMEM)


def iotas():
    row = lax.broadcasted_iota(jnp.int32, (HALF, HALF), 0)
    col = lax.broadcasted_iota(jnp.int32, (HALF, HALF), 1)
    return row, col


def packed(t):
    row, col = iotas()
    t00, t01 = t[:HALF, :HALF], t[:HALF, HALF:]
    t10, t11 = t[HALF:, :HALF], t[HALF:, HALF:]
    here = jnp.where(col >= row, t00, t11)
    there = jnp.where(col > row, t11, jnp.where(col < row, t00, 0.0))
    diagonal = jnp.sum(jnp.where(col == row, t11, 0.0), axis=0, keepdims=True)
    return here + there.T, t01 + t10.T, diagonal


def weigh_kernel(nblocks, weight, diag, tiles, rows):
    for b in range(nblocks):
        t = weight[0, 0] * diag[b, 1].astype(F32) + weight[0, 1] * diag[b, 0].astype(F32)
        first, second, diagonal = packed(t)
        tiles[b, 0] = first
        tiles[b, 1] = second
        rows[pl.ds(b, 1), :] = diagonal


def dot(left, right):
    return lax.dot_general(left, right, (((1,), (0,)), ((), ())), preferred_element_type=F32)


def dot_t(left, right):
    return lax.dot_general(left, right, (((1,), (1,)), ((), ())), preferred_element_type=F32)


def term_kernel(nblocks, bit, core, weight, link, up0, up1, up2, up3, tiles, rows, keep, send, pair):
    for level, up in enumerate((up0, up1, up2, up3)):
        pair[level, 0, :, :256] = up[0]
        pair[level, 0, :, 256:] = up[1]
        pair[level, 1, :, :256] = -up[1]
        pair[level, 1, :, 256:] = up[0]
    first_core = core[0] == 0

    def one(b, carry):
        level = bit[b]
        lr, li = link[b, 0], link[b, 1]
        middle = (dot(lr, pair[level, 0]) + dot(li, pair[level, 1])).astype(BF16)
        mr, mi = middle[:, :256], middle[:, 256:]
        real = dot_t(mr, lr) - dot_t(mi, li)
        imag = dot_t(mr, li) + dot_t(mi, lr)
        first, second, diagonal = packed(weight[0, 0] * imag + weight[0, 1] * real)
        first = first + tiles[b, 0]
        second = second + tiles[b, 1]
        at = pl.ds(pl.multiple_of(b * HALF, HALF), HALF)
        keep[at, :] = jnp.where(first_core, first, second)
        send[at, :] = jnp.where(first_core, second, first)
        own = pl.ds(nblocks * HALF + b, 1)
        keep[own, :] = diagonal + rows[pl.ds(b, 1), :]
        return carry

    lax.fori_loop(0, nblocks, one, 0)
    tail = pl.ds(nblocks * HALF, nblocks)
    send[tail, :] = keep[tail, :]
    rest = pl.ds(nblocks * HALF + nblocks, 8)
    keep[rest, :] = jnp.zeros((8, HALF), F32)
    send[rest, :] = jnp.zeros((8, HALF), F32)


def pick_kernel(nblocks, slots, where, before, own, after, out):
    position = lax.broadcasted_iota(jnp.int32, (16, HALF), 0)
    tail = pl.ds(nblocks * HALF, 16)
    diagonals = jnp.zeros((16, HALF), F32)
    for s in range(slots):
        side, b = where[s] // nblocks, where[s] % nblocks
        at = pl.ds(pl.multiple_of(b * HALF, HALF), HALF)
        for k, source in enumerate((before, own, after)):

            @pl.when(side == k)
            def _():
                tile = source[at, :]
                for y in range(out.shape[0]):
                    out[y, pl.ds(s * HALF, HALF), :] = tile

        edge = jnp.where(side == 0, before[tail, :], jnp.where(side == 1, own[tail, :], after[tail, :]))
        line = jnp.sum(jnp.where(position == b, edge.astype(F32), 0.0), axis=0, keepdims=True)
        diagonals = jnp.where(position == s, line, diagonals)
    for y in range(out.shape[0]):
        out[y, pl.ds(slots * HALF, 16), :] = diagonals.astype(BF16)


def grid_kernel(slots, core, count, own, other, values, out):
    row, col = iotas()
    first_core = core[0] == 0
    total = jnp.zeros(values.shape[1:], F32)
    for s in range(slots):
        at = pl.ds(s * HALF, HALF)
        mine, theirs = own[at, :], other[at, :]
        first = jnp.where(first_core, mine, theirs)
        second = jnp.where(first_core, theirs, mine)
        line = own[pl.ds(slots * HALF + s, 1), :]
        upper = jnp.where(col >= row, first, 0.0)
        lower = jnp.where(col < row, first, jnp.where(col == row, line, 0.0))
        top = jnp.concatenate([upper, second], axis=1)
        bottom = jnp.concatenate([jnp.zeros_like(lower), lower], axis=1)
        block = jnp.concatenate([top, bottom], axis=0).astype(BF16)
        v = values[s]
        inner = dot(v, block)
        total = total + jnp.where(s < count[0], v.astype(F32) * inner, 0.0)
    narrow = total[:, :HALF] + total[:, HALF:]
    for k in range(narrow.shape[0] // HALF):
        piece = narrow[k * HALF : (k + 1) * HALF].T
        out[:, k * HALF : (k + 1) * HALF] = jnp.sum(piece, axis=0, keepdims=True)


def call(kernel, out_shape, in_specs, scratch=(), flops=0, moved=0):
    out_specs = jax.tree.map(lambda _: VMEM, out_shape)
    return pl.pallas_call(
        kernel,
        out_shape=out_shape,
        in_specs=in_specs,
        out_specs=out_specs,
        scratch_shapes=list(scratch),
        cost_estimate=pl.CostEstimate(flops=flops, bytes_accessed=moved, transcendentals=0),
    )


def shape(dims, dtype):
    return jax.ShapeDtypeStruct(dims, dtype)


def shards(
    diag_inverse,
    coupling,
    ancestor_inverse,
    pole_weight,
    ancestor_bit,
    tile_blocks,
    tile_count,
    orbital_values,
):
    diag, link, own_upper = diag_inverse[0], coupling[0], ancestor_inverse[0, 0]
    nblocks, slots = diag.shape[0], orbital_values.shape[1]
    nsep, groups = lax.axis_size("sep"), lax.axis_size("yh")
    core = lax.axis_index("core").astype(jnp.int32).reshape(1)
    swap = [(0, 1), (1, 0)]

    uppers = [lax.ppermute(own_upper, "sep", [(i, i ^ 1 << k) for i in range(nsep)]) for k in range(LEVELS)]
    tiles, rows = call(
        lambda *refs: weigh_kernel(nblocks, *refs),
        (shape((nblocks, 2, HALF, HALF), F32), shape((nblocks, HALF), F32)),
        [SMEM, VMEM],
        flops=2_000_000,
        moved=3_200_000,
    )(pole_weight, diag)

    length = nblocks * HALF + 16
    keep, send = call(
        lambda *refs: term_kernel(nblocks, *refs),
        (shape((length, HALF), F32), shape((length, HALF), F32)),
        [SMEM, SMEM, SMEM] + [VMEM] * 7,
        [pltpu.VMEM((LEVELS, 2, 256, 512), BF16)],
        flops=2_100_000_000,
        moved=5_000_000,
    )(ancestor_bit, core, pole_weight, link, *uppers, tiles, rows)
    chip = (keep + lax.ppermute(send, "core", swap)).astype(BF16)

    before = lax.ppermute(chip, "sep", [(i, i + 1) for i in range(nsep - 1)])
    after = lax.ppermute(chip, "sep", [(i + 1, i) for i in range(nsep - 1)])
    where = tile_blocks[0] - (lax.axis_index("sep") - 1) * nblocks
    picked = call(
        lambda *refs: pick_kernel(nblocks, slots, *refs),
        shape((groups, slots * HALF + 16, HALF), BF16),
        [SMEM] + [VMEM] * 3,
        moved=1_500_000,
    )(where, before, chip, after)
    parts = lax.all_to_all(picked, "yh", 0, 0, tiled=True)
    own = jnp.sum(parts.astype(F32), axis=0)
    other = lax.ppermute(own, "core", swap)
    return call(
        lambda *refs: grid_kernel(slots, *refs),
        shape((1, orbital_values.shape[2]), F32),
        [SMEM, SMEM] + [VMEM] * 3,
        flops=200_000_000,
        moved=1_600_000,
    )(core, tile_count, own, other, orbital_values[0])


def solution(mesh):
    pole, sep = mesh.shape["pole"], mesh.shape["sep"]
    split = Mesh(mesh.devices.reshape(pole // 2, 2, sep), ("yh", "core", "sep"))
    poles = ("yh", "core")
    placed = (
        P(poles, "sep", None, None, None),
        P(poles, "sep", None, None, None),
        P(poles, "sep", None, None, None),
        P(poles, None),
        P("sep"),
        P("sep", None),
        P("sep"),
        P("sep", None, poles, None),
    )
    return jax.shard_map(shards, mesh=split, in_specs=placed, out_specs=P("sep", poles), check_vma=False)
```

time: 144 us -> 100 us (0.69)
  the two profiles are of different devices: /device:TPU:223 before, /device:TPU:199 now
where the time goes in v1:
time: 100 us; the launch traced here: 99.6 us
  starting transfers between devices  28.4 us (28%)
  blocking collectives  27.6 us (28%)
  waiting for transfers between devices  22.6 us (23%)
  Pallas kernels  16.5 us (16%)
  local copies, waits for them, and re-layouts  2.15 us (2%)
  other arithmetic  1.72 us (2%)
    all_to_all x1, blocking collectives, shards(): parts = lax.all_to_all(picked, 'yh', 0, 0, tiled=True)  27.6 us
    ppermute x4, waiting for transfers between devices, shards(): lax.ppermute(own_upper, 'sep', [(i, i ^ 1 << k) for i in range(nsep)])  10.1 us
    ppermute x4, starting transfers between devices, shards(): lax.ppermute(own_upper, 'sep', [(i, i ^ 1 << k) for i in range(nsep)])  9.02 us
    pallas_call x1, Pallas kernels, shards(): call(lambda *refs: term_kernel(nblocks, *refs), (shape((length, HALF), F3...  8.63 us
    ppermute x1, starting transfers between devices, shards(): before = lax.ppermute(chip, 'sep', [(i, i + 1) for i in range(nsep - 1)])  8.59 us
    ppermute x1, waiting for transfers between devices, shards(): after = lax.ppermute(chip, 'sep', [(i + 1, i) for i in range(nsep - 1)])  7.15 us
    ppermute x1, starting transfers between devices, shards(): other = lax.ppermute(own, 'core', swap)  4.74 us
    ppermute x1, starting transfers between devices, shards(): chip = (keep + lax.ppermute(send, 'core', swap)).astype(BF16)  4.09 us
  transfers between devices with their start and end apart: 8, of which 7 were waited for; matrix products, arithmetic and copies ran while one was open for 1% of the time, Pallas kernels for 3%

profile of v1, /device:TPU:199, one launch (start us, length us, event | category | flops | bytes accessed | tf_op | source)
XLA Modules:
  0.0 99.6 jit_solution(13968946484532287255)
XLA Ops:
  0.0 2.4 %collective-permute-start = (bf16[2,256,256]{2,1,0:T(8,128)(2,1)}, bf16[2,256,256]{2,1,0:T(8,128)(2,1)S(1)}, u32[]{:S(2)}, u32[]{:S(2)}) collective-permute-start(bf16[2,256,256]{2,1,0:T(8,128)(2,1)} %bitcast.10), channel_id=1, source_target_pairs={{0,1},{1,0},{2,3},{3,2},{4,5},{5,4},{6,7},{7,6},{8,9},{9,8},{10,11... | collective-permute-start | bytes 786440 | tf_op jit(solution)/shard_map/ppermute | solution.py:160
  2.5 2.7 %collective-permute-start.1 = (bf16[2,256,256]{2,1,0:T(8,128)(2,1)}, bf16[2,256,256]{2,1,0:T(8,128)(2,1)S(1)}, u32[]{:S(2)}, u32[]{:S(2)}) collective-permute-start(bf16[2,256,256]{2,1,0:T(8,128)(2,1)} %bitcast.11), channel_id=1, source_target_pairs={{0,2},{1,3},{2,0},{3,1},{4,6},{5,7},{6,4},{7,5},{8,10},{9,11},{10,... | collective-permute-start | bytes 786440 | tf_op jit(solution)/shard_map/ppermute | solution.py:160
  5.2 1.9 %collective-permute-start.2 = (bf16[2,256,256]{2,1,0:T(8,128)(2,1)}, bf16[2,256,256]{2,1,0:T(8,128)(2,1)S(1)}, u32[]{:S(2)}, u32[]{:S(2)}) collective-permute-start(bf16[2,256,256]{2,1,0:T(8,128)(2,1)} %bitcast.12), channel_id=1, source_target_pairs={{0,4},{1,5},{2,6},{3,7},{4,0},{5,1},{6,2},{7,3},{8,12},{9,13},{10,... | collective-permute-start | bytes 786440 | tf_op jit(solution)/shard_map/ppermute | solution.py:160
  7.1 1.9 %collective-permute-start.3 = (bf16[2,256,256]{2,1,0:T(8,128)(2,1)}, bf16[2,256,256]{2,1,0:T(8,128)(2,1)S(1)}, u32[]{:S(2)}, u32[]{:S(2)}) collective-permute-start(bf16[2,256,256]{2,1,0:T(8,128)(2,1)} %bitcast.13), channel_id=1, source_target_pairs={{0,8},{1,9},{2,10},{3,11},{4,12},{5,13},{6,14},{7,15},{8,0},{9,1},... | collective-permute-start | bytes 786440 | tf_op jit(solution)/shard_map/ppermute | solution.py:160
  9.1 3.2 %shard_map.82 = (f32[8,2,128,128]{3,2,1,0:T(8,128)}, f32[8,128]{1,0:T(8,128)}) custom-call(f32[1,2]{1,0:T(1,128)} %refs_2_.1, bf16[8,2,256,256]{3,2,1,0:T(8,128)(2,1)} %bitcast.7), custom_call_target="tpu_custom_call" | custom-call | flops 2000000 | bytes 3200000 | tf_op jit(solution)/shard_map/pallas_call | solution.py:161
  12.2 0.0 collective-permute-done.refs_4_
  12.2 0.0 copy-start.5
  12.2 2.6 %collective-permute-done.1.refs_5_ = bf16[2,256,256]{2,1,0:T(8,128)(2,1)S(1)} collective-permute-done((bf16[2,256,256]{2,1,0:T(8,128)(2,1)}, bf16[2,256,256]{2,1,0:T(8,128)(2,1)S(1)}, u32[]{:S(2)}, u32[]{:S(2)}) %collective-permute-start.1) | collective-permute-done | bytes 262176 | tf_op jit(solution)/shard_map/ppermute | solution.py:160
  14.8 0.0 copy-start.6
  14.8 1.3 %collective-permute-done.2.refs_6_ = bf16[2,256,256]{2,1,0:T(8,128)(2,1)S(1)} collective-permute-done((bf16[2,256,256]{2,1,0:T(8,128)(2,1)}, bf16[2,256,256]{2,1,0:T(8,128)(2,1)S(1)}, u32[]{:S(2)}, u32[]{:S(2)}) %collective-permute-start.2) | collective-permute-done | bytes 262176 | tf_op jit(solution)/shard_map/ppermute | solution.py:160
  16.1 0.0 copy-start.7
  16.1 6.2 %collective-permute-done.3.refs_7_ = bf16[2,256,256]{2,1,0:T(8,128)(2,1)S(1)} collective-permute-done((bf16[2,256,256]{2,1,0:T(8,128)(2,1)}, bf16[2,256,256]{2,1,0:T(8,128)(2,1)S(1)}, u32[]{:S(2)}, u32[]{:S(2)}) %collective-permute-start.3) | collective-permute-done | bytes 262176 | tf_op jit(solution)/shard_map/ppermute | solution.py:160
  22.3 0.0 copy-start.8
  22.3 0.0 copy-done.5
  22.3 0.0 copy-done.6
  22.3 0.0 copy-done.7
  22.3 0.7 copy-done.8
  23.0 0.0 copy-start.9
  23.0 8.6 %shard_map.83 = (f32[1040,128]{1,0:T(8,128)}, f32[1040,128]{1,0:T(8,128)}) custom-call(s32[8]{0:T(128)} %refs_0_.3, s32[1]{0:T(128)} %bitcast.refs_1_.refs_0_, f32[1,2]{1,0:T(1,128)} %refs_2_.1, bf16[8,2,256,256]{3,2,1,0:T(8,128)(2,1)} %bitcast.9, bf16[2,256,256]{2,1,0:T(8,128)(2,1)} %copy-done.5, bf16[2,256,256]{2,1,0:T(8,128)(2,1)} %copy-done.6, ...), custom_call_target="tpu_custom_call" | custom-call | flops 2100000000 | bytes 5000000 | tf_op jit(solution)/shard_map/pallas_call | solution.py:170
  31.6 4.1 %collective-permute-start.4 = (f32[1040,128]{1,0:T(8,128)}, f32[1040,128]{1,0:T(8,128)S(1)}, u32[]{:S(2)}, u32[]{:S(2)}) collective-permute-start(f32[1040,128]{1,0:T(8,128)} %get-tuple-element.12), channel_id=1, source_target_pairs={{0,64},{64,0},{1,65},{65,1},{2,66},{66,2},{3,67},{67,3},{4,68},{68... | collective-permute-start | bytes 1597448 | tf_op jit(solution)/shard_map/ppermute | solution.py:178
  35.7 1.7 %collective-permute-done.4 = f32[1040,128]{1,0:T(8,128)S(1)} collective-permute-done((f32[1040,128]{1,0:T(8,128)}, f32[1040,128]{1,0:T(8,128)S(1)}, u32[]{:S(2)}, u32[]{:S(2)}) %collective-permute-start.4) | collective-permute-done | bytes 532512 | tf_op jit(solution)/shard_map/ppermute | solution.py:178
  37.5 1.1 %add_convert_fusion.refs_2_ = bf16[1040,128]{1,0:T(8,128)(2,1)S(1)} fusion(f32[1040,128]{1,0:T(8,128)} %get-tuple-element.11, f32[1040,128]{1,0:T(8,128)S(1)} %collective-permute-done.4), kind=kLoop, calls=%fused_computation.1 | loop fusion | flops 266240 | bytes 1331200 | tf_op jit(solution)/shard_map/convert_element_type | solution.py:178
  38.6 0.0 copy-start.1
  38.6 8.6 %collective-permute-start.5 = (bf16[1040,128]{1,0:T(8,128)(2,1)S(1)}, bf16[1040,128]{1,0:T(8,128)(2,1)S(1)}, u32[]{:S(2)}, u32[]{:S(2)}) collective-permute-start(bf16[1040,128]{1,0:T(8,128)(2,1)S(1)} %add_convert_fusion.refs_2_), channel_id=1, source_target_pairs={{0,1},{1,2},{2,3},{3,4},{4,5},{5,6},{6,7},{7,8},{8,9},{9,10},{10,1... | collective-permute-start | bytes 798728 | tf_op jit(solution)/shard_map/ppermute | solution.py:180
  47.2 1.9 %collective-permute-start.6 = (bf16[1040,128]{1,0:T(8,128)(2,1)S(1)}, bf16[1040,128]{1,0:T(8,128)(2,1)S(1)}, u32[]{:S(2)}, u32[]{:S(2)}) collective-permute-start(bf16[1040,128]{1,0:T(8,128)(2,1)S(1)} %add_convert_fusion.refs_2_), channel_id=1, source_target_pairs={{1,0},{2,1},{3,2},{4,3},{5,4},{6,5},{7,6},{8,7},{9,8},{10,9},{11,1... | collective-permute-start | bytes 798728 | tf_op jit(solution)/shard_map/ppermute | solution.py:181
  49.1 0.0 copy-done.9
  49.1 0.5 subtract_bitcast_fusion.refs_0_
  49.6 2.9 %collective-permute-done.5.refs_1_ = bf16[1040,128]{1,0:T(8,128)(2,1)S(1)} collective-permute-done((bf16[1040,128]{1,0:T(8,128)(2,1)S(1)}, bf16[1040,128]{1,0:T(8,128)(2,1)S(1)}, u32[]{:S(2)}, u32[]{:S(2)}) %collective-permute-start.5) | collective-permute-done | bytes 266272 | tf_op jit(solution)/shard_map/ppermute | solution.py:180
  52.5 0.0 copy-start.3
  52.5 7.1 %collective-permute-done.6.refs_3_ = bf16[1040,128]{1,0:T(8,128)(2,1)S(1)} collective-permute-done((bf16[1040,128]{1,0:T(8,128)(2,1)S(1)}, bf16[1040,128]{1,0:T(8,128)(2,1)S(1)}, u32[]{:S(2)}, u32[]{:S(2)}) %collective-permute-start.6) | collective-permute-done | bytes 266272 | tf_op jit(solution)/shard_map/ppermute | solution.py:181
  59.7 0.0 copy-done.1
  59.7 0.0 copy-done.3
  59.7 0.0 copy-start.4
  59.7 0.7 copy-done.4
  60.4 2.3 %shard_map.84 = bf16[4,784,128]{2,1,0:T(8,128)(2,1)} custom-call(s32[6]{0:T(128)} %subtract_bitcast_fusion.refs_0_, bf16[1040,128]{1,0:T(8,128)(2,1)} %copy-done.3, bf16[1040,128]{1,0:T(8,128)(2,1)} %copy-done.1, bf16[1040,128]{1,0:T(8,128)(2,1)} %copy-done.4), custom_call_target="tpu_custom_call" | custom-call | bytes 1500000 | tf_op jit(solution)/shard_map/pallas_call | solution.py:183
  62.7 27.6 %all_to_all.5 = bf16[4,784,128]{2,1,0:T(8,128)(2,1)S(1)} all-to-all(bf16[4,784,128]{2,1,0:T(8,128)(2,1)} %shard_map.84), channel_id=1, replica_groups=mesh['yh'=4,'core'=2,'sep'=64] {'yh'}, dimensions={0} | all-to-all | bytes 1605632 | tf_op jit(solution)/shard_map/all_to_all | solution.py:189
  90.3 0.1 convert_reduce_fusion.refs_2_
  90.4 0.0 copy-start
  90.4 4.7 %collective-permute-start.7 = (f32[784,128]{1,0:T(8,128)S(1)}, f32[784,128]{1,0:T(8,128)S(1)}, u32[]{:S(2)}, u32[]{:S(2)}) collective-permute-start(f32[784,128]{1,0:T(8,128)S(1)} %convert_reduce_fusion.refs_2_), channel_id=1, source_target_pairs={{0,64},{64,0},{1,65},{65,1},{2,66},{66,2},{3,67},{67,3},{4,68},{68... | collective-permute-start | bytes 1204232 | tf_op jit(solution)/shard_map/ppermute | solution.py:191
  95.8 0.7 collective-permute-done.7.refs_3_
  96.5 0.0 copy-start.2
  96.5 0.0 copy-done
  96.5 0.7 copy-done.2
  97.2 2.4 %shard_map.85 = f32[1,256]{1,0:T(1,128)} custom-call(s32[1]{0:T(128)} %bitcast.refs_1_.refs_0_, s32[1]{0:T(128)S(6)} %copy.9.refs_1_, f32[784,128]{1,0:T(8,128)} %copy-done, f32[784,128]{1,0:T(8,128)} %copy-done.2, bf16[6,256,256]{2,1,0:T(8,128)(2,1)} %bitcast.8), custom_call_target="tpu_custom_call" | custom-call | flops 200000000 | bytes 1600000 | tf_op jit(solution)/shard_map/pallas_call | solution.py:192
Async XLA Ops:
  0.0 12.2 %collective-permute-start = (bf16[2,256,256]{2,1,0:T(8,128)(2,1)}, bf16[2,256,256]{2,1,0:T(8,128)(2,1)S(1)}, u32[]{:S(2)}, u32[]{:S(2)}) collective-permute-start(bf16[2,256,256]{2,1,0:T(8,128)(2,1)} %bitcast.10), channel_id=1, source_target_pairs={{0,1},{1,0},{2,3},{3,2},{4,5},{5,4},{6,7},{7,6},{8,9},{9,8},{10,11... | collective-permute-start | bytes 786440 | tf_op jit(solution)/shard_map/ppermute | solution.py:160
  2.5 12.4 %collective-permute-start.1 = (bf16[2,256,256]{2,1,0:T(8,128)(2,1)}, bf16[2,256,256]{2,1,0:T(8,128)(2,1)S(1)}, u32[]{:S(2)}, u32[]{:S(2)}) collective-permute-start(bf16[2,256,256]{2,1,0:T(8,128)(2,1)} %bitcast.11), channel_id=1, source_target_pairs={{0,2},{1,3},{2,0},{3,1},{4,6},{5,7},{6,4},{7,5},{8,10},{9,11},{10,... | collective-permute-start | bytes 786440 | tf_op jit(solution)/shard_map/ppermute | solution.py:160
  5.2 10.9 %collective-permute-start.2 = (bf16[2,256,256]{2,1,0:T(8,128)(2,1)}, bf16[2,256,256]{2,1,0:T(8,128)(2,1)S(1)}, u32[]{:S(2)}, u32[]{:S(2)}) collective-permute-start(bf16[2,256,256]{2,1,0:T(8,128)(2,1)} %bitcast.12), channel_id=1, source_target_pairs={{0,4},{1,5},{2,6},{3,7},{4,0},{5,1},{6,2},{7,3},{8,12},{9,13},{10,... | collective-permute-start | bytes 786440 | tf_op jit(solution)/shard_map/ppermute | solution.py:160
  7.1 15.2 %collective-permute-start.3 = (bf16[2,256,256]{2,1,0:T(8,128)(2,1)}, bf16[2,256,256]{2,1,0:T(8,128)(2,1)S(1)}, u32[]{:S(2)}, u32[]{:S(2)}) collective-permute-start(bf16[2,256,256]{2,1,0:T(8,128)(2,1)} %bitcast.13), channel_id=1, source_target_pairs={{0,8},{1,9},{2,10},{3,11},{4,12},{5,13},{6,14},{7,15},{8,0},{9,1},... | collective-permute-start | bytes 786440 | tf_op jit(solution)/shard_map/ppermute | solution.py:160
  12.2 10.1 %copy-start.5 = (bf16[2,256,256]{2,1,0:T(8,128)(2,1)}, bf16[2,256,256]{2,1,0:T(8,128)(2,1)S(1)}, u32[]{:S(2)}) copy-start(bf16[2,256,256]{2,1,0:T(8,128)(2,1)S(1)} %collective-permute-done.refs_4_) | copy-start | bytes 786436
  14.8 7.5 %copy-start.6 = (bf16[2,256,256]{2,1,0:T(8,128)(2,1)}, bf16[2,256,256]{2,1,0:T(8,128)(2,1)S(1)}, u32[]{:S(2)}) copy-start(bf16[2,256,256]{2,1,0:T(8,128)(2,1)S(1)} %collective-permute-done.1.refs_5_) | copy-start | bytes 786436
  16.1 6.2 %copy-start.7 = (bf16[2,256,256]{2,1,0:T(8,128)(2,1)}, bf16[2,256,256]{2,1,0:T(8,128)(2,1)S(1)}, u32[]{:S(2)}) copy-start(bf16[2,256,256]{2,1,0:T(8,128)(2,1)S(1)} %collective-permute-done.2.refs_6_) | copy-start | bytes 786436
  22.3 0.7 copy-start.8
  23.0 26.1 %copy-start.9 = (s32[1,6]{1,0:T(1,128)S(1)}, s32[1,6]{1,0:T(1,128)}, u32[]{:S(2)}) copy-start(s32[1,6]{1,0:T(1,128)} %param.13) | copy-start | bytes 76
  31.6 5.8 %collective-permute-start.4 = (f32[1040,128]{1,0:T(8,128)}, f32[1040,128]{1,0:T(8,128)S(1)}, u32[]{:S(2)}, u32[]{:S(2)}) collective-permute-start(f32[1040,128]{1,0:T(8,128)} %get-tuple-element.12), channel_id=1, source_target_pairs={{0,64},{64,0},{1,65},{65,1},{2,66},{66,2},{3,67},{67,3},{4,68},{68... | collective-permute-start | bytes 1597448 | tf_op jit(solution)/shard_map/ppermute | solution.py:178
  38.6 21.1 %copy-start.1 = (bf16[1040,128]{1,0:T(8,128)(2,1)}, bf16[1040,128]{1,0:T(8,128)(2,1)S(1)}, u32[]{:S(2)}) copy-start(bf16[1040,128]{1,0:T(8,128)(2,1)S(1)} %add_convert_fusion.refs_2_) | copy-start | bytes 798724
  38.6 14.0 %collective-permute-start.5 = (bf16[1040,128]{1,0:T(8,128)(2,1)S(1)}, bf16[1040,128]{1,0:T(8,128)(2,1)S(1)}, u32[]{:S(2)}, u32[]{:S(2)}) collective-permute-start(bf16[1040,128]{1,0:T(8,128)(2,1)S(1)} %add_convert_fusion.refs_2_), channel_id=1, source_target_pairs={{0,1},{1,2},{2,3},{3,4},{4,5},{5,6},{6,7},{7,8},{8,9},{9,10},{10,1... | collective-permute-start | bytes 798728 | tf_op jit(solution)/shard_map/ppermute | solution.py:180
  47.2 12.5 %collective-permute-start.6 = (bf16[1040,128]{1,0:T(8,128)(2,1)S(1)}, bf16[1040,128]{1,0:T(8,128)(2,1)S(1)}, u32[]{:S(2)}, u32[]{:S(2)}) collective-permute-start(bf16[1040,128]{1,0:T(8,128)(2,1)S(1)} %add_convert_fusion.refs_2_), channel_id=1, source_target_pairs={{1,0},{2,1},{3,2},{4,3},{5,4},{6,5},{7,6},{8,7},{9,8},{10,9},{11,1... | collective-permute-start | bytes 798728 | tf_op jit(solution)/shard_map/ppermute | solution.py:181
  52.5 7.2 %copy-start.3 = (bf16[1040,128]{1,0:T(8,128)(2,1)}, bf16[1040,128]{1,0:T(8,128)(2,1)S(1)}, u32[]{:S(2)}) copy-start(bf16[1040,128]{1,0:T(8,128)(2,1)S(1)} %collective-permute-done.5.refs_1_) | copy-start | bytes 798724
  59.7 0.7 copy-start.4
  90.4 6.1 %copy-start = (f32[784,128]{1,0:T(8,128)}, f32[784,128]{1,0:T(8,128)S(1)}, u32[]{:S(2)}) copy-start(f32[784,128]{1,0:T(8,128)S(1)} %convert_reduce_fusion.refs_2_) | copy-start | bytes 1204228
  90.4 6.1 %collective-permute-start.7 = (f32[784,128]{1,0:T(8,128)S(1)}, f32[784,128]{1,0:T(8,128)S(1)}, u32[]{:S(2)}, u32[]{:S(2)}) collective-permute-start(f32[784,128]{1,0:T(8,128)S(1)} %convert_reduce_fusion.refs_2_), channel_id=1, source_target_pairs={{0,64},{64,0},{1,65},{65,1},{2,66},{66,2},{3,67},{67,3},{4,68},{68... | collective-permute-start | bytes 1204232 | tf_op jit(solution)/shard_map/ppermute | solution.py:191
  96.5 0.7 copy-start.2

commit v2 on v1

--- a/solution.py
+++ b/solution.py
@@ -7,6 +7,7 @@
 
 LEVELS = 4
 HALF = 128
+UNROLL = 2
 F32 = jnp.float32
 BF16 = jnp.bfloat16
 SMEM = pl.BlockSpec(memory_space=pltpu.SMEM)
@@ -53,6 +54,8 @@
         pair[level, 1, :, :256] = -up[1]
         pair[level, 1, :, 256:] = up[0]
     first_core = core[0] == 0
+    groups = keep.shape[0]
+    step = HALF // groups
 
     def one(b, carry):
         level = bit[b]
@@ -64,55 +67,62 @@
         first, second, diagonal = packed(weight[0, 0] * imag + weight[0, 1] * real)
         first = first + tiles[b, 0]
         second = second + tiles[b, 1]
-        at = pl.ds(pl.multiple_of(b * HALF, HALF), HALF)
-        keep[at, :] = jnp.where(first_core, first, second)
-        send[at, :] = jnp.where(first_core, second, first)
-        own = pl.ds(nblocks * HALF + b, 1)
-        keep[own, :] = diagonal + rows[pl.ds(b, 1), :]
+        mine = jnp.where(first_core, first, second)
+        theirs = jnp.where(first_core, second, first)
+        at = pl.ds(pl.multiple_of(b * step, step), step)
+        for y in range(groups):
+            keep[y, at, :] = mine[y * step : (y + 1) * step]
+            send[y, at, :] = theirs[y * step : (y + 1) * step]
+        keep[0, pl.ds(nblocks * step + b, 1), :] = diagonal + rows[pl.ds(b, 1), :]
         return carry
 
-    lax.fori_loop(0, nblocks, one, 0)
-    tail = pl.ds(nblocks * HALF, nblocks)
-    send[tail, :] = keep[tail, :]
-    rest = pl.ds(nblocks * HALF + nblocks, 8)
-    keep[rest, :] = jnp.zeros((8, HALF), F32)
-    send[rest, :] = jnp.zeros((8, HALF), F32)
+    lax.fori_loop(0, nblocks, one, 0, unroll=UNROLL)
+    tail = keep[0, pl.ds(nblocks * step, nblocks), :]
+    for y in range(groups):
+        for ref in (keep, send):
+            ref[y, pl.ds(nblocks * step, nblocks), :] = tail
+            ref[y, pl.ds(nblocks * (step + 1), 8), :] = jnp.zeros((8, HALF), F32)
 
 
 def pick_kernel(nblocks, slots, where, before, own, after, out):
+    groups = out.shape[0]
+    step = HALF // groups
     position = lax.broadcasted_iota(jnp.int32, (16, HALF), 0)
-    tail = pl.ds(nblocks * HALF, 16)
+    tail = pl.ds(nblocks * step, 16)
     diagonals = jnp.zeros((16, HALF), F32)
     for s in range(slots):
         side, b = where[s] // nblocks, where[s] % nblocks
-        at = pl.ds(pl.multiple_of(b * HALF, HALF), HALF)
+        at = pl.ds(pl.multiple_of(b * step, step), step)
         for k, source in enumerate((before, own, after)):
 
             @pl.when(side == k)
             def _():
                 tile = source[at, :]
-                for y in range(out.shape[0]):
-                    out[y, pl.ds(s * HALF, HALF), :] = tile
+                for y in range(groups):
+                    out[y, pl.ds(s * step, step), :] = tile
 
         edge = jnp.where(side == 0, before[tail, :], jnp.where(side == 1, own[tail, :], after[tail, :]))
         line = jnp.sum(jnp.where(position == b, edge.astype(F32), 0.0), axis=0, keepdims=True)
         diagonals = jnp.where(position == s, line, diagonals)
-    for y in range(out.shape[0]):
-        out[y, pl.ds(slots * HALF, 16), :] = diagonals.astype(BF16)
+    for y in range(groups):
+        out[y, pl.ds(slots * step, 16), :] = diagonals.astype(BF16)
 
 
 def grid_kernel(slots, core, count, own, other, values, out):
     row, col = iotas()
     first_core = core[0] == 0
+    groups = own.shape[0]
+    step = HALF // groups
     total = jnp.zeros(values.shape[1:], F32)
+    lines = own[0, pl.ds(slots * step, 16), :].astype(F32)
     for s in range(slots):
-        at = pl.ds(s * HALF, HALF)
-        mine, theirs = own[at, :], other[at, :]
+        at = pl.ds(s * step, step)
+        mine = jnp.concatenate([own[y, at, :] for y in range(groups)], axis=0).astype(F32)
+        theirs = jnp.concatenate([other[y, at, :] for y in range(groups)], axis=0).astype(F32)
         first = jnp.where(first_core, mine, theirs)
         second = jnp.where(first_core, theirs, mine)
-        line = own[pl.ds(slots * HALF + s, 1), :]
         upper = jnp.where(col >= row, first, 0.0)
-        lower = jnp.where(col < row, first, jnp.where(col == row, line, 0.0))
+        lower = jnp.where(col < row, first, jnp.where(col == row, lines[s : s + 1], 0.0))
         top = jnp.concatenate([upper, second], axis=1)
         bottom = jnp.concatenate([jnp.zeros_like(lower), lower], axis=1)
         block = jnp.concatenate([top, bottom], axis=0).astype(BF16)
@@ -125,7 +135,7 @@
         out[:, k * HALF : (k + 1) * HALF] = jnp.sum(piece, axis=0, keepdims=True)
 
 
-def call(kernel, out_shape, in_specs, scratch=(), flops=0, moved=0):
+def call(kernel, out_shape, in_specs, scratch=(), flops=0, moved=0, vmem=8):
     out_specs = jax.tree.map(lambda _: VMEM, out_shape)
     return pl.pallas_call(
         kernel,
@@ -133,6 +143,7 @@
         in_specs=in_specs,
         out_specs=out_specs,
         scratch_shapes=list(scratch),
+        compiler_params=pltpu.CompilerParams(vmem_limit_bytes=vmem << 20),
         cost_estimate=pl.CostEstimate(flops=flops, bytes_accessed=moved, transcendentals=0),
     )
 
@@ -166,35 +177,38 @@
         moved=3_200_000,
     )(pole_weight, diag)
 
-    length = nblocks * HALF + 16
+    step = HALF // groups
+    length = nblocks * step + 16
     keep, send = call(
         lambda *refs: term_kernel(nblocks, *refs),
-        (shape((length, HALF), F32), shape((length, HALF), F32)),
+        (shape((groups, length, HALF), F32), shape((groups, length, HALF), F32)),
         [SMEM, SMEM, SMEM] + [VMEM] * 7,
         [pltpu.VMEM((LEVELS, 2, 256, 512), BF16)],
         flops=2_100_000_000,
         moved=5_000_000,
+        vmem=16,
     )(ancestor_bit, core, pole_weight, link, *uppers, tiles, rows)
     chip = (keep + lax.ppermute(send, "core", swap)).astype(BF16)
-
-    before = lax.ppermute(chip, "sep", [(i, i + 1) for i in range(nsep - 1)])
-    after = lax.ppermute(chip, "sep", [(i + 1, i) for i in range(nsep - 1)])
+    parts = lax.all_to_all(chip, "yh", 0, 0, tiled=True)
+    held = jnp.sum(parts.astype(F32), axis=0).astype(BF16)
+
+    before = lax.ppermute(held, "sep", [(i, i + 1) for i in range(nsep - 1)])
+    after = lax.ppermute(held, "sep", [(i + 1, i) for i in range(nsep - 1)])
     where = tile_blocks[0] - (lax.axis_index("sep") - 1) * nblocks
     picked = call(
         lambda *refs: pick_kernel(nblocks, slots, *refs),
-        shape((groups, slots * HALF + 16, HALF), BF16),
+        shape((groups, slots * step + 16, HALF), BF16),
         [SMEM] + [VMEM] * 3,
-        moved=1_500_000,
-    )(where, before, chip, after)
-    parts = lax.all_to_all(picked, "yh", 0, 0, tiled=True)
-    own = jnp.sum(parts.astype(F32), axis=0)
+        moved=500_000,
+    )(where, before, held, after)
+    own = lax.all_to_all(picked, "yh", 0, 0, tiled=True)
     other = lax.ppermute(own, "core", swap)
     return call(
         lambda *refs: grid_kernel(slots, *refs),
         shape((1, orbital_values.shape[2]), F32),
         [SMEM, SMEM] + [VMEM] * 3,
         flops=200_000_000,
-        moved=1_600_000,
+        moved=1_300_000,
     )(core, tile_count, own, other, orbital_values[0])
 
 

time: 100 us -> 89.1 us (0.89)
  blocking collectives: 27.6 us -> 13.1 us
  Pallas kernels: 16.5 us -> 8.16 us
  starting transfers between devices: 28.4 us -> 36.5 us
  waiting for transfers between devices: 22.6 us -> 27.1 us
    all_to_all x1, blocking collectives: 27.6 us -> 13.1 us  [shards(): own = lax.all_to_all(picked, 'yh', 0, 0, tiled=True)]
    all_to_all x0 -> x1, waiting for transfers between devices: none -> 8.8 us  [shards(): parts = lax.all_to_all(chip, 'yh', 0, 0, tiled=True)]
    all_to_all x0 -> x1, starting transfers between devices: none -> 6.82 us  [shards(): parts = lax.all_to_all(chip, 'yh', 0, 0, tiled=True)]
    ppermute x2, waiting for transfers between devices: 10 us -> 6.41 us  [the longest x1 6.41 us: shards(): after = lax.ppermute(held, 'sep', [(i + 1, i) for i in range(nsep - 1)])]
    pallas_call x1, Pallas kernels: 8.63 us -> 5.24 us  [shards(): call(lambda *refs: term_kernel(nblocks, *refs), (shape((groups, length, H...]
    pallas_call x1, Pallas kernels: 3.16 us -> 1.13 us  [shards(): call(lambda *refs: weigh_kernel(nblocks, *refs), (shape((nblocks, 2, HALF...]
    pallas_call x1, Pallas kernels: 2.28 us -> 0.72 us  [shards(): call(lambda *refs: pick_kernel(nblocks, slots, *refs), shape((groups, slo...]
    pallas_call x1, Pallas kernels: 2.42 us -> 1.06 us  [shards(): call(lambda *refs: grid_kernel(slots, *refs), shape((1, orbital_values.sh...]
  transfers between devices with their start and end apart: 8 -> 9, of which waited for: 7 -> 7; matrix products, arithmetic and copies ran while one was open for 1% -> 0% of each run, Pallas kernels for 3% -> 1%
where the time goes in v2:
time: 89.1 us; the launch traced here: 88.6 us
  starting transfers between devices  36.5 us (41%)
  waiting for transfers between devices  27.1 us (30%)
  blocking collectives  13.1 us (15%)
  Pallas kernels  8.16 us (9%)
  local copies, waits for them, and re-layouts  2.26 us (3%)
    all_to_all x1, blocking collectives, shards(): own = lax.all_to_all(picked, 'yh', 0, 0, tiled=True)  13.1 us
    ppermute x4, waiting for transfers between devices, shards(): lax.ppermute(own_upper, 'sep', [(i, i ^ 1 << k) for i in range(nsep)])  9.87 us
    ppermute x4, starting transfers between devices, shards(): lax.ppermute(own_upper, 'sep', [(i, i ^ 1 << k) for i in range(nsep)])  9.16 us
    all_to_all x1, waiting for transfers between devices, shards(): parts = lax.all_to_all(chip, 'yh', 0, 0, tiled=True)  8.8 us
    ppermute x1, starting transfers between devices, shards(): before = lax.ppermute(held, 'sep', [(i, i + 1) for i in range(nsep - 1)])  8.58 us
    all_to_all x1, starting transfers between devices, shards(): parts = lax.all_to_all(chip, 'yh', 0, 0, tiled=True)  6.82 us
    ppermute x1, waiting for transfers between devices, shards(): after = lax.ppermute(held, 'sep', [(i + 1, i) for i in range(nsep - 1)])  6.41 us
    ppermute x1, starting transfers between devices, shards(): other = lax.ppermute(own, 'core', swap)  5.75 us
  transfers between devices with their start and end apart: 9, of which 7 were waited for; matrix products, arithmetic and copies ran while one was open for 0% of the time, Pallas kernels for 1%

profile of v2, /device:TPU:199, one launch (start us, length us, event | category | flops | bytes accessed | tf_op | source)
XLA Modules:
  0.0 88.6 jit_solution(7293450752041269510)
XLA Ops:
  0.0 0.0 copy-start.3
  0.0 0.0 copy-start.5
  0.0 2.6 %collective-permute-start = (bf16[2,256,256]{2,1,0:T(8,128)(2,1)}, bf16[2,256,256]{2,1,0:T(8,128)(2,1)S(1)}, u32[]{:S(2)}, u32[]{:S(2)}) collective-permute-start(bf16[2,256,256]{2,1,0:T(8,128)(2,1)} %bitcast.10), channel_id=1, source_target_pairs={{0,1},{1,0},{2,3},{3,2},{4,5},{5,4},{6,7},{7,6},{8,9},{9,8},{10,11... | collective-permute-start | bytes 786440 | tf_op jit(solution)/shard_map/ppermute | solution.py:171
  2.6 2.7 %collective-permute-start.1 = (bf16[2,256,256]{2,1,0:T(8,128)(2,1)}, bf16[2,256,256]{2,1,0:T(8,128)(2,1)S(1)}, u32[]{:S(2)}, u32[]{:S(2)}) collective-permute-start(bf16[2,256,256]{2,1,0:T(8,128)(2,1)} %bitcast.11), channel_id=1, source_target_pairs={{0,2},{1,3},{2,0},{3,1},{4,6},{5,7},{6,4},{7,5},{8,10},{9,11},{10,... | collective-permute-start | bytes 786440 | tf_op jit(solution)/shard_map/ppermute | solution.py:171
  5.3 1.9 %collective-permute-start.2 = (bf16[2,256,256]{2,1,0:T(8,128)(2,1)}, bf16[2,256,256]{2,1,0:T(8,128)(2,1)S(1)}, u32[]{:S(2)}, u32[]{:S(2)}) collective-permute-start(bf16[2,256,256]{2,1,0:T(8,128)(2,1)} %bitcast.12), channel_id=1, source_target_pairs={{0,4},{1,5},{2,6},{3,7},{4,0},{5,1},{6,2},{7,3},{8,12},{9,13},{10,... | collective-permute-start | bytes 786440 | tf_op jit(solution)/shard_map/ppermute | solution.py:171
  7.3 1.9 %collective-permute-start.3 = (bf16[2,256,256]{2,1,0:T(8,128)(2,1)}, bf16[2,256,256]{2,1,0:T(8,128)(2,1)S(1)}, u32[]{:S(2)}, u32[]{:S(2)}) collective-permute-start(bf16[2,256,256]{2,1,0:T(8,128)(2,1)} %bitcast.13), channel_id=1, source_target_pairs={{0,8},{1,9},{2,10},{3,11},{4,12},{5,13},{6,14},{7,15},{8,0},{9,1},... | collective-permute-start | bytes 786440 | tf_op jit(solution)/shard_map/ppermute | solution.py:171
  9.2 0.0 copy-start
  9.2 1.6 %copy-done = bf16[1,8,2,256,256]{4,3,2,1,0:T(8,128)(2,1)S(1)} copy-done((bf16[1,8,2,256,256]{4,3,2,1,0:T(8,128)(2,1)S(1)}, bf16[1,8,2,256,256]{4,3,2,1,0:T(8,128)(2,1)}, u32[]{:S(2)}) %copy-start) | copy-done | bytes 2097176
  10.8 0.0 copy-start.2
  10.8 0.7 copy-done.2
  11.4 0.0 copy-start.4
  11.4 1.1 %shard_map.82 = (f32[8,2,128,128]{3,2,1,0:T(8,128)S(1)}, f32[8,128]{1,0:T(8,128)S(1)}) custom-call(f32[1,2]{1,0:T(1,128)S(1)} %copy-done.2, bf16[8,2,256,256]{3,2,1,0:T(8,128)(2,1)S(1)} %bitcast.7), custom_call_target="tpu_custom_call" | custom-call | flops 2000000 | bytes 3200000 | tf_op jit(solution)/shard_map/pallas_call | solution.py:172
  12.6 0.0 collective-permute-done.refs_4_
  12.6 2.4 %collective-permute-done.1.refs_5_ = bf16[2,256,256]{2,1,0:T(8,128)(2,1)S(1)} collective-permute-done((bf16[2,256,256]{2,1,0:T(8,128)(2,1)}, bf16[2,256,256]{2,1,0:T(8,128)(2,1)S(1)}, u32[]{:S(2)}, u32[]{:S(2)}) %collective-permute-start.1) | collective-permute-done | bytes 262176 | tf_op jit(solution)/shard_map/ppermute | solution.py:171
  15.0 1.3 %collective-permute-done.2.refs_6_ = bf16[2,256,256]{2,1,0:T(8,128)(2,1)S(1)} collective-permute-done((bf16[2,256,256]{2,1,0:T(8,128)(2,1)}, bf16[2,256,256]{2,1,0:T(8,128)(2,1)S(1)}, u32[]{:S(2)}, u32[]{:S(2)}) %collective-permute-start.2) | collective-permute-done | bytes 262176 | tf_op jit(solution)/shard_map/ppermute | solution.py:171
  16.2 6.2 %collective-permute-done.3.refs_7_ = bf16[2,256,256]{2,1,0:T(8,128)(2,1)S(1)} collective-permute-done((bf16[2,256,256]{2,1,0:T(8,128)(2,1)}, bf16[2,256,256]{2,1,0:T(8,128)(2,1)S(1)}, u32[]{:S(2)}, u32[]{:S(2)}) %collective-permute-start.3) | collective-permute-done | bytes 262176 | tf_op jit(solution)/shard_map/ppermute | solution.py:171
  22.5 0.0 copy-done.3
  22.5 0.0 copy-done.5
  22.5 0.0 copy-done.4
  22.5 5.2 %shard_map.83 = (f32[4,272,128]{2,1,0:T(8,128)S(1)}, f32[4,272,128]{2,1,0:T(8,128)S(1)}) custom-call(s32[8]{0:T(128)S(1)} %copy-done.5, s32[1]{0:T(128)} %bitcast.refs_1_.refs_0_, f32[1,2]{1,0:T(1,128)S(1)} %copy-done.3, bf16[8,2,256,256]{3,2,1,0:T(8,128)(2,1)S(1)} %bitcast.9, bf16[2,256,256]{2,1,0:T(8,128)(2,1)S(1)} %collective-permute-done.refs_4_, ...), custom_call_target="tpu_custom_call" | custom-call | flops 2100000000 | bytes 5000000 | tf_op jit(solution)/shard_map/pallas_call | solution.py:182
  27.7 0.0 copy-start.6
  27.7 0.0 copy-start.1
  27.7 4.2 %collective-permute-start.4 = (f32[4,272,128]{2,1,0:T(8,128)S(1)}, f32[4,272,128]{2,1,0:T(8,128)S(1)}, u32[]{:S(2)}, u32[]{:S(2)}) collective-permute-start(f32[4,272,128]{2,1,0:T(8,128)S(1)} %get-tuple-element.12), channel_id=1, source_target_pairs={{0,64},{64,0},{1,65},{65,1},{2,66},{66,2},{3,67},{67,3},{4,68},{68... | collective-permute-start | bytes 1671176 | tf_op jit(solution)/shard_map/ppermute | solution.py:191
  32.0 1.6 %collective-permute-done.4 = f32[4,272,128]{2,1,0:T(8,128)S(1)} collective-permute-done((f32[4,272,128]{2,1,0:T(8,128)S(1)}, f32[4,272,128]{2,1,0:T(8,128)S(1)}, u32[]{:S(2)}, u32[]{:S(2)}) %collective-permute-start.4) | collective-permute-done | bytes 557088 | tf_op jit(solution)/shard_map/ppermute | solution.py:191
  33.5 0.8 add_convert_fusion
  34.3 6.8 %all-to-all-start = ((bf16[4,272,128]{2,1,0:T(8,128)(2,1)}), bf16[4,272,128]{2,1,0:T(8,128)(2,1)S(1)}, u32[]{:S(2)}, u32[]{:S(2)}) async-start(bf16[4,272,128]{2,1,0:T(8,128)(2,1)} %add_convert_fusion), calls=%async_computation | async-start | bytes 557056 | tf_op jit(solution)/shard_map/all_to_all | solution.py:192
  41.1 8.8 %all-to-all-done = bf16[4,272,128]{2,1,0:T(8,128)(2,1)S(1)} async-done(((bf16[4,272,128]{2,1,0:T(8,128)(2,1)}), bf16[4,272,128]{2,1,0:T(8,128)(2,1)S(1)}, u32[]{:S(2)}, u32[]{:S(2)}) %all-to-all-start) | async-done | bytes 278560 | tf_op jit(solution)/shard_map/all_to_all | solution.py:192
  50.0 8.6 %collective-permute-start.5 = (bf16[272,128]{1,0:T(8,128)(2,1)S(1)}, bf16[272,128]{1,0:T(8,128)(2,1)S(1)}, u32[]{:S(2)}, u32[]{:S(2)}) collective-permute-start(bf16[272,128]{1,0:T(8,128)(2,1)S(1)} %reduce_sum.12.refs_2_), channel_id=1, source_target_pairs={{0,1},{1,2},{2,3},{3,4},{4,5},{5,6},{6,7},{7,8},{8,9},{9,10},{10,1... | collective-permute-start | bytes 208904 | tf_op jit(solution)/shard_map/ppermute | solution.py:195
  58.5 1.9 %collective-permute-start.6 = (bf16[272,128]{1,0:T(8,128)(2,1)S(1)}, bf16[272,128]{1,0:T(8,128)(2,1)S(1)}, u32[]{:S(2)}, u32[]{:S(2)}) collective-permute-start(bf16[272,128]{1,0:T(8,128)(2,1)S(1)} %reduce_sum.12.refs_2_), channel_id=1, source_target_pairs={{1,0},{2,1},{3,2},{4,3},{5,4},{6,5},{7,6},{8,7},{9,8},{10,9},{11,1... | collective-permute-start | bytes 208904 | tf_op jit(solution)/shard_map/ppermute | solution.py:196
  60.5 0.0 copy-done.6
  60.5 0.0 collective-permute-done.5.refs_1_
  60.5 6.4 %collective-permute-done.6.refs_3_ = bf16[272,128]{1,0:T(8,128)(2,1)S(1)} collective-permute-done((bf16[272,128]{1,0:T(8,128)(2,1)S(1)}, bf16[272,128]{1,0:T(8,128)(2,1)S(1)}, u32[]{:S(2)}, u32[]{:S(2)}) %collective-permute-start.6) | collective-permute-done | bytes 69664 | tf_op jit(solution)/shard_map/ppermute | solution.py:196
  66.9 0.7 shard_map.84
  67.6 13.1 %all_to_all.10.refs_2_ = bf16[4,208,128]{2,1,0:T(8,128)(2,1)S(1)} all-to-all(bf16[4,208,128]{2,1,0:T(8,128)(2,1)S(1)} %shard_map.84), channel_id=1, replica_groups=mesh['yh'=4,'core'=2,'sep'=64] {'yh'}, dimensions={0} | all-to-all | bytes 425984 | tf_op jit(solution)/shard_map/all_to_all | solution.py:204
  80.7 5.7 %collective-permute-start.7 = (bf16[4,208,128]{2,1,0:T(8,128)(2,1)S(1)}, bf16[4,208,128]{2,1,0:T(8,128)(2,1)S(1)}, u32[]{:S(2)}, u32[]{:S(2)}) collective-permute-start(bf16[4,208,128]{2,1,0:T(8,128)(2,1)S(1)} %all_to_all.10.refs_2_), channel_id=1, source_target_pairs={{0,64},{64,0},{1,65},{65,1},{2,66},{66,2},{3,67},{67,3},{4,68},{68... | collective-permute-start | bytes 638984 | tf_op jit(solution)/shard_map/ppermute | solution.py:205
  87.1 0.4 collective-permute-done.7.refs_3_
  87.6 0.0 copy-done.1
  87.6 1.1 %shard_map.85 = f32[1,256]{1,0:T(1,128)} custom-call(s32[1]{0:T(128)} %bitcast.refs_1_.refs_0_, s32[1]{0:T(128)S(6)} %copy.9.refs_1_, bf16[4,208,128]{2,1,0:T(8,128)(2,1)S(1)} %all_to_all.10.refs_2_, bf16[4,208,128]{2,1,0:T(8,128)(2,1)S(1)} %collective-permute-done.7.refs_3_, bf16[6,256,256]{2,1,0:T(8,128)(2,1)S(1)} %bitcast.8), custom_call_target="tpu_custom_call" | custom-call | flops 200000000 | bytes 1300000 | tf_op jit(solution)/shard_map/pallas_call | solution.py:206
  (2 shorter events, 0.1 us)
Async XLA Ops:
  0.0 22.5 %copy-start.3 = (f32[1,2]{1,0:T(1,128)S(1)}, f32[1,2]{1,0:T(1,128)}, u32[]{:S(2)}) copy-start(f32[1,2]{1,0:T(1,128)} %refs_2_.1) | copy-start | bytes 28
  0.0 22.5 %copy-start.5 = (s32[8]{0:T(128)S(1)}, s32[8]{0:T(128)}, u32[]{:S(2)}) copy-start(s32[8]{0:T(128)} %refs_0_.3) | copy-start | bytes 100
  0.0 12.6 %collective-permute-start = (bf16[2,256,256]{2,1,0:T(8,128)(2,1)}, bf16[2,256,256]{2,1,0:T(8,128)(2,1)S(1)}, u32[]{:S(2)}, u32[]{:S(2)}) collective-permute-start(bf16[2,256,256]{2,1,0:T(8,128)(2,1)} %bitcast.10), channel_id=1, source_target_pairs={{0,1},{1,0},{2,3},{3,2},{4,5},{5,4},{6,7},{7,6},{8,9},{9,8},{10,11... | collective-permute-start | bytes 786440 | tf_op jit(solution)/shard_map/ppermute | solution.py:171
  2.6 12.4 %collective-permute-start.1 = (bf16[2,256,256]{2,1,0:T(8,128)(2,1)}, bf16[2,256,256]{2,1,0:T(8,128)(2,1)S(1)}, u32[]{:S(2)}, u32[]{:S(2)}) collective-permute-start(bf16[2,256,256]{2,1,0:T(8,128)(2,1)} %bitcast.11), channel_id=1, source_target_pairs={{0,2},{1,3},{2,0},{3,1},{4,6},{5,7},{6,4},{7,5},{8,10},{9,11},{10,... | collective-permute-start | bytes 786440 | tf_op jit(solution)/shard_map/ppermute | solution.py:171
  5.3 10.9 %collective-permute-start.2 = (bf16[2,256,256]{2,1,0:T(8,128)(2,1)}, bf16[2,256,256]{2,1,0:T(8,128)(2,1)S(1)}, u32[]{:S(2)}, u32[]{:S(2)}) collective-permute-start(bf16[2,256,256]{2,1,0:T(8,128)(2,1)} %bitcast.12), channel_id=1, source_target_pairs={{0,4},{1,5},{2,6},{3,7},{4,0},{5,1},{6,2},{7,3},{8,12},{9,13},{10,... | collective-permute-start | bytes 786440 | tf_op jit(solution)/shard_map/ppermute | solution.py:171
  7.3 15.2 %collective-permute-start.3 = (bf16[2,256,256]{2,1,0:T(8,128)(2,1)}, bf16[2,256,256]{2,1,0:T(8,128)(2,1)S(1)}, u32[]{:S(2)}, u32[]{:S(2)}) collective-permute-start(bf16[2,256,256]{2,1,0:T(8,128)(2,1)} %bitcast.13), channel_id=1, source_target_pairs={{0,8},{1,9},{2,10},{3,11},{4,12},{5,13},{6,14},{7,15},{8,0},{9,1},... | collective-permute-start | bytes 786440 | tf_op jit(solution)/shard_map/ppermute | solution.py:171
  9.2 1.6 %copy-start = (bf16[1,8,2,256,256]{4,3,2,1,0:T(8,128)(2,1)S(1)}, bf16[1,8,2,256,256]{4,3,2,1,0:T(8,128)(2,1)}, u32[]{:S(2)}) copy-start(bf16[1,8,2,256,256]{4,3,2,1,0:T(8,128)(2,1)} %param.8) | copy-start | bytes 6291460
  10.8 0.7 copy-start.2
  11.4 11.0 %copy-start.4 = (bf16[1,8,2,256,256]{4,3,2,1,0:T(8,128)(2,1)S(1)}, bf16[1,8,2,256,256]{4,3,2,1,0:T(8,128)(2,1)}, u32[]{:S(2)}) copy-start(bf16[1,8,2,256,256]{4,3,2,1,0:T(8,128)(2,1)} %param.9) | copy-start | bytes 6291460
  27.7 32.8 %copy-start.6 = (s32[1,6]{1,0:T(1,128)S(1)}, s32[1,6]{1,0:T(1,128)}, u32[]{:S(2)}) copy-start(s32[1,6]{1,0:T(1,128)} %param.13) | copy-start | bytes 76
  27.7 59.8 %copy-start.1 = (bf16[1,6,256,256]{3,2,1,0:T(8,128)(2,1)S(1)}, bf16[1,6,256,256]{3,2,1,0:T(8,128)(2,1)}, u32[]{:S(2)}) copy-start(bf16[1,6,256,256]{3,2,1,0:T(8,128)(2,1)} %param.15) | copy-start | bytes 2359300
  27.7 5.8 %collective-permute-start.4 = (f32[4,272,128]{2,1,0:T(8,128)S(1)}, f32[4,272,128]{2,1,0:T(8,128)S(1)}, u32[]{:S(2)}, u32[]{:S(2)}) collective-permute-start(f32[4,272,128]{2,1,0:T(8,128)S(1)} %get-tuple-element.12), channel_id=1, source_target_pairs={{0,64},{64,0},{1,65},{65,1},{2,66},{66,2},{3,67},{67,3},{4,68},{68... | collective-permute-start | bytes 1671176 | tf_op jit(solution)/shard_map/ppermute | solution.py:191
  34.3 15.6 %all-to-all-start = ((bf16[4,272,128]{2,1,0:T(8,128)(2,1)}), bf16[4,272,128]{2,1,0:T(8,128)(2,1)S(1)}, u32[]{:S(2)}, u32[]{:S(2)}) async-start(bf16[4,272,128]{2,1,0:T(8,128)(2,1)} %add_convert_fusion), calls=%async_computation | async-start | bytes 557056 | tf_op jit(solution)/shard_map/all_to_all | solution.py:192
  50.0 10.5 %collective-permute-start.5 = (bf16[272,128]{1,0:T(8,128)(2,1)S(1)}, bf16[272,128]{1,0:T(8,128)(2,1)S(1)}, u32[]{:S(2)}, u32[]{:S(2)}) collective-permute-start(bf16[272,128]{1,0:T(8,128)(2,1)S(1)} %reduce_sum.12.refs_2_), channel_id=1, source_target_pairs={{0,1},{1,2},{2,3},{3,4},{4,5},{5,6},{6,7},{7,8},{8,9},{9,10},{10,1... | collective-permute-start | bytes 208904 | tf_op jit(solution)/shard_map/ppermute | solution.py:195
  58.5 8.4 %collective-permute-start.6 = (bf16[272,128]{1,0:T(8,128)(2,1)S(1)}, bf16[272,128]{1,0:T(8,128)(2,1)S(1)}, u32[]{:S(2)}, u32[]{:S(2)}) collective-permute-start(bf16[272,128]{1,0:T(8,128)(2,1)S(1)} %reduce_sum.12.refs_2_), channel_id=1, source_target_pairs={{1,0},{2,1},{3,2},{4,3},{5,4},{6,5},{7,6},{8,7},{9,8},{10,9},{11,1... | collective-permute-start | bytes 208904 | tf_op jit(solution)/shard_map/ppermute | solution.py:196
  80.7 6.8 %collective-permute-start.7 = (bf16[4,208,128]{2,1,0:T(8,128)(2,1)S(1)}, bf16[4,208,128]{2,1,0:T(8,128)(2,1)S(1)}, u32[]{:S(2)}, u32[]{:S(2)}) collective-permute-start(bf16[4,208,128]{2,1,0:T(8,128)(2,1)S(1)} %all_to_all.10.refs_2_), channel_id=1, source_target_pairs={{0,64},{64,0},{1,65},{65,1},{2,66},{66,2},{3,67},{67,3},{4,68},{68... | collective-permute-start | bytes 638984 | tf_op jit(solution)/shard_map/ppermute | solution.py:205

commit v3 on v2

--- a/solution.py
+++ b/solution.py
@@ -7,7 +7,6 @@
 
 LEVELS = 4
 HALF = 128
-UNROLL = 2
 F32 = jnp.float32
 BF16 = jnp.bfloat16
 SMEM = pl.BlockSpec(memory_space=pltpu.SMEM)
@@ -30,7 +29,11 @@
     return here + there.T, t01 + t10.T, diagonal
 
 
-def weigh_kernel(nblocks, weight, diag, tiles, rows):
+def weigh_kernel(nblocks, slots, weight, place, listed, count, diag, tiles, rows, plan):
+    for s in range(slots):
+        plan[s] = listed[0, s] - (place[0] - 1) * nblocks
+    plan[slots] = count[0]
+    plan[slots + 1] = place[1]
     for b in range(nblocks):
         t = weight[0, 0] * diag[b, 1].astype(F32) + weight[0, 1] * diag[b, 0].astype(F32)
         first, second, diagonal = packed(t)
@@ -47,17 +50,18 @@
     return lax.dot_general(left, right, (((1,), (1,)), ((), ())), preferred_element_type=F32)
 
 
-def term_kernel(nblocks, bit, core, weight, link, up0, up1, up2, up3, tiles, rows, keep, send, pair):
-    for level, up in enumerate((up0, up1, up2, up3)):
+def term_kernel(nblocks, order, bit, core, weight, link, tiles, rows, *refs):
+    uppers, (keep, send, pair) = refs[: len(order)], refs[len(order) :]
+    for level, up in zip(order, uppers):
         pair[level, 0, :, :256] = up[0]
         pair[level, 0, :, 256:] = up[1]
         pair[level, 1, :, :256] = -up[1]
         pair[level, 1, :, 256:] = up[0]
-    first_core = core[0] == 0
+    first_core = core[core.shape[0] - 1] == 0
     groups = keep.shape[0]
     step = HALF // groups
 
-    def one(b, carry):
+    def one(b):
         level = bit[b]
         lr, li = link[b, 0], link[b, 1]
         middle = (dot(lr, pair[level, 0]) + dot(li, pair[level, 1])).astype(BF16)
@@ -69,19 +73,30 @@
         second = second + tiles[b, 1]
         mine = jnp.where(first_core, first, second)
         theirs = jnp.where(first_core, second, first)
-        at = pl.ds(pl.multiple_of(b * step, step), step)
+        at = pl.ds(b * step, step)
         for y in range(groups):
             keep[y, at, :] = mine[y * step : (y + 1) * step]
             send[y, at, :] = theirs[y * step : (y + 1) * step]
         keep[0, pl.ds(nblocks * step + b, 1), :] = diagonal + rows[pl.ds(b, 1), :]
-        return carry
-
-    lax.fori_loop(0, nblocks, one, 0, unroll=UNROLL)
+
+    for b in range(nblocks):
+        one(b)
     tail = keep[0, pl.ds(nblocks * step, nblocks), :]
     for y in range(groups):
         for ref in (keep, send):
             ref[y, pl.ds(nblocks * step, nblocks), :] = tail
             ref[y, pl.ds(nblocks * (step + 1), 8), :] = jnp.zeros((8, HALF), F32)
+
+
+def chip_kernel(mine, theirs, out):
+    out[...] = (mine[...] + theirs[...]).astype(BF16)
+
+
+def group_kernel(parts, out):
+    total = parts[0].astype(F32)
+    for y in range(1, parts.shape[0]):
+        total = total + parts[y].astype(F32)
+    out[...] = total.astype(BF16)
 
 
 def pick_kernel(nblocks, slots, where, before, own, after, out):
@@ -108,9 +123,9 @@
         out[y, pl.ds(slots * step, 16), :] = diagonals.astype(BF16)
 
 
-def grid_kernel(slots, core, count, own, other, values, out):
+def grid_kernel(slots, plan, own, other, values, out):
     row, col = iotas()
-    first_core = core[0] == 0
+    first_core = plan[slots + 1] == 0
     groups = own.shape[0]
     step = HALF // groups
     total = jnp.zeros(values.shape[1:], F32)
@@ -128,7 +143,7 @@
         block = jnp.concatenate([top, bottom], axis=0).astype(BF16)
         v = values[s]
         inner = dot(v, block)
-        total = total + jnp.where(s < count[0], v.astype(F32) * inner, 0.0)
+        total = total + jnp.where(s < plan[slots], v.astype(F32) * inner, 0.0)
     narrow = total[:, :HALF] + total[:, HALF:]
     for k in range(narrow.shape[0] // HALF):
         piece = narrow[k * HALF : (k + 1) * HALF].T
@@ -136,7 +151,7 @@
 
 
 def call(kernel, out_shape, in_specs, scratch=(), flops=0, moved=0, vmem=8):
-    out_specs = jax.tree.map(lambda _: VMEM, out_shape)
+    out_specs = jax.tree.map(lambda each: SMEM if each.dtype == jnp.int32 else VMEM, out_shape)
     return pl.pallas_call(
         kernel,
         out_shape=out_shape,
@@ -165,51 +180,57 @@
     diag, link, own_upper = diag_inverse[0], coupling[0], ancestor_inverse[0, 0]
     nblocks, slots = diag.shape[0], orbital_values.shape[1]
     nsep, groups = lax.axis_size("sep"), lax.axis_size("yh")
-    core = lax.axis_index("core").astype(jnp.int32).reshape(1)
+    core = lax.axis_index("core").astype(jnp.int32)
+    place = jnp.stack([lax.axis_index("sep").astype(jnp.int32), core])
     swap = [(0, 1), (1, 0)]
 
-    uppers = [lax.ppermute(own_upper, "sep", [(i, i ^ 1 << k) for i in range(nsep)]) for k in range(LEVELS)]
-    tiles, rows = call(
-        lambda *refs: weigh_kernel(nblocks, *refs),
-        (shape((nblocks, 2, HALF, HALF), F32), shape((nblocks, HALF), F32)),
-        [SMEM, VMEM],
+    order = (0, 2, 1, 3)
+    uppers = [lax.ppermute(own_upper, "sep", [(i, i ^ 1 << k) for i in range(nsep)]) for k in order]
+    tiles, rows, plan = call(
+        lambda *refs: weigh_kernel(nblocks, slots, *refs),
+        (
+            shape((nblocks, 2, HALF, HALF), F32),
+            shape((nblocks, HALF), F32),
+            shape((slots + 2,), jnp.int32),
+        ),
+        [SMEM] * 4 + [VMEM],
         flops=2_000_000,
         moved=3_200_000,
-    )(pole_weight, diag)
+    )(pole_weight, place, tile_blocks, tile_count, diag)
 
     step = HALF // groups
     length = nblocks * step + 16
     keep, send = call(
-        lambda *refs: term_kernel(nblocks, *refs),
+        lambda *refs: term_kernel(nblocks, order, *refs),
         (shape((groups, length, HALF), F32), shape((groups, length, HALF), F32)),
         [SMEM, SMEM, SMEM] + [VMEM] * 7,
         [pltpu.VMEM((LEVELS, 2, 256, 512), BF16)],
         flops=2_100_000_000,
         moved=5_000_000,
         vmem=16,
-    )(ancestor_bit, core, pole_weight, link, *uppers, tiles, rows)
-    chip = (keep + lax.ppermute(send, "core", swap)).astype(BF16)
+    )(ancestor_bit, plan, pole_weight, link, tiles, rows, *uppers)
+    received = lax.ppermute(send, "core", swap)
+    chip = call(chip_kernel, shape((groups, length, HALF), BF16), [VMEM] * 2, moved=1_400_000)(keep, received)
     parts = lax.all_to_all(chip, "yh", 0, 0, tiled=True)
-    held = jnp.sum(parts.astype(F32), axis=0).astype(BF16)
+    held = call(group_kernel, shape((length, HALF), BF16), [VMEM], moved=350_000)(parts)
 
     before = lax.ppermute(held, "sep", [(i, i + 1) for i in range(nsep - 1)])
     after = lax.ppermute(held, "sep", [(i + 1, i) for i in range(nsep - 1)])
-    where = tile_blocks[0] - (lax.axis_index("sep") - 1) * nblocks
     picked = call(
         lambda *refs: pick_kernel(nblocks, slots, *refs),
         shape((groups, slots * step + 16, HALF), BF16),
         [SMEM] + [VMEM] * 3,
         moved=500_000,
-    )(where, before, held, after)
+    )(plan, before, held, after)
     own = lax.all_to_all(picked, "yh", 0, 0, tiled=True)
     other = lax.ppermute(own, "core", swap)
     return call(
         lambda *refs: grid_kernel(slots, *refs),
         shape((1, orbital_values.shape[2]), F32),
-        [SMEM, SMEM] + [VMEM] * 3,
+        [SMEM] + [VMEM] * 3,
         flops=200_000_000,
         moved=1_300_000,
-    )(core, tile_count, own, other, orbital_values[0])
+    )(plan, own, other, orbital_values[0])
 
 
 def solution(mesh):

time: 89.1 us -> 89.4 us (level)
  the two profiles are of different devices: /device:TPU:199 before, /device:TPU:9 now
where the time goes in v3:
time: 89.4 us; the launch traced here: 89 us
  starting transfers between devices  38.6 us (43%)
  blocking collectives  27 us (30%)
  waiting for transfers between devices  12 us (13%)
  Pallas kernels  7.53 us (8%)
  local copies, waits for them, and re-layouts  2.92 us (3%)
    ppermute x4, starting transfers between devices, shards(): lax.ppermute(own_upper, 'sep', [(i, i ^ 1 << k) for i in range(nsep)])  16.8 us
    all_to_all x1, blocking collectives, shards(): parts = lax.all_to_all(chip, 'yh', 0, 0, tiled=True)  15.3 us
    all_to_all x1, blocking collectives, shards(): own = lax.all_to_all(picked, 'yh', 0, 0, tiled=True)  11.7 us
    ppermute x1, starting transfers between devices, shards(): after = lax.ppermute(held, 'sep', [(i + 1, i) for i in range(nsep - 1)])  10.3 us
    ppermute x1, waiting for transfers between devices, shards(): before = lax.ppermute(held, 'sep', [(i, i + 1) for i in range(nsep - 1)])  7.33 us
    ppermute x1, starting transfers between devices, shards(): other = lax.ppermute(own, 'core', swap)  6.27 us
    pallas_call x1, Pallas kernels, shards(): call(lambda *refs: term_kernel(nblocks, order, *refs), (shape((groups, le...  3.5 us
    ppermute x1, starting transfers between devices, shards(): received = lax.ppermute(send, 'core', swap)  3.33 us
  transfers between devices with their start and end apart: 8, of which 4 were waited for; matrix products, arithmetic and copies ran while one was open for 0% of the time, Pallas kernels for 2%

profile of v3, /device:TPU:9, one launch (start us, length us, event | category | flops | bytes accessed | tf_op | source)
XLA Modules:
  0.0 89.0 jit_solution(4595680566594752651)
XLA Ops:
  0.0 0.0 copy-start.4
  0.0 0.0 copy-start.6
  0.0 5.9 %collective-permute-start.3 = (bf16[2,256,256]{2,1,0:T(8,128)(2,1)}, bf16[2,256,256]{2,1,0:T(8,128)(2,1)S(1)}, u32[]{:S(2)}, u32[]{:S(2)}) collective-permute-start(bf16[2,256,256]{2,1,0:T(8,128)(2,1)} %bitcast.9), channel_id=1, source_target_pairs={{0,8},{1,9},{2,10},{3,11},{4,12},{5,13},{6,14},{7,15},{8,0},{9,1},... | collective-permute-start | bytes 786440 | tf_op jit(solution)/shard_map/ppermute | solution.py:188
  5.9 4.7 %collective-permute-start.2 = (bf16[2,256,256]{2,1,0:T(8,128)(2,1)}, bf16[2,256,256]{2,1,0:T(8,128)(2,1)S(1)}, u32[]{:S(2)}, u32[]{:S(2)}) collective-permute-start(bf16[2,256,256]{2,1,0:T(8,128)(2,1)} %bitcast.10), channel_id=1, source_target_pairs={{0,2},{1,3},{2,0},{3,1},{4,6},{5,7},{6,4},{7,5},{8,10},{9,11},{10,... | collective-permute-start | bytes 786440 | tf_op jit(solution)/shard_map/ppermute | solution.py:188
  10.6 4.0 %collective-permute-start.1 = (bf16[2,256,256]{2,1,0:T(8,128)(2,1)}, bf16[2,256,256]{2,1,0:T(8,128)(2,1)S(1)}, u32[]{:S(2)}, u32[]{:S(2)}) collective-permute-start(bf16[2,256,256]{2,1,0:T(8,128)(2,1)} %bitcast.11), channel_id=1, source_target_pairs={{0,4},{1,5},{2,6},{3,7},{4,0},{5,1},{6,2},{7,3},{8,12},{9,13},{10,... | collective-permute-start | bytes 786440 | tf_op jit(solution)/shard_map/ppermute | solution.py:188
  14.6 2.2 %collective-permute-start = (bf16[2,256,256]{2,1,0:T(8,128)(2,1)}, bf16[2,256,256]{2,1,0:T(8,128)(2,1)S(1)}, u32[]{:S(2)}, u32[]{:S(2)}) collective-permute-start(bf16[2,256,256]{2,1,0:T(8,128)(2,1)} %bitcast.12), channel_id=1, source_target_pairs={{0,1},{1,0},{2,3},{3,2},{4,5},{5,4},{6,7},{7,6},{8,9},{9,8},{10,11... | collective-permute-start | bytes 786440 | tf_op jit(solution)/shard_map/ppermute | solution.py:188
  17.5 0.1 pad_add_fusion.refs_1_
  17.6 0.0 copy-start
  17.6 1.6 %copy-done = bf16[1,8,2,256,256]{4,3,2,1,0:T(8,128)(2,1)S(1)} copy-done((bf16[1,8,2,256,256]{4,3,2,1,0:T(8,128)(2,1)S(1)}, bf16[1,8,2,256,256]{4,3,2,1,0:T(8,128)(2,1)}, u32[]{:S(2)}) %copy-start) | copy-done | bytes 2097176
  19.2 0.0 copy-start.2
  19.2 0.7 copy-done.2
  19.8 0.0 copy-start.3
  19.8 0.7 copy-done.3
  20.5 0.0 copy-start.5
  20.5 1.6 %shard_map.82 = (f32[8,2,128,128]{3,2,1,0:T(8,128)S(1)}, f32[8,128]{1,0:T(8,128)S(1)}, s32[8]{0:T(128)S(1)}) custom-call(f32[1,2]{1,0:T(1,128)S(1)} %copy-done.3, s32[2]{0:T(128)S(1)} %pad_add_fusion.refs_1_, s32[1,6]{1,0:T(1,128)S(1)} %copy-done.2, s32[1]{0:T(128)S(6)} %copy.9.refs_3_, bf16[8,2,256,256]{3,2,1,0:T(8,128)(2,1)S(1)} %bitcast.6), custom_call_target="tpu_custom_call" | custom-call | flops 2000000 | bytes 3200000 | tf_op jit(solution)/shard_map/pallas_call | solution.py:189
  22.1 0.0 collective-permute-done.3.refs_9_
  22.1 0.0 collective-permute-done.2.refs_8_
  22.1 2.0 %collective-permute-done.1.refs_7_ = bf16[2,256,256]{2,1,0:T(8,128)(2,1)S(1)} collective-permute-done((bf16[2,256,256]{2,1,0:T(8,128)(2,1)}, bf16[2,256,256]{2,1,0:T(8,128)(2,1)S(1)}, u32[]{:S(2)}, u32[]{:S(2)}) %collective-permute-start.1) | collective-permute-done | bytes 262176 | tf_op jit(solution)/shard_map/ppermute | solution.py:188
  24.1 0.0 collective-permute-done.refs_6_
  24.1 0.0 copy-done.4
  24.1 0.0 copy-done.6
  24.1 0.0 copy-done.5
  24.2 3.5 %shard_map.83 = (f32[4,272,128]{2,1,0:T(8,128)S(1)}, f32[4,272,128]{2,1,0:T(8,128)S(1)}) custom-call(s32[8]{0:T(128)S(1)} %copy-done.6, s32[8]{0:T(128)S(1)} %get-tuple-element.10.refs_1_.refs_0_, f32[1,2]{1,0:T(1,128)S(1)} %copy-done.4, bf16[8,2,256,256]{3,2,1,0:T(8,128)(2,1)S(1)} %bitcast.8, f32[8,2,128,128]{3,2,1,0:T(8,128)S(1)} %get-tuple-element.11.refs_4_, ...), custom_call_target="tpu_custom_call" | custom-call | flops 2100000000 | bytes 5000000 | tf_op jit(solution)/shard_map/pallas_call | solution.py:203
  27.7 0.0 copy-start.1
  27.7 3.3 %collective-permute-start.4 = (f32[4,272,128]{2,1,0:T(8,128)S(1)}, f32[4,272,128]{2,1,0:T(8,128)S(1)}, u32[]{:S(2)}, u32[]{:S(2)}) collective-permute-start(f32[4,272,128]{2,1,0:T(8,128)S(1)} %get-tuple-element.14), channel_id=1, source_target_pairs={{0,64},{64,0},{1,65},{65,1},{2,66},{66,2},{3,67},{67,3},{4,68},{68... | collective-permute-start | bytes 1671176 | tf_op jit(solution)/shard_map/ppermute | solution.py:212
  31.0 1.6 %collective-permute-done.4.theirs = f32[4,272,128]{2,1,0:T(8,128)S(1)} collective-permute-done((f32[4,272,128]{2,1,0:T(8,128)S(1)}, f32[4,272,128]{2,1,0:T(8,128)S(1)}, u32[]{:S(2)}, u32[]{:S(2)}) %collective-permute-start.4) | collective-permute-done | bytes 557088 | tf_op jit(solution)/shard_map/ppermute | solution.py:212
  32.6 0.1 shard_map.84
  32.6 15.3 %all_to_all.10.parts = bf16[4,272,128]{2,1,0:T(8,128)(2,1)S(1)} all-to-all(bf16[4,272,128]{2,1,0:T(8,128)(2,1)S(1)} %shard_map.84), channel_id=1, replica_groups=mesh['yh'=4,'core'=2,'sep'=64] {'yh'}, dimensions={0} | all-to-all | bytes 557056 | tf_op jit(solution)/shard_map/all_to_all | solution.py:214
  48.0 10.3 %collective-permute-start.6 = (bf16[272,128]{1,0:T(8,128)(2,1)S(1)}, bf16[272,128]{1,0:T(8,128)(2,1)S(1)}, u32[]{:S(2)}, u32[]{:S(2)}) collective-permute-start(bf16[272,128]{1,0:T(8,128)(2,1)S(1)} %shard_map.85.refs_2_), channel_id=1, source_target_pairs={{1,0},{2,1},{3,2},{4,3},{5,4},{6,5},{7,6},{8,7},{9,8},{10,9},{11,1... | collective-permute-start | bytes 208904 | tf_op jit(solution)/shard_map/ppermute | solution.py:218
  58.3 1.9 %collective-permute-start.5 = (bf16[272,128]{1,0:T(8,128)(2,1)S(1)}, bf16[272,128]{1,0:T(8,128)(2,1)S(1)}, u32[]{:S(2)}, u32[]{:S(2)}) collective-permute-start(bf16[272,128]{1,0:T(8,128)(2,1)S(1)} %shard_map.85.refs_2_), channel_id=1, source_target_pairs={{0,1},{1,2},{2,3},{3,4},{4,5},{5,6},{6,7},{7,8},{8,9},{9,10},{10,1... | collective-permute-start | bytes 208904 | tf_op jit(solution)/shard_map/ppermute | solution.py:217
  60.2 0.0 collective-permute-done.6.refs_3_
  60.2 7.3 %collective-permute-done.5.refs_1_ = bf16[272,128]{1,0:T(8,128)(2,1)S(1)} collective-permute-done((bf16[272,128]{1,0:T(8,128)(2,1)S(1)}, bf16[272,128]{1,0:T(8,128)(2,1)S(1)}, u32[]{:S(2)}, u32[]{:S(2)}) %collective-permute-start.5) | collective-permute-done | bytes 69664 | tf_op jit(solution)/shard_map/ppermute | solution.py:217
  67.6 0.7 shard_map.86
  68.3 11.7 %all_to_all.11.refs_1_ = bf16[4,208,128]{2,1,0:T(8,128)(2,1)S(1)} all-to-all(bf16[4,208,128]{2,1,0:T(8,128)(2,1)S(1)} %shard_map.86), channel_id=1, replica_groups=mesh['yh'=4,'core'=2,'sep'=64] {'yh'}, dimensions={0} | all-to-all | bytes 425984 | tf_op jit(solution)/shard_map/all_to_all | solution.py:225
  80.0 6.3 %collective-permute-start.7 = (bf16[4,208,128]{2,1,0:T(8,128)(2,1)S(1)}, bf16[4,208,128]{2,1,0:T(8,128)(2,1)S(1)}, u32[]{:S(2)}, u32[]{:S(2)}) collective-permute-start(bf16[4,208,128]{2,1,0:T(8,128)(2,1)S(1)} %all_to_all.11.refs_1_), channel_id=1, source_target_pairs={{0,64},{64,0},{1,65},{65,1},{2,66},{66,2},{3,67},{67,3},{4,68},{68... | collective-permute-start | bytes 638984 | tf_op jit(solution)/shard_map/ppermute | solution.py:226
  86.3 1.1 %collective-permute-done.7.refs_2_ = bf16[4,208,128]{2,1,0:T(8,128)(2,1)S(1)} collective-permute-done((bf16[4,208,128]{2,1,0:T(8,128)(2,1)S(1)}, bf16[4,208,128]{2,1,0:T(8,128)(2,1)S(1)}, u32[]{:S(2)}, u32[]{:S(2)}) %collective-permute-start.7) | collective-permute-done | bytes 213024 | tf_op jit(solution)/shard_map/ppermute | solution.py:226
  87.4 0.0 copy-done.1
  87.4 1.6 %shard_map.87 = f32[1,256]{1,0:T(1,128)} custom-call(s32[8]{0:T(128)S(1)} %get-tuple-element.10.refs_1_.refs_0_, bf16[4,208,128]{2,1,0:T(8,128)(2,1)S(1)} %all_to_all.11.refs_1_, bf16[4,208,128]{2,1,0:T(8,128)(2,1)S(1)} %collective-permute-done.7.refs_2_, bf16[6,256,256]{2,1,0:T(8,128)(2,1)S(1)} %bitcast.7), custom_call_target="tpu_custom_call" | custom-call | flops 200000000 | bytes 1300000 | tf_op jit(solution)/shard_map/pallas_call | solution.py:227
  (1 shorter events, 0.0 us)
Async XLA Ops:
  0.0 24.1 %copy-start.4 = (f32[1,2]{1,0:T(1,128)S(1)}, f32[1,2]{1,0:T(1,128)}, u32[]{:S(2)}) copy-start(f32[1,2]{1,0:T(1,128)} %refs_2_.3) | copy-start | bytes 28
  0.0 24.1 %copy-start.6 = (s32[8]{0:T(128)S(1)}, s32[8]{0:T(128)}, u32[]{:S(2)}) copy-start(s32[8]{0:T(128)} %refs_0_.3) | copy-start | bytes 100
  0.0 22.1 %collective-permute-start.3 = (bf16[2,256,256]{2,1,0:T(8,128)(2,1)}, bf16[2,256,256]{2,1,0:T(8,128)(2,1)S(1)}, u32[]{:S(2)}, u32[]{:S(2)}) collective-permute-start(bf16[2,256,256]{2,1,0:T(8,128)(2,1)} %bitcast.9), channel_id=1, source_target_pairs={{0,8},{1,9},{2,10},{3,11},{4,12},{5,13},{6,14},{7,15},{8,0},{9,1},... | collective-permute-start | bytes 786440 | tf_op jit(solution)/shard_map/ppermute | solution.py:188
  5.9 16.1 %collective-permute-start.2 = (bf16[2,256,256]{2,1,0:T(8,128)(2,1)}, bf16[2,256,256]{2,1,0:T(8,128)(2,1)S(1)}, u32[]{:S(2)}, u32[]{:S(2)}) collective-permute-start(bf16[2,256,256]{2,1,0:T(8,128)(2,1)} %bitcast.10), channel_id=1, source_target_pairs={{0,2},{1,3},{2,0},{3,1},{4,6},{5,7},{6,4},{7,5},{8,10},{9,11},{10,... | collective-permute-start | bytes 786440 | tf_op jit(solution)/shard_map/ppermute | solution.py:188
  10.6 13.5 %collective-permute-start.1 = (bf16[2,256,256]{2,1,0:T(8,128)(2,1)}, bf16[2,256,256]{2,1,0:T(8,128)(2,1)S(1)}, u32[]{:S(2)}, u32[]{:S(2)}) collective-permute-start(bf16[2,256,256]{2,1,0:T(8,128)(2,1)} %bitcast.11), channel_id=1, source_target_pairs={{0,4},{1,5},{2,6},{3,7},{4,0},{5,1},{6,2},{7,3},{8,12},{9,13},{10,... | collective-permute-start | bytes 786440 | tf_op jit(solution)/shard_map/ppermute | solution.py:188
  14.6 9.5 %collective-permute-start = (bf16[2,256,256]{2,1,0:T(8,128)(2,1)}, bf16[2,256,256]{2,1,0:T(8,128)(2,1)S(1)}, u32[]{:S(2)}, u32[]{:S(2)}) collective-permute-start(bf16[2,256,256]{2,1,0:T(8,128)(2,1)} %bitcast.12), channel_id=1, source_target_pairs={{0,1},{1,0},{2,3},{3,2},{4,5},{5,4},{6,7},{7,6},{8,9},{9,8},{10,11... | collective-permute-start | bytes 786440 | tf_op jit(solution)/shard_map/ppermute | solution.py:188
  17.6 1.6 %copy-start = (bf16[1,8,2,256,256]{4,3,2,1,0:T(8,128)(2,1)S(1)}, bf16[1,8,2,256,256]{4,3,2,1,0:T(8,128)(2,1)}, u32[]{:S(2)}) copy-start(bf16[1,8,2,256,256]{4,3,2,1,0:T(8,128)(2,1)} %param.8) | copy-start | bytes 6291460
  19.2 0.7 copy-start.2
  19.8 0.7 copy-start.3
  20.5 3.7 %copy-start.5 = (bf16[1,8,2,256,256]{4,3,2,1,0:T(8,128)(2,1)S(1)}, bf16[1,8,2,256,256]{4,3,2,1,0:T(8,128)(2,1)}, u32[]{:S(2)}) copy-start(bf16[1,8,2,256,256]{4,3,2,1,0:T(8,128)(2,1)} %param.9) | copy-start | bytes 6291460
  27.7 59.7 %copy-start.1 = (bf16[1,6,256,256]{3,2,1,0:T(8,128)(2,1)S(1)}, bf16[1,6,256,256]{3,2,1,0:T(8,128)(2,1)}, u32[]{:S(2)}) copy-start(bf16[1,6,256,256]{3,2,1,0:T(8,128)(2,1)} %param.15) | copy-start | bytes 2359300
  27.7 4.9 %collective-permute-start.4 = (f32[4,272,128]{2,1,0:T(8,128)S(1)}, f32[4,272,128]{2,1,0:T(8,128)S(1)}, u32[]{:S(2)}, u32[]{:S(2)}) collective-permute-start(f32[4,272,128]{2,1,0:T(8,128)S(1)} %get-tuple-element.14), channel_id=1, source_target_pairs={{0,64},{64,0},{1,65},{65,1},{2,66},{66,2},{3,67},{67,3},{4,68},{68... | collective-permute-start | bytes 1671176 | tf_op jit(solution)/shard_map/ppermute | solution.py:212
  48.0 12.3 %collective-permute-start.6 = (bf16[272,128]{1,0:T(8,128)(2,1)S(1)}, bf16[272,128]{1,0:T(8,128)(2,1)S(1)}, u32[]{:S(2)}, u32[]{:S(2)}) collective-permute-start(bf16[272,128]{1,0:T(8,128)(2,1)S(1)} %shard_map.85.refs_2_), channel_id=1, source_target_pairs={{1,0},{2,1},{3,2},{4,3},{5,4},{6,5},{7,6},{8,7},{9,8},{10,9},{11,1... | collective-permute-start | bytes 208904 | tf_op jit(solution)/shard_map/ppermute | solution.py:218
  58.3 9.3 %collective-permute-start.5 = (bf16[272,128]{1,0:T(8,128)(2,1)S(1)}, bf16[272,128]{1,0:T(8,128)(2,1)S(1)}, u32[]{:S(2)}, u32[]{:S(2)}) collective-permute-start(bf16[272,128]{1,0:T(8,128)(2,1)S(1)} %shard_map.85.refs_2_), channel_id=1, source_target_pairs={{0,1},{1,2},{2,3},{3,4},{4,5},{5,6},{6,7},{7,8},{8,9},{9,10},{10,1... | collective-permute-start | bytes 208904 | tf_op jit(solution)/shard_map/ppermute | solution.py:217
  80.0 7.3 %collective-permute-start.7 = (bf16[4,208,128]{2,1,0:T(8,128)(2,1)S(1)}, bf16[4,208,128]{2,1,0:T(8,128)(2,1)S(1)}, u32[]{:S(2)}, u32[]{:S(2)}) collective-permute-start(bf16[4,208,128]{2,1,0:T(8,128)(2,1)S(1)} %all_to_all.11.refs_1_), channel_id=1, source_target_pairs={{0,64},{64,0},{1,65},{65,1},{2,66},{66,2},{3,67},{67,3},{4,68},{68... | collective-permute-start | bytes 638984 | tf_op jit(solution)/shard_map/ppermute | solution.py:226

commit v4 on v1

--- a/solution.py
+++ b/solution.py
@@ -46,15 +46,15 @@
     return lax.dot_general(left, right, (((1,), (1,)), ((), ())), preferred_element_type=F32)
 
 
-def term_kernel(nblocks, bit, core, weight, link, up0, up1, up2, up3, tiles, rows, keep, send, pair):
-    for level, up in enumerate((up0, up1, up2, up3)):
+def term_kernel(nblocks, order, bit, weight, link, tiles, rows, *refs):
+    uppers, (keep, send, pair) = refs[: len(order)], refs[len(order) :]
+    for level, up in zip(order, uppers):
         pair[level, 0, :, :256] = up[0]
         pair[level, 0, :, 256:] = up[1]
         pair[level, 1, :, :256] = -up[1]
         pair[level, 1, :, 256:] = up[0]
-    first_core = core[0] == 0
-
-    def one(b, carry):
+    first_core = lax.axis_index("core") == 0
+    for b in range(nblocks):
         level = bit[b]
         lr, li = link[b, 0], link[b, 1]
         middle = (dot(lr, pair[level, 0]) + dot(li, pair[level, 1])).astype(BF16)
@@ -64,55 +64,66 @@
         first, second, diagonal = packed(weight[0, 0] * imag + weight[0, 1] * real)
         first = first + tiles[b, 0]
         second = second + tiles[b, 1]
-        at = pl.ds(pl.multiple_of(b * HALF, HALF), HALF)
+        at = pl.ds(b * HALF, HALF)
         keep[at, :] = jnp.where(first_core, first, second)
         send[at, :] = jnp.where(first_core, second, first)
-        own = pl.ds(nblocks * HALF + b, 1)
-        keep[own, :] = diagonal + rows[pl.ds(b, 1), :]
-        return carry
-
-    lax.fori_loop(0, nblocks, one, 0)
+        keep[pl.ds(nblocks * HALF + b, 1), :] = diagonal + rows[pl.ds(b, 1), :]
     tail = pl.ds(nblocks * HALF, nblocks)
     send[tail, :] = keep[tail, :]
-    rest = pl.ds(nblocks * HALF + nblocks, 8)
+    rest = pl.ds(nblocks * (HALF + 1), 8)
     keep[rest, :] = jnp.zeros((8, HALF), F32)
     send[rest, :] = jnp.zeros((8, HALF), F32)
 
 
-def pick_kernel(nblocks, slots, where, before, own, after, out):
+def chip_kernel(mine, theirs, out):
+    out[...] = (mine[...] + theirs[...]).astype(BF16)
+
+
+def pick_kernel(nblocks, slots, listed, before, own, after, out):
+    groups = out.shape[0]
+    base = (lax.axis_index("sep") - 1) * nblocks
     position = lax.broadcasted_iota(jnp.int32, (16, HALF), 0)
     tail = pl.ds(nblocks * HALF, 16)
+    edges = [each[tail, :].astype(F32) for each in (before, own, after)]
     diagonals = jnp.zeros((16, HALF), F32)
     for s in range(slots):
-        side, b = where[s] // nblocks, where[s] % nblocks
+        where = listed[0, s] - base
+        side, b = where // nblocks, where % nblocks
         at = pl.ds(pl.multiple_of(b * HALF, HALF), HALF)
         for k, source in enumerate((before, own, after)):
 
             @pl.when(side == k)
             def _():
                 tile = source[at, :]
-                for y in range(out.shape[0]):
+                for y in range(groups):
                     out[y, pl.ds(s * HALF, HALF), :] = tile
 
-        edge = jnp.where(side == 0, before[tail, :], jnp.where(side == 1, own[tail, :], after[tail, :]))
-        line = jnp.sum(jnp.where(position == b, edge.astype(F32), 0.0), axis=0, keepdims=True)
+        edge = jnp.where(side == 0, edges[0], jnp.where(side == 1, edges[1], edges[2]))
+        line = jnp.sum(jnp.where(position == b, edge, 0.0), axis=0, keepdims=True)
         diagonals = jnp.where(position == s, line, diagonals)
-    for y in range(out.shape[0]):
+    for y in range(groups):
         out[y, pl.ds(slots * HALF, 16), :] = diagonals.astype(BF16)
 
 
-def grid_kernel(slots, core, count, own, other, values, out):
+def group_kernel(parts, out):
+    total = parts[0].astype(F32)
+    for y in range(1, parts.shape[0]):
+        total = total + parts[y].astype(F32)
+    out[...] = total.astype(BF16)
+
+
+def grid_kernel(slots, count, own, other, values, out):
     row, col = iotas()
-    first_core = core[0] == 0
+    first_core = lax.axis_index("core") == 0
     total = jnp.zeros(values.shape[1:], F32)
+    lines = own[pl.ds(slots * HALF, 16), :].astype(F32)
     for s in range(slots):
         at = pl.ds(s * HALF, HALF)
-        mine, theirs = own[at, :], other[at, :]
+        mine, theirs = own[at, :].astype(F32), other[at, :].astype(F32)
         first = jnp.where(first_core, mine, theirs)
         second = jnp.where(first_core, theirs, mine)
-        line = own[pl.ds(slots * HALF + s, 1), :]
         upper = jnp.where(col >= row, first, 0.0)
-        lower = jnp.where(col < row, first, jnp.where(col == row, line, 0.0))
+        lower = jnp.where(col < row, first, jnp.where(col == row, lines[s : s + 1], 0.0))
         top = jnp.concatenate([upper, second], axis=1)
         bottom = jnp.concatenate([jnp.zeros_like(lower), lower], axis=1)
         block = jnp.concatenate([top, bottom], axis=0).astype(BF16)
@@ -125,7 +136,7 @@
         out[:, k * HALF : (k + 1) * HALF] = jnp.sum(piece, axis=0, keepdims=True)
 
 
-def call(kernel, out_shape, in_specs, scratch=(), flops=0, moved=0):
+def call(kernel, out_shape, in_specs, scratch=(), flops=0, moved=0, vmem=8):
     out_specs = jax.tree.map(lambda _: VMEM, out_shape)
     return pl.pallas_call(
         kernel,
@@ -133,6 +144,7 @@
         in_specs=in_specs,
         out_specs=out_specs,
         scratch_shapes=list(scratch),
+        compiler_params=pltpu.CompilerParams(vmem_limit_bytes=vmem << 20),
         cost_estimate=pl.CostEstimate(flops=flops, bytes_accessed=moved, transcendentals=0),
     )
 
@@ -154,10 +166,10 @@
     diag, link, own_upper = diag_inverse[0], coupling[0], ancestor_inverse[0, 0]
     nblocks, slots = diag.shape[0], orbital_values.shape[1]
     nsep, groups = lax.axis_size("sep"), lax.axis_size("yh")
-    core = lax.axis_index("core").astype(jnp.int32).reshape(1)
     swap = [(0, 1), (1, 0)]
 
-    uppers = [lax.ppermute(own_upper, "sep", [(i, i ^ 1 << k) for i in range(nsep)]) for k in range(LEVELS)]
+    order = (3, 1, 2, 0)
+    uppers = [lax.ppermute(own_upper, "sep", [(i, i ^ 1 << k) for i in range(nsep)]) for k in order]
     tiles, rows = call(
         lambda *refs: weigh_kernel(nblocks, *refs),
         (shape((nblocks, 2, HALF, HALF), F32), shape((nblocks, HALF), F32)),
@@ -168,34 +180,36 @@
 
     length = nblocks * HALF + 16
     keep, send = call(
-        lambda *refs: term_kernel(nblocks, *refs),
+        lambda *refs: term_kernel(nblocks, order, *refs),
         (shape((length, HALF), F32), shape((length, HALF), F32)),
-        [SMEM, SMEM, SMEM] + [VMEM] * 7,
+        [SMEM, SMEM] + [VMEM] * (3 + LEVELS),
         [pltpu.VMEM((LEVELS, 2, 256, 512), BF16)],
         flops=2_100_000_000,
         moved=5_000_000,
-    )(ancestor_bit, core, pole_weight, link, *uppers, tiles, rows)
-    chip = (keep + lax.ppermute(send, "core", swap)).astype(BF16)
+        vmem=16,
+    )(ancestor_bit, pole_weight, link, tiles, rows, *uppers)
+    received = lax.ppermute(send, "core", swap)
+    chip = call(chip_kernel, shape((length, HALF), BF16), [VMEM] * 2, moved=1_400_000)(keep, received)
 
     before = lax.ppermute(chip, "sep", [(i, i + 1) for i in range(nsep - 1)])
     after = lax.ppermute(chip, "sep", [(i + 1, i) for i in range(nsep - 1)])
-    where = tile_blocks[0] - (lax.axis_index("sep") - 1) * nblocks
+    span = slots * HALF + 16
     picked = call(
         lambda *refs: pick_kernel(nblocks, slots, *refs),
-        shape((groups, slots * HALF + 16, HALF), BF16),
+        shape((groups, span, HALF), BF16),
         [SMEM] + [VMEM] * 3,
         moved=1_500_000,
-    )(where, before, chip, after)
+    )(tile_blocks, before, chip, after)
     parts = lax.all_to_all(picked, "yh", 0, 0, tiled=True)
-    own = jnp.sum(parts.astype(F32), axis=0)
+    own = call(group_kernel, shape((span, HALF), BF16), [VMEM], moved=1_000_000)(parts)
     other = lax.ppermute(own, "core", swap)
     return call(
         lambda *refs: grid_kernel(slots, *refs),
         shape((1, orbital_values.shape[2]), F32),
-        [SMEM, SMEM] + [VMEM] * 3,
+        [SMEM] + [VMEM] * 3,
         flops=200_000_000,
-        moved=1_600_000,
-    )(core, tile_count, own, other, orbital_values[0])
+        moved=1_300_000,
+    )(tile_count, own, other, orbital_values[0])
 
 
 def solution(mesh):

time: 100 us -> 83.6 us (0.84)
  Pallas kernels: 16.5 us -> 6.81 us
  starting transfers between devices: 28.4 us -> 25.6 us
  waiting for transfers between devices: 22.6 us -> 20.4 us
  other arithmetic: 1.72 us -> 0 us
    pallas_call x2 -> x4, Pallas kernels: 10.9 us -> 4.6 us  [the longest x1 3.6 us: shards(): call(lambda *refs: term_kernel(nblocks, order, *refs), (shape((length, HA...]
    ppermute x4, waiting for transfers between devices: 10.1 us -> 7.88 us  [shards(): lax.ppermute(own_upper, 'sep', [(i, i ^ 1 << k) for i in range(nsep)])]
    pallas_call x1, Pallas kernels: 3.16 us -> 1.13 us  [shards(): call(lambda *refs: weigh_kernel(nblocks, *refs), (shape((nblocks, 2, HALF...]
    ppermute x1, starting transfers between devices: 8.59 us -> 6.9 us  [shards(): before = lax.ppermute(chip, 'sep', [(i, i + 1) for i in range(nsep - 1)])]
    pallas_call x1, Pallas kernels: 2.42 us -> 1.08 us  [shards(): call(lambda *refs: grid_kernel(slots, *refs), shape((1, orbital_values.sh...]
    convert_element_type x1 -> x0, other arithmetic: 1.1 us -> none  [shards(): chip = (keep + lax.ppermute(send, 'core', swap)).astype(BF16)]
    unnamed x20 -> x14, local copies, waits for them, and re-layouts: 2.15 us -> 2.26 us
  transfers between devices with their start and end apart: 8 -> 8, of which waited for: 7 -> 6; matrix products, arithmetic and copies ran while one was open for 1% -> 0% of each run, Pallas kernels for 3% -> 1%
where the time goes in v4:
time: 83.6 us; the launch traced here: 83.2 us
  blocking collectives  27.4 us (33%)
  starting transfers between devices  25.6 us (31%)
  waiting for transfers between devices  20.4 us (24%)
  Pallas kernels  6.81 us (8%)
  local copies, waits for them, and re-layouts  2.26 us (3%)
    all_to_all x1, blocking collectives, shards(): parts = lax.all_to_all(picked, 'yh', 0, 0, tiled=True)  27.4 us
    ppermute x4, starting transfers between devices, shards(): lax.ppermute(own_upper, 'sep', [(i, i ^ 1 << k) for i in range(nsep)])  8.91 us
    ppermute x4, waiting for transfers between devices, shards(): lax.ppermute(own_upper, 'sep', [(i, i ^ 1 << k) for i in range(nsep)])  7.88 us
    ppermute x1, waiting for transfers between devices, shards(): after = lax.ppermute(chip, 'sep', [(i + 1, i) for i in range(nsep - 1)])  7.15 us
    ppermute x1, starting transfers between devices, shards(): before = lax.ppermute(chip, 'sep', [(i, i + 1) for i in range(nsep - 1)])  6.9 us
    ppermute x1, starting transfers between devices, shards(): other = lax.ppermute(own, 'core', swap)  4.74 us
    pallas_call x1, Pallas kernels, shards(): call(lambda *refs: term_kernel(nblocks, order, *refs), (shape((length, HA...  3.6 us
    ppermute x1, waiting for transfers between devices, shards(): before = lax.ppermute(chip, 'sep', [(i, i + 1) for i in range(nsep - 1)])  3.43 us
  transfers between devices with their start and end apart: 8, of which 6 were waited for; matrix products, arithmetic and copies ran while one was open for 0% of the time, Pallas kernels for 1%

profile of v4, /device:TPU:199, one launch (start us, length us, event | category | flops | bytes accessed | tf_op | source)
XLA Modules:
  0.0 83.2 jit_solution(9577768923680618869)
XLA Ops:
  0.0 0.0 copy-start.3
  0.0 0.0 copy-start.6
  0.0 2.0 %collective-permute-start = (bf16[2,256,256]{2,1,0:T(8,128)(2,1)}, bf16[2,256,256]{2,1,0:T(8,128)(2,1)S(1)}, u32[]{:S(2)}, u32[]{:S(2)}) collective-permute-start(bf16[2,256,256]{2,1,0:T(8,128)(2,1)} %bitcast.7), channel_id=1, source_target_pairs={{0,8},{1,9},{2,10},{3,11},{4,12},{5,13},{6,14},{7,15},{8,0},{9,1},... | collective-permute-start | bytes 786440 | tf_op jit(solution)/shard_map/ppermute | solution.py:172
  2.1 3.0 %collective-permute-start.1 = (bf16[2,256,256]{2,1,0:T(8,128)(2,1)}, bf16[2,256,256]{2,1,0:T(8,128)(2,1)S(1)}, u32[]{:S(2)}, u32[]{:S(2)}) collective-permute-start(bf16[2,256,256]{2,1,0:T(8,128)(2,1)} %bitcast.8), channel_id=1, source_target_pairs={{0,2},{1,3},{2,0},{3,1},{4,6},{5,7},{6,4},{7,5},{8,10},{9,11},{10,... | collective-permute-start | bytes 786440 | tf_op jit(solution)/shard_map/ppermute | solution.py:172
  5.1 1.9 %collective-permute-start.2 = (bf16[2,256,256]{2,1,0:T(8,128)(2,1)}, bf16[2,256,256]{2,1,0:T(8,128)(2,1)S(1)}, u32[]{:S(2)}, u32[]{:S(2)}) collective-permute-start(bf16[2,256,256]{2,1,0:T(8,128)(2,1)} %bitcast.9), channel_id=1, source_target_pairs={{0,4},{1,5},{2,6},{3,7},{4,0},{5,1},{6,2},{7,3},{8,12},{9,13},{10,... | collective-permute-start | bytes 786440 | tf_op jit(solution)/shard_map/ppermute | solution.py:172
  7.0 1.9 %collective-permute-start.3 = (bf16[2,256,256]{2,1,0:T(8,128)(2,1)}, bf16[2,256,256]{2,1,0:T(8,128)(2,1)S(1)}, u32[]{:S(2)}, u32[]{:S(2)}) collective-permute-start(bf16[2,256,256]{2,1,0:T(8,128)(2,1)} %bitcast.10), channel_id=1, source_target_pairs={{0,1},{1,0},{2,3},{3,2},{4,5},{5,4},{6,7},{7,6},{8,9},{9,8},{10,11... | collective-permute-start | bytes 786440 | tf_op jit(solution)/shard_map/ppermute | solution.py:172
  8.9 0.0 copy-start
  9.0 1.6 %copy-done = bf16[1,8,2,256,256]{4,3,2,1,0:T(8,128)(2,1)S(1)} copy-done((bf16[1,8,2,256,256]{4,3,2,1,0:T(8,128)(2,1)S(1)}, bf16[1,8,2,256,256]{4,3,2,1,0:T(8,128)(2,1)}, u32[]{:S(2)}) %copy-start) | copy-done | bytes 2097176
  10.5 0.0 copy-start.2
  10.5 0.7 copy-done.2
  11.2 0.0 copy-start.5
  11.2 1.1 %shard_map.82 = (f32[8,2,128,128]{3,2,1,0:T(8,128)S(1)}, f32[8,128]{1,0:T(8,128)S(1)}) custom-call(f32[1,2]{1,0:T(1,128)S(1)} %copy-done.2, bf16[8,2,256,256]{3,2,1,0:T(8,128)(2,1)S(1)} %bitcast.4), custom_call_target="tpu_custom_call" | custom-call | flops 2000000 | bytes 3200000 | tf_op jit(solution)/shard_map/pallas_call | solution.py:173
  12.3 3.8 %collective-permute-done.refs_5_ = bf16[2,256,256]{2,1,0:T(8,128)(2,1)S(1)} collective-permute-done((bf16[2,256,256]{2,1,0:T(8,128)(2,1)}, bf16[2,256,256]{2,1,0:T(8,128)(2,1)S(1)}, u32[]{:S(2)}, u32[]{:S(2)}) %collective-permute-start) | collective-permute-done | bytes 262176 | tf_op jit(solution)/shard_map/ppermute | solution.py:172
  16.1 0.0 collective-permute-done.1.refs_6_
  16.1 4.1 %collective-permute-done.2.refs_7_ = bf16[2,256,256]{2,1,0:T(8,128)(2,1)S(1)} collective-permute-done((bf16[2,256,256]{2,1,0:T(8,128)(2,1)}, bf16[2,256,256]{2,1,0:T(8,128)(2,1)S(1)}, u32[]{:S(2)}, u32[]{:S(2)}) %collective-permute-start.2) | collective-permute-done | bytes 262176 | tf_op jit(solution)/shard_map/ppermute | solution.py:172
  20.2 0.0 collective-permute-done.3.refs_8_
  20.2 0.0 copy-done.3
  20.2 0.0 copy-done.6
  20.2 0.0 copy-done.5
  20.2 0.0 copy-start.4
  20.2 3.6 %shard_map.83 = (f32[1040,128]{1,0:T(8,128)S(1)}, f32[1040,128]{1,0:T(8,128)S(1)}) custom-call(s32[8]{0:T(128)S(1)} %copy-done.6, f32[1,2]{1,0:T(1,128)S(1)} %copy-done.3, bf16[8,2,256,256]{3,2,1,0:T(8,128)(2,1)S(1)} %bitcast.6, f32[8,2,128,128]{3,2,1,0:T(8,128)S(1)} %get-tuple-element.9.refs_3_, f32[8,128]{1,0:T(8,128)S(1)} %get-tuple-element.10.refs_4_, ...), custom_call_target="tpu_custom_call" | custom-call | flops 2100000000 | bytes 5000000 | tf_op jit(solution)/shard_map/pallas_call | solution.py:182
  23.8 3.1 %collective-permute-start.4 = (f32[1040,128]{1,0:T(8,128)S(1)}, f32[1040,128]{1,0:T(8,128)S(1)}, u32[]{:S(2)}, u32[]{:S(2)}) collective-permute-start(f32[1040,128]{1,0:T(8,128)S(1)} %get-tuple-element.12), channel_id=1, source_target_pairs={{0,64},{64,0},{1,65},{65,1},{2,66},{66,2},{3,67},{67,3},{4,68},{68... | collective-permute-start | bytes 1597448 | tf_op jit(solution)/shard_map/ppermute | solution.py:191
  27.0 1.5 %collective-permute-done.4.theirs = f32[1040,128]{1,0:T(8,128)S(1)} collective-permute-done((f32[1040,128]{1,0:T(8,128)S(1)}, f32[1040,128]{1,0:T(8,128)S(1)}, u32[]{:S(2)}, u32[]{:S(2)}) %collective-permute-start.4) | collective-permute-done | bytes 532512 | tf_op jit(solution)/shard_map/ppermute | solution.py:191
  28.5 0.1 shard_map.84.refs_2_
  28.6 0.0 copy-start.1
  28.6 6.9 %collective-permute-start.5 = (bf16[1040,128]{1,0:T(8,128)(2,1)S(1)}, bf16[1040,128]{1,0:T(8,128)(2,1)S(1)}, u32[]{:S(2)}, u32[]{:S(2)}) collective-permute-start(bf16[1040,128]{1,0:T(8,128)(2,1)S(1)} %shard_map.84.refs_2_), channel_id=1, source_target_pairs={{0,1},{1,2},{2,3},{3,4},{4,5},{5,6},{6,7},{7,8},{8,9},{9,10},{10,1... | collective-permute-start | bytes 798728 | tf_op jit(solution)/shard_map/ppermute | solution.py:194
  35.5 1.9 %collective-permute-start.6 = (bf16[1040,128]{1,0:T(8,128)(2,1)S(1)}, bf16[1040,128]{1,0:T(8,128)(2,1)S(1)}, u32[]{:S(2)}, u32[]{:S(2)}) collective-permute-start(bf16[1040,128]{1,0:T(8,128)(2,1)S(1)} %shard_map.84.refs_2_), channel_id=1, source_target_pairs={{1,0},{2,1},{3,2},{4,3},{5,4},{6,5},{7,6},{8,7},{9,8},{10,9},{11,1... | collective-permute-start | bytes 798728 | tf_op jit(solution)/shard_map/ppermute | solution.py:195
  37.5 3.4 %collective-permute-done.5.refs_1_ = bf16[1040,128]{1,0:T(8,128)(2,1)S(1)} collective-permute-done((bf16[1040,128]{1,0:T(8,128)(2,1)S(1)}, bf16[1040,128]{1,0:T(8,128)(2,1)S(1)}, u32[]{:S(2)}, u32[]{:S(2)}) %collective-permute-start.5) | collective-permute-done | bytes 266272 | tf_op jit(solution)/shard_map/ppermute | solution.py:194
  40.9 7.2 %collective-permute-done.6.refs_3_ = bf16[1040,128]{1,0:T(8,128)(2,1)S(1)} collective-permute-done((bf16[1040,128]{1,0:T(8,128)(2,1)S(1)}, bf16[1040,128]{1,0:T(8,128)(2,1)S(1)}, u32[]{:S(2)}, u32[]{:S(2)}) %collective-permute-start.6) | collective-permute-done | bytes 266272 | tf_op jit(solution)/shard_map/ppermute | solution.py:195
  48.0 0.0 copy-done.4
  48.1 0.8 shard_map.85
  48.9 27.4 %all_to_all.5.parts = bf16[4,784,128]{2,1,0:T(8,128)(2,1)S(1)} all-to-all(bf16[4,784,128]{2,1,0:T(8,128)(2,1)S(1)} %shard_map.85), channel_id=1, replica_groups=mesh['yh'=4,'core'=2,'sep'=64] {'yh'}, dimensions={0} | all-to-all | bytes 1605632 | tf_op jit(solution)/shard_map/all_to_all | solution.py:203
  76.2 0.1 shard_map.86.refs_1_
  76.3 4.7 %collective-permute-start.7 = (bf16[784,128]{1,0:T(8,128)(2,1)S(1)}, bf16[784,128]{1,0:T(8,128)(2,1)S(1)}, u32[]{:S(2)}, u32[]{:S(2)}) collective-permute-start(bf16[784,128]{1,0:T(8,128)(2,1)S(1)} %shard_map.86.refs_1_), channel_id=1, source_target_pairs={{0,64},{64,0},{1,65},{65,1},{2,66},{66,2},{3,67},{67,3},{4,68},{68... | collective-permute-start | bytes 602120 | tf_op jit(solution)/shard_map/ppermute | solution.py:205
  81.7 0.4 collective-permute-done.7.refs_2_
  82.1 0.0 copy-done.1
  82.1 1.1 %shard_map.87 = f32[1,256]{1,0:T(1,128)} custom-call(s32[1]{0:T(128)S(6)} %copy.9.refs_0_, bf16[784,128]{1,0:T(8,128)(2,1)S(1)} %shard_map.86.refs_1_, bf16[784,128]{1,0:T(8,128)(2,1)S(1)} %collective-permute-done.7.refs_2_, bf16[6,256,256]{2,1,0:T(8,128)(2,1)S(1)} %bitcast.5), custom_call_target="tpu_custom_call" | custom-call | flops 200000000 | bytes 1300000 | tf_op jit(solution)/shard_map/pallas_call | solution.py:206
Async XLA Ops:
  0.0 20.2 %copy-start.3 = (f32[1,2]{1,0:T(1,128)S(1)}, f32[1,2]{1,0:T(1,128)}, u32[]{:S(2)}) copy-start(f32[1,2]{1,0:T(1,128)} %refs_1_.1) | copy-start | bytes 28
  0.0 20.2 %copy-start.6 = (s32[8]{0:T(128)S(1)}, s32[8]{0:T(128)}, u32[]{:S(2)}) copy-start(s32[8]{0:T(128)} %refs_0_.5) | copy-start | bytes 100
  0.0 16.1 %collective-permute-start = (bf16[2,256,256]{2,1,0:T(8,128)(2,1)}, bf16[2,256,256]{2,1,0:T(8,128)(2,1)S(1)}, u32[]{:S(2)}, u32[]{:S(2)}) collective-permute-start(bf16[2,256,256]{2,1,0:T(8,128)(2,1)} %bitcast.7), channel_id=1, source_target_pairs={{0,8},{1,9},{2,10},{3,11},{4,12},{5,13},{6,14},{7,15},{8,0},{9,1},... | collective-permute-start | bytes 786440 | tf_op jit(solution)/shard_map/ppermute | solution.py:172
  2.1 14.1 %collective-permute-start.1 = (bf16[2,256,256]{2,1,0:T(8,128)(2,1)}, bf16[2,256,256]{2,1,0:T(8,128)(2,1)S(1)}, u32[]{:S(2)}, u32[]{:S(2)}) collective-permute-start(bf16[2,256,256]{2,1,0:T(8,128)(2,1)} %bitcast.8), channel_id=1, source_target_pairs={{0,2},{1,3},{2,0},{3,1},{4,6},{5,7},{6,4},{7,5},{8,10},{9,11},{10,... | collective-permute-start | bytes 786440 | tf_op jit(solution)/shard_map/ppermute | solution.py:172
  5.1 15.1 %collective-permute-start.2 = (bf16[2,256,256]{2,1,0:T(8,128)(2,1)}, bf16[2,256,256]{2,1,0:T(8,128)(2,1)S(1)}, u32[]{:S(2)}, u32[]{:S(2)}) collective-permute-start(bf16[2,256,256]{2,1,0:T(8,128)(2,1)} %bitcast.9), channel_id=1, source_target_pairs={{0,4},{1,5},{2,6},{3,7},{4,0},{5,1},{6,2},{7,3},{8,12},{9,13},{10,... | collective-permute-start | bytes 786440 | tf_op jit(solution)/shard_map/ppermute | solution.py:172
  7.0 13.2 %collective-permute-start.3 = (bf16[2,256,256]{2,1,0:T(8,128)(2,1)}, bf16[2,256,256]{2,1,0:T(8,128)(2,1)S(1)}, u32[]{:S(2)}, u32[]{:S(2)}) collective-permute-start(bf16[2,256,256]{2,1,0:T(8,128)(2,1)} %bitcast.10), channel_id=1, source_target_pairs={{0,1},{1,0},{2,3},{3,2},{4,5},{5,4},{6,7},{7,6},{8,9},{9,8},{10,11... | collective-permute-start | bytes 786440 | tf_op jit(solution)/shard_map/ppermute | solution.py:172
  8.9 1.6 %copy-start = (bf16[1,8,2,256,256]{4,3,2,1,0:T(8,128)(2,1)S(1)}, bf16[1,8,2,256,256]{4,3,2,1,0:T(8,128)(2,1)}, u32[]{:S(2)}) copy-start(bf16[1,8,2,256,256]{4,3,2,1,0:T(8,128)(2,1)} %param.8) | copy-start | bytes 6291460
  10.5 0.7 copy-start.2
  11.2 9.0 %copy-start.5 = (bf16[1,8,2,256,256]{4,3,2,1,0:T(8,128)(2,1)S(1)}, bf16[1,8,2,256,256]{4,3,2,1,0:T(8,128)(2,1)}, u32[]{:S(2)}) copy-start(bf16[1,8,2,256,256]{4,3,2,1,0:T(8,128)(2,1)} %param.9) | copy-start | bytes 6291460
  20.2 27.8 %copy-start.4 = (s32[1,6]{1,0:T(1,128)S(1)}, s32[1,6]{1,0:T(1,128)}, u32[]{:S(2)}) copy-start(s32[1,6]{1,0:T(1,128)} %refs_0_.6) | copy-start | bytes 76
  23.8 4.7 %collective-permute-start.4 = (f32[1040,128]{1,0:T(8,128)S(1)}, f32[1040,128]{1,0:T(8,128)S(1)}, u32[]{:S(2)}, u32[]{:S(2)}) collective-permute-start(f32[1040,128]{1,0:T(8,128)S(1)} %get-tuple-element.12), channel_id=1, source_target_pairs={{0,64},{64,0},{1,65},{65,1},{2,66},{66,2},{3,67},{67,3},{4,68},{68... | collective-permute-start | bytes 1597448 | tf_op jit(solution)/shard_map/ppermute | solution.py:191
  28.6 53.5 %copy-start.1 = (bf16[1,6,256,256]{3,2,1,0:T(8,128)(2,1)S(1)}, bf16[1,6,256,256]{3,2,1,0:T(8,128)(2,1)}, u32[]{:S(2)}) copy-start(bf16[1,6,256,256]{3,2,1,0:T(8,128)(2,1)} %param.15) | copy-start | bytes 2359300
  28.6 12.3 %collective-permute-start.5 = (bf16[1040,128]{1,0:T(8,128)(2,1)S(1)}, bf16[1040,128]{1,0:T(8,128)(2,1)S(1)}, u32[]{:S(2)}, u32[]{:S(2)}) collective-permute-start(bf16[1040,128]{1,0:T(8,128)(2,1)S(1)} %shard_map.84.refs_2_), channel_id=1, source_target_pairs={{0,1},{1,2},{2,3},{3,4},{4,5},{5,6},{6,7},{7,8},{8,9},{9,10},{10,1... | collective-permute-start | bytes 798728 | tf_op jit(solution)/shard_map/ppermute | solution.py:194
  35.5 12.5 %collective-permute-start.6 = (bf16[1040,128]{1,0:T(8,128)(2,1)S(1)}, bf16[1040,128]{1,0:T(8,128)(2,1)S(1)}, u32[]{:S(2)}, u32[]{:S(2)}) collective-permute-start(bf16[1040,128]{1,0:T(8,128)(2,1)S(1)} %shard_map.84.refs_2_), channel_id=1, source_target_pairs={{1,0},{2,1},{3,2},{4,3},{5,4},{6,5},{7,6},{8,7},{9,8},{10,9},{11,1... | collective-permute-start | bytes 798728 | tf_op jit(solution)/shard_map/ppermute | solution.py:195
  76.3 5.8 %collective-permute-start.7 = (bf16[784,128]{1,0:T(8,128)(2,1)S(1)}, bf16[784,128]{1,0:T(8,128)(2,1)S(1)}, u32[]{:S(2)}, u32[]{:S(2)}) collective-permute-start(bf16[784,128]{1,0:T(8,128)(2,1)S(1)} %shard_map.86.refs_1_), channel_id=1, source_target_pairs={{0,64},{64,0},{1,65},{65,1},{2,66},{66,2},{3,67},{67,3},{4,68},{68... | collective-permute-start | bytes 602120 | tf_op jit(solution)/shard_map/ppermute | solution.py:205

commit v5 on v4

--- a/solution.py
+++ b/solution.py
@@ -168,7 +168,7 @@
     nsep, groups = lax.axis_size("sep"), lax.axis_size("yh")
     swap = [(0, 1), (1, 0)]
 
-    order = (3, 1, 2, 0)
+    order = (3, 0, 2, 1)
     uppers = [lax.ppermute(own_upper, "sep", [(i, i ^ 1 << k) for i in range(nsep)]) for k in order]
     tiles, rows = call(
         lambda *refs: weigh_kernel(nblocks, *refs),

time: 83.6 us -> 83.3 us (level)
  waiting for transfers between devices: 20.4 us -> 19 us
  starting transfers between devices: 25.6 us -> 26.7 us
    ppermute x4, waiting for transfers between devices: 7.88 us -> 6.49 us  [shards(): lax.ppermute(own_upper, 'sep', [(i, i ^ 1 << k) for i in range(nsep)])]
where the time goes in v5:
time: 83.3 us; the launch traced here: 82.9 us
  blocking collectives  27.4 us (33%)
  starting transfers between devices  26.7 us (32%)
  waiting for transfers between devices  19 us (23%)
  Pallas kernels  6.82 us (8%)
  local copies, waits for them, and re-layouts  2.26 us (3%)
    all_to_all x1, blocking collectives, shards(): parts = lax.all_to_all(picked, 'yh', 0, 0, tiled=True)  27.4 us
    ppermute x4, starting transfers between devices, shards(): lax.ppermute(own_upper, 'sep', [(i, i ^ 1 << k) for i in range(nsep)])  9.16 us
    ppermute x1, starting transfers between devices, shards(): before = lax.ppermute(chip, 'sep', [(i, i + 1) for i in range(nsep - 1)])  7.17 us
    ppermute x1, waiting for transfers between devices, shards(): after = lax.ppermute(chip, 'sep', [(i + 1, i) for i in range(nsep - 1)])  7.15 us
    ppermute x4, waiting for transfers between devices, shards(): lax.ppermute(own_upper, 'sep', [(i, i ^ 1 << k) for i in range(nsep)])  6.49 us
    ppermute x1, starting transfers between devices, shards(): other = lax.ppermute(own, 'core', swap)  4.75 us
    ppermute x1, starting transfers between devices, shards(): received = lax.ppermute(send, 'core', swap)  3.71 us
    pallas_call x1, Pallas kernels, shards(): call(lambda *refs: term_kernel(nblocks, order, *refs), (shape((length, HA...  3.6 us
  transfers between devices with their start and end apart: 8, of which 6 were waited for; matrix products, arithmetic and copies ran while one was open for 0% of the time, Pallas kernels for 1%

profile of v5, /device:TPU:199, one launch (start us, length us, event | category | flops | bytes accessed | tf_op | source)
XLA Modules:
  0.0 82.9 jit_solution(15284773873196464197)
XLA Ops:
  0.0 0.0 copy-start.3
  0.0 0.0 copy-start.6
  0.0 2.0 %collective-permute-start = (bf16[2,256,256]{2,1,0:T(8,128)(2,1)}, bf16[2,256,256]{2,1,0:T(8,128)(2,1)S(1)}, u32[]{:S(2)}, u32[]{:S(2)}) collective-permute-start(bf16[2,256,256]{2,1,0:T(8,128)(2,1)} %bitcast.7), channel_id=1, source_target_pairs={{0,8},{1,9},{2,10},{3,11},{4,12},{5,13},{6,14},{7,15},{8,0},{9,1},... | collective-permute-start | bytes 786440 | tf_op jit(solution)/shard_map/ppermute | solution.py:172
  2.1 2.5 %collective-permute-start.1 = (bf16[2,256,256]{2,1,0:T(8,128)(2,1)}, bf16[2,256,256]{2,1,0:T(8,128)(2,1)S(1)}, u32[]{:S(2)}, u32[]{:S(2)}) collective-permute-start(bf16[2,256,256]{2,1,0:T(8,128)(2,1)} %bitcast.8), channel_id=1, source_target_pairs={{0,1},{1,0},{2,3},{3,2},{4,5},{5,4},{6,7},{7,6},{8,9},{9,8},{10,11... | collective-permute-start | bytes 786440 | tf_op jit(solution)/shard_map/ppermute | solution.py:172
  4.5 1.9 %collective-permute-start.2 = (bf16[2,256,256]{2,1,0:T(8,128)(2,1)}, bf16[2,256,256]{2,1,0:T(8,128)(2,1)S(1)}, u32[]{:S(2)}, u32[]{:S(2)}) collective-permute-start(bf16[2,256,256]{2,1,0:T(8,128)(2,1)} %bitcast.9), channel_id=1, source_target_pairs={{0,4},{1,5},{2,6},{3,7},{4,0},{5,1},{6,2},{7,3},{8,12},{9,13},{10,... | collective-permute-start | bytes 786440 | tf_op jit(solution)/shard_map/ppermute | solution.py:172
  6.4 2.7 %collective-permute-start.3 = (bf16[2,256,256]{2,1,0:T(8,128)(2,1)}, bf16[2,256,256]{2,1,0:T(8,128)(2,1)S(1)}, u32[]{:S(2)}, u32[]{:S(2)}) collective-permute-start(bf16[2,256,256]{2,1,0:T(8,128)(2,1)} %bitcast.10), channel_id=1, source_target_pairs={{0,2},{1,3},{2,0},{3,1},{4,6},{5,7},{6,4},{7,5},{8,10},{9,11},{10,... | collective-permute-start | bytes 786440 | tf_op jit(solution)/shard_map/ppermute | solution.py:172
  9.2 0.0 copy-start
  9.2 1.6 %copy-done = bf16[1,8,2,256,256]{4,3,2,1,0:T(8,128)(2,1)S(1)} copy-done((bf16[1,8,2,256,256]{4,3,2,1,0:T(8,128)(2,1)S(1)}, bf16[1,8,2,256,256]{4,3,2,1,0:T(8,128)(2,1)}, u32[]{:S(2)}) %copy-start) | copy-done | bytes 2097176
  10.8 0.0 copy-start.2
  10.8 0.7 copy-done.2
  11.4 0.0 copy-start.5
  11.4 1.1 %shard_map.82 = (f32[8,2,128,128]{3,2,1,0:T(8,128)S(1)}, f32[8,128]{1,0:T(8,128)S(1)}) custom-call(f32[1,2]{1,0:T(1,128)S(1)} %copy-done.2, bf16[8,2,256,256]{3,2,1,0:T(8,128)(2,1)S(1)} %bitcast.4), custom_call_target="tpu_custom_call" | custom-call | flops 2000000 | bytes 3200000 | tf_op jit(solution)/shard_map/pallas_call | solution.py:173
  12.6 3.5 %collective-permute-done.refs_5_ = bf16[2,256,256]{2,1,0:T(8,128)(2,1)S(1)} collective-permute-done((bf16[2,256,256]{2,1,0:T(8,128)(2,1)}, bf16[2,256,256]{2,1,0:T(8,128)(2,1)S(1)}, u32[]{:S(2)}, u32[]{:S(2)}) %collective-permute-start) | collective-permute-done | bytes 262176 | tf_op jit(solution)/shard_map/ppermute | solution.py:172
  16.1 0.0 collective-permute-done.1.refs_6_
  16.1 2.9 %collective-permute-done.2.refs_7_ = bf16[2,256,256]{2,1,0:T(8,128)(2,1)S(1)} collective-permute-done((bf16[2,256,256]{2,1,0:T(8,128)(2,1)}, bf16[2,256,256]{2,1,0:T(8,128)(2,1)S(1)}, u32[]{:S(2)}, u32[]{:S(2)}) %collective-permute-start.2) | collective-permute-done | bytes 262176 | tf_op jit(solution)/shard_map/ppermute | solution.py:172
  19.1 0.0 collective-permute-done.3.refs_8_
  19.1 0.0 copy-done.3
  19.1 0.0 copy-done.6
  19.1 0.0 copy-done.5
  19.1 0.0 copy-start.4
  19.1 3.6 %shard_map.83 = (f32[1040,128]{1,0:T(8,128)S(1)}, f32[1040,128]{1,0:T(8,128)S(1)}) custom-call(s32[8]{0:T(128)S(1)} %copy-done.6, f32[1,2]{1,0:T(1,128)S(1)} %copy-done.3, bf16[8,2,256,256]{3,2,1,0:T(8,128)(2,1)S(1)} %bitcast.6, f32[8,2,128,128]{3,2,1,0:T(8,128)S(1)} %get-tuple-element.9.refs_3_, f32[8,128]{1,0:T(8,128)S(1)} %get-tuple-element.10.refs_4_, ...), custom_call_target="tpu_custom_call" | custom-call | flops 2100000000 | bytes 5000000 | tf_op jit(solution)/shard_map/pallas_call | solution.py:182
  22.7 3.7 %collective-permute-start.4 = (f32[1040,128]{1,0:T(8,128)S(1)}, f32[1040,128]{1,0:T(8,128)S(1)}, u32[]{:S(2)}, u32[]{:S(2)}) collective-permute-start(f32[1040,128]{1,0:T(8,128)S(1)} %get-tuple-element.12), channel_id=1, source_target_pairs={{0,64},{64,0},{1,65},{65,1},{2,66},{66,2},{3,67},{67,3},{4,68},{68... | collective-permute-start | bytes 1597448 | tf_op jit(solution)/shard_map/ppermute | solution.py:191
  26.4 1.5 %collective-permute-done.4.theirs = f32[1040,128]{1,0:T(8,128)S(1)} collective-permute-done((f32[1040,128]{1,0:T(8,128)S(1)}, f32[1040,128]{1,0:T(8,128)S(1)}, u32[]{:S(2)}, u32[]{:S(2)}) %collective-permute-start.4) | collective-permute-done | bytes 532512 | tf_op jit(solution)/shard_map/ppermute | solution.py:191
  27.9 0.1 shard_map.84.refs_2_
  28.0 0.0 copy-start.1
  28.0 7.2 %collective-permute-start.5 = (bf16[1040,128]{1,0:T(8,128)(2,1)S(1)}, bf16[1040,128]{1,0:T(8,128)(2,1)S(1)}, u32[]{:S(2)}, u32[]{:S(2)}) collective-permute-start(bf16[1040,128]{1,0:T(8,128)(2,1)S(1)} %shard_map.84.refs_2_), channel_id=1, source_target_pairs={{0,1},{1,2},{2,3},{3,4},{4,5},{5,6},{6,7},{7,8},{8,9},{9,10},{10,1... | collective-permute-start | bytes 798728 | tf_op jit(solution)/shard_map/ppermute | solution.py:194
  35.2 1.9 %collective-permute-start.6 = (bf16[1040,128]{1,0:T(8,128)(2,1)S(1)}, bf16[1040,128]{1,0:T(8,128)(2,1)S(1)}, u32[]{:S(2)}, u32[]{:S(2)}) collective-permute-start(bf16[1040,128]{1,0:T(8,128)(2,1)S(1)} %shard_map.84.refs_2_), channel_id=1, source_target_pairs={{1,0},{2,1},{3,2},{4,3},{5,4},{6,5},{7,6},{8,7},{9,8},{10,9},{11,1... | collective-permute-start | bytes 798728 | tf_op jit(solution)/shard_map/ppermute | solution.py:195
  37.2 3.4 %collective-permute-done.5.refs_1_ = bf16[1040,128]{1,0:T(8,128)(2,1)S(1)} collective-permute-done((bf16[1040,128]{1,0:T(8,128)(2,1)S(1)}, bf16[1040,128]{1,0:T(8,128)(2,1)S(1)}, u32[]{:S(2)}, u32[]{:S(2)}) %collective-permute-start.5) | collective-permute-done | bytes 266272 | tf_op jit(solution)/shard_map/ppermute | solution.py:194
  40.6 7.2 %collective-permute-done.6.refs_3_ = bf16[1040,128]{1,0:T(8,128)(2,1)S(1)} collective-permute-done((bf16[1040,128]{1,0:T(8,128)(2,1)S(1)}, bf16[1040,128]{1,0:T(8,128)(2,1)S(1)}, u32[]{:S(2)}, u32[]{:S(2)}) %collective-permute-start.6) | collective-permute-done | bytes 266272 | tf_op jit(solution)/shard_map/ppermute | solution.py:195
  47.7 0.0 copy-done.4
  47.7 0.8 shard_map.85
  48.5 27.4 %all_to_all.5.parts = bf16[4,784,128]{2,1,0:T(8,128)(2,1)S(1)} all-to-all(bf16[4,784,128]{2,1,0:T(8,128)(2,1)S(1)} %shard_map.85), channel_id=1, replica_groups=mesh['yh'=4,'core'=2,'sep'=64] {'yh'}, dimensions={0} | all-to-all | bytes 1605632 | tf_op jit(solution)/shard_map/all_to_all | solution.py:203
  75.9 0.1 shard_map.86.refs_1_
  76.0 4.8 %collective-permute-start.7 = (bf16[784,128]{1,0:T(8,128)(2,1)S(1)}, bf16[784,128]{1,0:T(8,128)(2,1)S(1)}, u32[]{:S(2)}, u32[]{:S(2)}) collective-permute-start(bf16[784,128]{1,0:T(8,128)(2,1)S(1)} %shard_map.86.refs_1_), channel_id=1, source_target_pairs={{0,64},{64,0},{1,65},{65,1},{2,66},{66,2},{3,67},{67,3},{4,68},{68... | collective-permute-start | bytes 602120 | tf_op jit(solution)/shard_map/ppermute | solution.py:205
  81.4 0.4 collective-permute-done.7.refs_2_
  81.8 0.0 copy-done.1
  81.8 1.1 %shard_map.87 = f32[1,256]{1,0:T(1,128)} custom-call(s32[1]{0:T(128)S(6)} %copy.9.refs_0_, bf16[784,128]{1,0:T(8,128)(2,1)S(1)} %shard_map.86.refs_1_, bf16[784,128]{1,0:T(8,128)(2,1)S(1)} %collective-permute-done.7.refs_2_, bf16[6,256,256]{2,1,0:T(8,128)(2,1)S(1)} %bitcast.5), custom_call_target="tpu_custom_call" | custom-call | flops 200000000 | bytes 1300000 | tf_op jit(solution)/shard_map/pallas_call | solution.py:206
Async XLA Ops:
  0.0 19.1 %copy-start.3 = (f32[1,2]{1,0:T(1,128)S(1)}, f32[1,2]{1,0:T(1,128)}, u32[]{:S(2)}) copy-start(f32[1,2]{1,0:T(1,128)} %refs_1_.1) | copy-start | bytes 28
  0.0 19.1 %copy-start.6 = (s32[8]{0:T(128)S(1)}, s32[8]{0:T(128)}, u32[]{:S(2)}) copy-start(s32[8]{0:T(128)} %refs_0_.5) | copy-start | bytes 100
  0.0 16.1 %collective-permute-start = (bf16[2,256,256]{2,1,0:T(8,128)(2,1)}, bf16[2,256,256]{2,1,0:T(8,128)(2,1)S(1)}, u32[]{:S(2)}, u32[]{:S(2)}) collective-permute-start(bf16[2,256,256]{2,1,0:T(8,128)(2,1)} %bitcast.7), channel_id=1, source_target_pairs={{0,8},{1,9},{2,10},{3,11},{4,12},{5,13},{6,14},{7,15},{8,0},{9,1},... | collective-permute-start | bytes 786440 | tf_op jit(solution)/shard_map/ppermute | solution.py:172
  2.1 14.1 %collective-permute-start.1 = (bf16[2,256,256]{2,1,0:T(8,128)(2,1)}, bf16[2,256,256]{2,1,0:T(8,128)(2,1)S(1)}, u32[]{:S(2)}, u32[]{:S(2)}) collective-permute-start(bf16[2,256,256]{2,1,0:T(8,128)(2,1)} %bitcast.8), channel_id=1, source_target_pairs={{0,1},{1,0},{2,3},{3,2},{4,5},{5,4},{6,7},{7,6},{8,9},{9,8},{10,11... | collective-permute-start | bytes 786440 | tf_op jit(solution)/shard_map/ppermute | solution.py:172
  4.5 14.5 %collective-permute-start.2 = (bf16[2,256,256]{2,1,0:T(8,128)(2,1)}, bf16[2,256,256]{2,1,0:T(8,128)(2,1)S(1)}, u32[]{:S(2)}, u32[]{:S(2)}) collective-permute-start(bf16[2,256,256]{2,1,0:T(8,128)(2,1)} %bitcast.9), channel_id=1, source_target_pairs={{0,4},{1,5},{2,6},{3,7},{4,0},{5,1},{6,2},{7,3},{8,12},{9,13},{10,... | collective-permute-start | bytes 786440 | tf_op jit(solution)/shard_map/ppermute | solution.py:172
  6.4 12.6 %collective-permute-start.3 = (bf16[2,256,256]{2,1,0:T(8,128)(2,1)}, bf16[2,256,256]{2,1,0:T(8,128)(2,1)S(1)}, u32[]{:S(2)}, u32[]{:S(2)}) collective-permute-start(bf16[2,256,256]{2,1,0:T(8,128)(2,1)} %bitcast.10), channel_id=1, source_target_pairs={{0,2},{1,3},{2,0},{3,1},{4,6},{5,7},{6,4},{7,5},{8,10},{9,11},{10,... | collective-permute-start | bytes 786440 | tf_op jit(solution)/shard_map/ppermute | solution.py:172
  9.2 1.6 %copy-start = (bf16[1,8,2,256,256]{4,3,2,1,0:T(8,128)(2,1)S(1)}, bf16[1,8,2,256,256]{4,3,2,1,0:T(8,128)(2,1)}, u32[]{:S(2)}) copy-start(bf16[1,8,2,256,256]{4,3,2,1,0:T(8,128)(2,1)} %param.8) | copy-start | bytes 6291460
  10.8 0.7 copy-start.2
  11.4 7.6 %copy-start.5 = (bf16[1,8,2,256,256]{4,3,2,1,0:T(8,128)(2,1)S(1)}, bf16[1,8,2,256,256]{4,3,2,1,0:T(8,128)(2,1)}, u32[]{:S(2)}) copy-start(bf16[1,8,2,256,256]{4,3,2,1,0:T(8,128)(2,1)} %param.9) | copy-start | bytes 6291460
  19.1 28.7 %copy-start.4 = (s32[1,6]{1,0:T(1,128)S(1)}, s32[1,6]{1,0:T(1,128)}, u32[]{:S(2)}) copy-start(s32[1,6]{1,0:T(1,128)} %refs_0_.6) | copy-start | bytes 76
  22.7 5.2 %collective-permute-start.4 = (f32[1040,128]{1,0:T(8,128)S(1)}, f32[1040,128]{1,0:T(8,128)S(1)}, u32[]{:S(2)}, u32[]{:S(2)}) collective-permute-start(f32[1040,128]{1,0:T(8,128)S(1)} %get-tuple-element.12), channel_id=1, source_target_pairs={{0,64},{64,0},{1,65},{65,1},{2,66},{66,2},{3,67},{67,3},{4,68},{68... | collective-permute-start | bytes 1597448 | tf_op jit(solution)/shard_map/ppermute | solution.py:191
  28.0 53.8 %copy-start.1 = (bf16[1,6,256,256]{3,2,1,0:T(8,128)(2,1)S(1)}, bf16[1,6,256,256]{3,2,1,0:T(8,128)(2,1)}, u32[]{:S(2)}) copy-start(bf16[1,6,256,256]{3,2,1,0:T(8,128)(2,1)} %param.15) | copy-start | bytes 2359300
  28.0 12.5 %collective-permute-start.5 = (bf16[1040,128]{1,0:T(8,128)(2,1)S(1)}, bf16[1040,128]{1,0:T(8,128)(2,1)S(1)}, u32[]{:S(2)}, u32[]{:S(2)}) collective-permute-start(bf16[1040,128]{1,0:T(8,128)(2,1)S(1)} %shard_map.84.refs_2_), channel_id=1, source_target_pairs={{0,1},{1,2},{2,3},{3,4},{4,5},{5,6},{6,7},{7,8},{8,9},{9,10},{10,1... | collective-permute-start | bytes 798728 | tf_op jit(solution)/shard_map/ppermute | solution.py:194
  35.2 12.5 %collective-permute-start.6 = (bf16[1040,128]{1,0:T(8,128)(2,1)S(1)}, bf16[1040,128]{1,0:T(8,128)(2,1)S(1)}, u32[]{:S(2)}, u32[]{:S(2)}) collective-permute-start(bf16[1040,128]{1,0:T(8,128)(2,1)S(1)} %shard_map.84.refs_2_), channel_id=1, source_target_pairs={{1,0},{2,1},{3,2},{4,3},{5,4},{6,5},{7,6},{8,7},{9,8},{10,9},{11,1... | collective-permute-start | bytes 798728 | tf_op jit(solution)/shard_map/ppermute | solution.py:195
  76.0 5.8 %collective-permute-start.7 = (bf16[784,128]{1,0:T(8,128)(2,1)S(1)}, bf16[784,128]{1,0:T(8,128)(2,1)S(1)}, u32[]{:S(2)}, u32[]{:S(2)}) collective-permute-start(bf16[784,128]{1,0:T(8,128)(2,1)S(1)} %shard_map.86.refs_1_), channel_id=1, source_target_pairs={{0,64},{64,0},{1,65},{65,1},{2,66},{66,2},{3,67},{67,3},{4,68},{68... | collective-permute-start | bytes 602120 | tf_op jit(solution)/shard_map/ppermute | solution.py:205

commit v6 on v2

--- a/solution.py
+++ b/solution.py
@@ -7,7 +7,6 @@
 
 LEVELS = 4
 HALF = 128
-UNROLL = 2
 F32 = jnp.float32
 BF16 = jnp.bfloat16
 SMEM = pl.BlockSpec(memory_space=pltpu.SMEM)
@@ -47,17 +46,17 @@
     return lax.dot_general(left, right, (((1,), (1,)), ((), ())), preferred_element_type=F32)
 
 
-def term_kernel(nblocks, bit, core, weight, link, up0, up1, up2, up3, tiles, rows, keep, send, pair):
-    for level, up in enumerate((up0, up1, up2, up3)):
+def term_kernel(nblocks, order, bit, weight, link, tiles, rows, *refs):
+    uppers, (keep, send, pair) = refs[: len(order)], refs[len(order) :]
+    for level, up in zip(order, uppers):
         pair[level, 0, :, :256] = up[0]
         pair[level, 0, :, 256:] = up[1]
         pair[level, 1, :, :256] = -up[1]
         pair[level, 1, :, 256:] = up[0]
-    first_core = core[0] == 0
+    first_core = lax.axis_index("core") == 0
     groups = keep.shape[0]
     step = HALF // groups
-
-    def one(b, carry):
+    for b in range(nblocks):
         level = bit[b]
         lr, li = link[b, 0], link[b, 1]
         middle = (dot(lr, pair[level, 0]) + dot(li, pair[level, 1])).astype(BF16)
@@ -69,14 +68,11 @@
         second = second + tiles[b, 1]
         mine = jnp.where(first_core, first, second)
         theirs = jnp.where(first_core, second, first)
-        at = pl.ds(pl.multiple_of(b * step, step), step)
+        at = pl.ds(b * step, step)
         for y in range(groups):
             keep[y, at, :] = mine[y * step : (y + 1) * step]
             send[y, at, :] = theirs[y * step : (y + 1) * step]
         keep[0, pl.ds(nblocks * step + b, 1), :] = diagonal + rows[pl.ds(b, 1), :]
-        return carry
-
-    lax.fori_loop(0, nblocks, one, 0, unroll=UNROLL)
     tail = keep[0, pl.ds(nblocks * step, nblocks), :]
     for y in range(groups):
         for ref in (keep, send):
@@ -84,14 +80,21 @@
             ref[y, pl.ds(nblocks * (step + 1), 8), :] = jnp.zeros((8, HALF), F32)
 
 
-def pick_kernel(nblocks, slots, where, before, own, after, out):
+def chip_kernel(mine, theirs, out):
+    out[...] = (mine[...] + theirs[...]).astype(BF16)
+
+
+def pick_kernel(nblocks, slots, listed, before, own, after, out):
     groups = out.shape[0]
     step = HALF // groups
+    base = (lax.axis_index("sep") - 1) * nblocks
     position = lax.broadcasted_iota(jnp.int32, (16, HALF), 0)
     tail = pl.ds(nblocks * step, 16)
+    edges = [each[tail, :].astype(F32) for each in (before, own, after)]
     diagonals = jnp.zeros((16, HALF), F32)
     for s in range(slots):
-        side, b = where[s] // nblocks, where[s] % nblocks
+        where = listed[0, s] - base
+        side, b = where // nblocks, where % nblocks
         at = pl.ds(pl.multiple_of(b * step, step), step)
         for k, source in enumerate((before, own, after)):
 
@@ -101,16 +104,23 @@
                 for y in range(groups):
                     out[y, pl.ds(s * step, step), :] = tile
 
-        edge = jnp.where(side == 0, before[tail, :], jnp.where(side == 1, own[tail, :], after[tail, :]))
-        line = jnp.sum(jnp.where(position == b, edge.astype(F32), 0.0), axis=0, keepdims=True)
+        edge = jnp.where(side == 0, edges[0], jnp.where(side == 1, edges[1], edges[2]))
+        line = jnp.sum(jnp.where(position == b, edge, 0.0), axis=0, keepdims=True)
         diagonals = jnp.where(position == s, line, diagonals)
     for y in range(groups):
         out[y, pl.ds(slots * step, 16), :] = diagonals.astype(BF16)
 
 
-def grid_kernel(slots, core, count, own, other, values, out):
+def group_kernel(parts, out):
+    total = parts[0].astype(F32)
+    for y in range(1, parts.shape[0]):
+        total = total + parts[y].astype(F32)
+    out[...] = total.astype(BF16)
+
+
+def grid_kernel(slots, count, own, other, values, out):
     row, col = iotas()
-    first_core = core[0] == 0
+    first_core = lax.axis_index("core") == 0
     groups = own.shape[0]
     step = HALF // groups
     total = jnp.zeros(values.shape[1:], F32)
@@ -165,10 +175,10 @@
     diag, link, own_upper = diag_inverse[0], coupling[0], ancestor_inverse[0, 0]
     nblocks, slots = diag.shape[0], orbital_values.shape[1]
     nsep, groups = lax.axis_size("sep"), lax.axis_size("yh")
-    core = lax.axis_index("core").astype(jnp.int32).reshape(1)
     swap = [(0, 1), (1, 0)]
 
-    uppers = [lax.ppermute(own_upper, "sep", [(i, i ^ 1 << k) for i in range(nsep)]) for k in range(LEVELS)]
+    order = (2, 0, 3, 1)
+    uppers = [lax.ppermute(own_upper, "sep", [(i, i ^ 1 << k) for i in range(nsep)]) for k in order]
     tiles, rows = call(
         lambda *refs: weigh_kernel(nblocks, *refs),
         (shape((nblocks, 2, HALF, HALF), F32), shape((nblocks, HALF), F32)),
@@ -180,36 +190,36 @@
     step = HALF // groups
     length = nblocks * step + 16
     keep, send = call(
-        lambda *refs: term_kernel(nblocks, *refs),
+        lambda *refs: term_kernel(nblocks, order, *refs),
         (shape((groups, length, HALF), F32), shape((groups, length, HALF), F32)),
-        [SMEM, SMEM, SMEM] + [VMEM] * 7,
+        [SMEM, SMEM] + [VMEM] * (3 + LEVELS),
         [pltpu.VMEM((LEVELS, 2, 256, 512), BF16)],
         flops=2_100_000_000,
         moved=5_000_000,
         vmem=16,
-    )(ancestor_bit, core, pole_weight, link, *uppers, tiles, rows)
-    chip = (keep + lax.ppermute(send, "core", swap)).astype(BF16)
+    )(ancestor_bit, pole_weight, link, tiles, rows, *uppers)
+    received = lax.ppermute(send, "core", swap)
+    chip = call(chip_kernel, shape((groups, length, HALF), BF16), [VMEM] * 2, moved=1_400_000)(keep, received)
     parts = lax.all_to_all(chip, "yh", 0, 0, tiled=True)
-    held = jnp.sum(parts.astype(F32), axis=0).astype(BF16)
+    held = call(group_kernel, shape((length, HALF), BF16), [VMEM], moved=350_000)(parts)
 
     before = lax.ppermute(held, "sep", [(i, i + 1) for i in range(nsep - 1)])
     after = lax.ppermute(held, "sep", [(i + 1, i) for i in range(nsep - 1)])
-    where = tile_blocks[0] - (lax.axis_index("sep") - 1) * nblocks
     picked = call(
         lambda *refs: pick_kernel(nblocks, slots, *refs),
         shape((groups, slots * step + 16, HALF), BF16),
         [SMEM] + [VMEM] * 3,
         moved=500_000,
-    )(where, before, held, after)
+    )(tile_blocks, before, held, after)
     own = lax.all_to_all(picked, "yh", 0, 0, tiled=True)
     other = lax.ppermute(own, "core", swap)
     return call(
         lambda *refs: grid_kernel(slots, *refs),
         shape((1, orbital_values.shape[2]), F32),
-        [SMEM, SMEM] + [VMEM] * 3,
+        [SMEM] + [VMEM] * 3,
         flops=200_000_000,
         moved=1_300_000,
-    )(core, tile_count, own, other, orbital_values[0])
+    )(tile_count, own, other, orbital_values[0])
 
 
 def solution(mesh):

time: 89.1 us -> 82.6 us (0.927)
  blocking collectives: 13.1 us -> 28.5 us
  waiting for transfers between devices: 27.1 us -> 16.1 us
  starting transfers between devices: 36.5 us -> 27.6 us
  Pallas kernels: 8.16 us -> 6.68 us
    all_to_all x0 -> x1, blocking collectives: none -> 16.6 us  [shards(): parts = lax.all_to_all(chip, 'yh', 0, 0, tiled=True)]
    all_to_all x1 -> x0, waiting for transfers between devices: 8.8 us -> none  [shards(): parts = lax.all_to_all(chip, 'yh', 0, 0, tiled=True)]
    all_to_all x1 -> x0, starting transfers between devices: 6.82 us -> none  [shards(): parts = lax.all_to_all(chip, 'yh', 0, 0, tiled=True)]
    ppermute x4, waiting for transfers between devices: 9.87 us -> 7.7 us  [shards(): lax.ppermute(own_upper, 'sep', [(i, i ^ 1 << k) for i in range(nsep)])]
    ppermute x1, starting transfers between devices: 8.58 us -> 6.92 us  [shards(): before = lax.ppermute(held, 'sep', [(i, i + 1) for i in range(nsep - 1)])]
    pallas_call x1 -> x3, Pallas kernels: 5.24 us -> 3.74 us  [the longest x1 3.6 us: shards(): call(lambda *refs: term_kernel(nblocks, order, *refs), (shape((groups, le...]
    all_to_all x1, blocking collectives: 13.1 us -> 11.9 us  [shards(): own = lax.all_to_all(picked, 'yh', 0, 0, tiled=True)]
  transfers between devices with their start and end apart: 9 -> 8, of which waited for: 7 -> 4; matrix products, arithmetic and copies ran while one was open for 0% -> 0% of each run, Pallas kernels for 1% -> 1%
where the time goes in v6:
time: 82.6 us; the launch traced here: 82 us
  blocking collectives  28.5 us (35%)
  starting transfers between devices  27.6 us (33%)
  waiting for transfers between devices  16.1 us (19%)
  Pallas kernels  6.68 us (8%)
  local copies, waits for them, and re-layouts  2.26 us (3%)
    all_to_all x1, blocking collectives, shards(): parts = lax.all_to_all(chip, 'yh', 0, 0, tiled=True)  16.6 us
    all_to_all x1, blocking collectives, shards(): own = lax.all_to_all(picked, 'yh', 0, 0, tiled=True)  11.9 us
    ppermute x4, starting transfers between devices, shards(): lax.ppermute(own_upper, 'sep', [(i, i ^ 1 << k) for i in range(nsep)])  9.16 us
    ppermute x4, waiting for transfers between devices, shards(): lax.ppermute(own_upper, 'sep', [(i, i ^ 1 << k) for i in range(nsep)])  7.7 us
    ppermute x1, starting transfers between devices, shards(): before = lax.ppermute(held, 'sep', [(i, i + 1) for i in range(nsep - 1)])  6.92 us
    ppermute x1, waiting for transfers between devices, shards(): after = lax.ppermute(held, 'sep', [(i + 1, i) for i in range(nsep - 1)])  6.43 us
    ppermute x1, starting transfers between devices, shards(): other = lax.ppermute(own, 'core', swap)  5.99 us
    ppermute x1, starting transfers between devices, shards(): received = lax.ppermute(send, 'core', swap)  3.66 us
  transfers between devices with their start and end apart: 8, of which 4 were waited for; matrix products, arithmetic and copies ran while one was open for 0% of the time, Pallas kernels for 1%

profile of v6, /device:TPU:199, one launch (start us, length us, event | category | flops | bytes accessed | tf_op | source)
XLA Modules:
  0.0 82.0 jit_solution(10876626131026911872)
XLA Ops:
  0.0 0.0 copy-start.3
  0.0 0.0 copy-start.6
  0.0 2.0 %collective-permute-start = (bf16[2,256,256]{2,1,0:T(8,128)(2,1)}, bf16[2,256,256]{2,1,0:T(8,128)(2,1)S(1)}, u32[]{:S(2)}, u32[]{:S(2)}) collective-permute-start(bf16[2,256,256]{2,1,0:T(8,128)(2,1)} %bitcast.7), channel_id=1, source_target_pairs={{0,4},{1,5},{2,6},{3,7},{4,0},{5,1},{6,2},{7,3},{8,12},{9,13},{10,... | collective-permute-start | bytes 786440 | tf_op jit(solution)/shard_map/ppermute | solution.py:181
  2.1 2.5 %collective-permute-start.1 = (bf16[2,256,256]{2,1,0:T(8,128)(2,1)}, bf16[2,256,256]{2,1,0:T(8,128)(2,1)S(1)}, u32[]{:S(2)}, u32[]{:S(2)}) collective-permute-start(bf16[2,256,256]{2,1,0:T(8,128)(2,1)} %bitcast.8), channel_id=1, source_target_pairs={{0,1},{1,0},{2,3},{3,2},{4,5},{5,4},{6,7},{7,6},{8,9},{9,8},{10,11... | collective-permute-start | bytes 786440 | tf_op jit(solution)/shard_map/ppermute | solution.py:181
  4.5 1.9 %collective-permute-start.2 = (bf16[2,256,256]{2,1,0:T(8,128)(2,1)}, bf16[2,256,256]{2,1,0:T(8,128)(2,1)S(1)}, u32[]{:S(2)}, u32[]{:S(2)}) collective-permute-start(bf16[2,256,256]{2,1,0:T(8,128)(2,1)} %bitcast.9), channel_id=1, source_target_pairs={{0,8},{1,9},{2,10},{3,11},{4,12},{5,13},{6,14},{7,15},{8,0},{9,1},... | collective-permute-start | bytes 786440 | tf_op jit(solution)/shard_map/ppermute | solution.py:181
  6.4 2.7 %collective-permute-start.3 = (bf16[2,256,256]{2,1,0:T(8,128)(2,1)}, bf16[2,256,256]{2,1,0:T(8,128)(2,1)S(1)}, u32[]{:S(2)}, u32[]{:S(2)}) collective-permute-start(bf16[2,256,256]{2,1,0:T(8,128)(2,1)} %bitcast.10), channel_id=1, source_target_pairs={{0,2},{1,3},{2,0},{3,1},{4,6},{5,7},{6,4},{7,5},{8,10},{9,11},{10,... | collective-permute-start | bytes 786440 | tf_op jit(solution)/shard_map/ppermute | solution.py:181
  9.2 0.0 copy-start
  9.2 1.6 %copy-done = bf16[1,8,2,256,256]{4,3,2,1,0:T(8,128)(2,1)S(1)} copy-done((bf16[1,8,2,256,256]{4,3,2,1,0:T(8,128)(2,1)S(1)}, bf16[1,8,2,256,256]{4,3,2,1,0:T(8,128)(2,1)}, u32[]{:S(2)}) %copy-start) | copy-done | bytes 2097176
  10.8 0.0 copy-start.2
  10.8 0.7 copy-done.2
  11.4 0.0 copy-start.5
  11.4 1.1 %shard_map.82 = (f32[8,2,128,128]{3,2,1,0:T(8,128)S(1)}, f32[8,128]{1,0:T(8,128)S(1)}) custom-call(f32[1,2]{1,0:T(1,128)S(1)} %copy-done.2, bf16[8,2,256,256]{3,2,1,0:T(8,128)(2,1)S(1)} %bitcast.4), custom_call_target="tpu_custom_call" | custom-call | flops 2000000 | bytes 3200000 | tf_op jit(solution)/shard_map/pallas_call | solution.py:182
  12.6 0.0 collective-permute-done.refs_5_
  12.6 0.0 collective-permute-done.1.refs_6_
  12.6 7.7 %collective-permute-done.2.refs_7_ = bf16[2,256,256]{2,1,0:T(8,128)(2,1)S(1)} collective-permute-done((bf16[2,256,256]{2,1,0:T(8,128)(2,1)}, bf16[2,256,256]{2,1,0:T(8,128)(2,1)S(1)}, u32[]{:S(2)}, u32[]{:S(2)}) %collective-permute-start.2) | collective-permute-done | bytes 262176 | tf_op jit(solution)/shard_map/ppermute | solution.py:181
  20.3 0.0 collective-permute-done.3.refs_8_
  20.3 0.0 copy-done.3
  20.3 0.0 copy-done.6
  20.3 0.0 copy-done.5
  20.3 3.6 %shard_map.83 = (f32[4,272,128]{2,1,0:T(8,128)S(1)}, f32[4,272,128]{2,1,0:T(8,128)S(1)}) custom-call(s32[8]{0:T(128)S(1)} %copy-done.6, f32[1,2]{1,0:T(1,128)S(1)} %copy-done.3, bf16[8,2,256,256]{3,2,1,0:T(8,128)(2,1)S(1)} %bitcast.6, f32[8,2,128,128]{3,2,1,0:T(8,128)S(1)} %get-tuple-element.9.refs_3_, f32[8,128]{1,0:T(8,128)S(1)} %get-tuple-element.10.refs_4_, ...), custom_call_target="tpu_custom_call" | custom-call | flops 2100000000 | bytes 5000000 | tf_op jit(solution)/shard_map/pallas_call | solution.py:192
  23.9 0.0 copy-start.4
  23.9 0.0 copy-start.1
  23.9 3.7 %collective-permute-start.4 = (f32[4,272,128]{2,1,0:T(8,128)S(1)}, f32[4,272,128]{2,1,0:T(8,128)S(1)}, u32[]{:S(2)}, u32[]{:S(2)}) collective-permute-start(f32[4,272,128]{2,1,0:T(8,128)S(1)} %get-tuple-element.12), channel_id=1, source_target_pairs={{0,64},{64,0},{1,65},{65,1},{2,66},{66,2},{3,67},{67,3},{4,68},{68... | collective-permute-start | bytes 1671176 | tf_op jit(solution)/shard_map/ppermute | solution.py:201
  27.6 1.6 %collective-permute-done.4.theirs = f32[4,272,128]{2,1,0:T(8,128)S(1)} collective-permute-done((f32[4,272,128]{2,1,0:T(8,128)S(1)}, f32[4,272,128]{2,1,0:T(8,128)S(1)}, u32[]{:S(2)}, u32[]{:S(2)}) %collective-permute-start.4) | collective-permute-done | bytes 557088 | tf_op jit(solution)/shard_map/ppermute | solution.py:201
  29.2 0.1 shard_map.84
  29.3 16.6 %all_to_all.10.parts = bf16[4,272,128]{2,1,0:T(8,128)(2,1)S(1)} all-to-all(bf16[4,272,128]{2,1,0:T(8,128)(2,1)S(1)} %shard_map.84), channel_id=1, replica_groups=mesh['yh'=4,'core'=2,'sep'=64] {'yh'}, dimensions={0} | all-to-all | bytes 557056 | tf_op jit(solution)/shard_map/all_to_all | solution.py:203
  45.9 6.9 %collective-permute-start.5 = (bf16[272,128]{1,0:T(8,128)(2,1)S(1)}, bf16[272,128]{1,0:T(8,128)(2,1)S(1)}, u32[]{:S(2)}, u32[]{:S(2)}) collective-permute-start(bf16[272,128]{1,0:T(8,128)(2,1)S(1)} %shard_map.85.refs_2_), channel_id=1, source_target_pairs={{0,1},{1,2},{2,3},{3,4},{4,5},{5,6},{6,7},{7,8},{8,9},{9,10},{10,1... | collective-permute-start | bytes 208904 | tf_op jit(solution)/shard_map/ppermute | solution.py:206
  52.8 1.9 %collective-permute-start.6 = (bf16[272,128]{1,0:T(8,128)(2,1)S(1)}, bf16[272,128]{1,0:T(8,128)(2,1)S(1)}, u32[]{:S(2)}, u32[]{:S(2)}) collective-permute-start(bf16[272,128]{1,0:T(8,128)(2,1)S(1)} %shard_map.85.refs_2_), channel_id=1, source_target_pairs={{1,0},{2,1},{3,2},{4,3},{5,4},{6,5},{7,6},{8,7},{9,8},{10,9},{11,1... | collective-permute-start | bytes 208904 | tf_op jit(solution)/shard_map/ppermute | solution.py:207
  54.8 0.0 collective-permute-done.5.refs_1_
  54.8 6.4 %collective-permute-done.6.refs_3_ = bf16[272,128]{1,0:T(8,128)(2,1)S(1)} collective-permute-done((bf16[272,128]{1,0:T(8,128)(2,1)S(1)}, bf16[272,128]{1,0:T(8,128)(2,1)S(1)}, u32[]{:S(2)}, u32[]{:S(2)}) %collective-permute-start.6) | collective-permute-done | bytes 69664 | tf_op jit(solution)/shard_map/ppermute | solution.py:207
  61.2 0.0 copy-done.4
  61.2 0.7 shard_map.86
  62.0 11.9 %all_to_all.11.refs_1_ = bf16[4,208,128]{2,1,0:T(8,128)(2,1)S(1)} all-to-all(bf16[4,208,128]{2,1,0:T(8,128)(2,1)S(1)} %shard_map.86), channel_id=1, replica_groups=mesh['yh'=4,'core'=2,'sep'=64] {'yh'}, dimensions={0} | all-to-all | bytes 425984 | tf_op jit(solution)/shard_map/all_to_all | solution.py:214
  73.9 6.0 %collective-permute-start.7 = (bf16[4,208,128]{2,1,0:T(8,128)(2,1)S(1)}, bf16[4,208,128]{2,1,0:T(8,128)(2,1)S(1)}, u32[]{:S(2)}, u32[]{:S(2)}) collective-permute-start(bf16[4,208,128]{2,1,0:T(8,128)(2,1)S(1)} %all_to_all.11.refs_1_), channel_id=1, source_target_pairs={{0,64},{64,0},{1,65},{65,1},{2,66},{66,2},{3,67},{67,3},{4,68},{68... | collective-permute-start | bytes 638984 | tf_op jit(solution)/shard_map/ppermute | solution.py:215
  80.5 0.4 collective-permute-done.7.refs_2_
  80.9 0.0 copy-done.1
  80.9 1.1 %shard_map.87 = f32[1,256]{1,0:T(1,128)} custom-call(s32[1]{0:T(128)S(6)} %copy.9.refs_0_, bf16[4,208,128]{2,1,0:T(8,128)(2,1)S(1)} %all_to_all.11.refs_1_, bf16[4,208,128]{2,1,0:T(8,128)(2,1)S(1)} %collective-permute-done.7.refs_2_, bf16[6,256,256]{2,1,0:T(8,128)(2,1)S(1)} %bitcast.5), custom_call_target="tpu_custom_call" | custom-call | flops 200000000 | bytes 1300000 | tf_op jit(solution)/shard_map/pallas_call | solution.py:216
  (1 shorter events, 0.0 us)
Async XLA Ops:
  0.0 20.3 %copy-start.3 = (f32[1,2]{1,0:T(1,128)S(1)}, f32[1,2]{1,0:T(1,128)}, u32[]{:S(2)}) copy-start(f32[1,2]{1,0:T(1,128)} %refs_1_.1) | copy-start | bytes 28
  0.0 20.3 %copy-start.6 = (s32[8]{0:T(128)S(1)}, s32[8]{0:T(128)}, u32[]{:S(2)}) copy-start(s32[8]{0:T(128)} %refs_0_.5) | copy-start | bytes 100
  0.0 12.6 %collective-permute-start = (bf16[2,256,256]{2,1,0:T(8,128)(2,1)}, bf16[2,256,256]{2,1,0:T(8,128)(2,1)S(1)}, u32[]{:S(2)}, u32[]{:S(2)}) collective-permute-start(bf16[2,256,256]{2,1,0:T(8,128)(2,1)} %bitcast.7), channel_id=1, source_target_pairs={{0,4},{1,5},{2,6},{3,7},{4,0},{5,1},{6,2},{7,3},{8,12},{9,13},{10,... | collective-permute-start | bytes 786440 | tf_op jit(solution)/shard_map/ppermute | solution.py:181
  2.1 10.5 %collective-permute-start.1 = (bf16[2,256,256]{2,1,0:T(8,128)(2,1)}, bf16[2,256,256]{2,1,0:T(8,128)(2,1)S(1)}, u32[]{:S(2)}, u32[]{:S(2)}) collective-permute-start(bf16[2,256,256]{2,1,0:T(8,128)(2,1)} %bitcast.8), channel_id=1, source_target_pairs={{0,1},{1,0},{2,3},{3,2},{4,5},{5,4},{6,7},{7,6},{8,9},{9,8},{10,11... | collective-permute-start | bytes 786440 | tf_op jit(solution)/shard_map/ppermute | solution.py:181
  4.5 15.8 %collective-permute-start.2 = (bf16[2,256,256]{2,1,0:T(8,128)(2,1)}, bf16[2,256,256]{2,1,0:T(8,128)(2,1)S(1)}, u32[]{:S(2)}, u32[]{:S(2)}) collective-permute-start(bf16[2,256,256]{2,1,0:T(8,128)(2,1)} %bitcast.9), channel_id=1, source_target_pairs={{0,8},{1,9},{2,10},{3,11},{4,12},{5,13},{6,14},{7,15},{8,0},{9,1},... | collective-permute-start | bytes 786440 | tf_op jit(solution)/shard_map/ppermute | solution.py:181
  6.4 13.8 %collective-permute-start.3 = (bf16[2,256,256]{2,1,0:T(8,128)(2,1)}, bf16[2,256,256]{2,1,0:T(8,128)(2,1)S(1)}, u32[]{:S(2)}, u32[]{:S(2)}) collective-permute-start(bf16[2,256,256]{2,1,0:T(8,128)(2,1)} %bitcast.10), channel_id=1, source_target_pairs={{0,2},{1,3},{2,0},{3,1},{4,6},{5,7},{6,4},{7,5},{8,10},{9,11},{10,... | collective-permute-start | bytes 786440 | tf_op jit(solution)/shard_map/ppermute | solution.py:181
  9.2 1.6 %copy-start = (bf16[1,8,2,256,256]{4,3,2,1,0:T(8,128)(2,1)S(1)}, bf16[1,8,2,256,256]{4,3,2,1,0:T(8,128)(2,1)}, u32[]{:S(2)}) copy-start(bf16[1,8,2,256,256]{4,3,2,1,0:T(8,128)(2,1)} %param.8) | copy-start | bytes 6291460
  10.8 0.7 copy-start.2
  11.4 8.9 %copy-start.5 = (bf16[1,8,2,256,256]{4,3,2,1,0:T(8,128)(2,1)S(1)}, bf16[1,8,2,256,256]{4,3,2,1,0:T(8,128)(2,1)}, u32[]{:S(2)}) copy-start(bf16[1,8,2,256,256]{4,3,2,1,0:T(8,128)(2,1)} %param.9) | copy-start | bytes 6291460
  23.9 37.3 %copy-start.4 = (s32[1,6]{1,0:T(1,128)S(1)}, s32[1,6]{1,0:T(1,128)}, u32[]{:S(2)}) copy-start(s32[1,6]{1,0:T(1,128)} %refs_0_.6) | copy-start | bytes 76
  23.9 57.0 %copy-start.1 = (bf16[1,6,256,256]{3,2,1,0:T(8,128)(2,1)S(1)}, bf16[1,6,256,256]{3,2,1,0:T(8,128)(2,1)}, u32[]{:S(2)}) copy-start(bf16[1,6,256,256]{3,2,1,0:T(8,128)(2,1)} %param.15) | copy-start | bytes 2359300
  23.9 5.2 %collective-permute-start.4 = (f32[4,272,128]{2,1,0:T(8,128)S(1)}, f32[4,272,128]{2,1,0:T(8,128)S(1)}, u32[]{:S(2)}, u32[]{:S(2)}) collective-permute-start(f32[4,272,128]{2,1,0:T(8,128)S(1)} %get-tuple-element.12), channel_id=1, source_target_pairs={{0,64},{64,0},{1,65},{65,1},{2,66},{66,2},{3,67},{67,3},{4,68},{68... | collective-permute-start | bytes 1671176 | tf_op jit(solution)/shard_map/ppermute | solution.py:201
  45.9 8.9 %collective-permute-start.5 = (bf16[272,128]{1,0:T(8,128)(2,1)S(1)}, bf16[272,128]{1,0:T(8,128)(2,1)S(1)}, u32[]{:S(2)}, u32[]{:S(2)}) collective-permute-start(bf16[272,128]{1,0:T(8,128)(2,1)S(1)} %shard_map.85.refs_2_), channel_id=1, source_target_pairs={{0,1},{1,2},{2,3},{3,4},{4,5},{5,6},{6,7},{7,8},{8,9},{9,10},{10,1... | collective-permute-start | bytes 208904 | tf_op jit(solution)/shard_map/ppermute | solution.py:206
  52.8 8.4 %collective-permute-start.6 = (bf16[272,128]{1,0:T(8,128)(2,1)S(1)}, bf16[272,128]{1,0:T(8,128)(2,1)S(1)}, u32[]{:S(2)}, u32[]{:S(2)}) collective-permute-start(bf16[272,128]{1,0:T(8,128)(2,1)S(1)} %shard_map.85.refs_2_), channel_id=1, source_target_pairs={{1,0},{2,1},{3,2},{4,3},{5,4},{6,5},{7,6},{8,7},{9,8},{10,9},{11,1... | collective-permute-start | bytes 208904 | tf_op jit(solution)/shard_map/ppermute | solution.py:207
  73.9 7.1 %collective-permute-start.7 = (bf16[4,208,128]{2,1,0:T(8,128)(2,1)S(1)}, bf16[4,208,128]{2,1,0:T(8,128)(2,1)S(1)}, u32[]{:S(2)}, u32[]{:S(2)}) collective-permute-start(bf16[4,208,128]{2,1,0:T(8,128)(2,1)S(1)} %all_to_all.11.refs_1_), channel_id=1, source_target_pairs={{0,64},{64,0},{1,65},{65,1},{2,66},{66,2},{3,67},{67,3},{4,68},{68... | collective-permute-start | bytes 638984 | tf_op jit(solution)/shard_map/ppermute | solution.py:215

commit v7 on v6

--- a/solution.py
+++ b/solution.py
@@ -71,55 +71,54 @@
         at = pl.ds(b * step, step)
         for y in range(groups):
             keep[y, at, :] = mine[y * step : (y + 1) * step]
-            send[y, at, :] = theirs[y * step : (y + 1) * step]
+            send[y, at, :] = theirs[y * step : (y + 1) * step].astype(BF16)
         keep[0, pl.ds(nblocks * step + b, 1), :] = diagonal + rows[pl.ds(b, 1), :]
-    tail = keep[0, pl.ds(nblocks * step, nblocks), :]
+    tail = pl.ds(nblocks * step, 16)
+    keep[0, pl.ds(nblocks * step + nblocks, 16 - nblocks), :] = jnp.zeros((16 - nblocks, HALF), F32)
+    edge = keep[0, tail, :]
     for y in range(groups):
-        for ref in (keep, send):
-            ref[y, pl.ds(nblocks * step, nblocks), :] = tail
-            ref[y, pl.ds(nblocks * (step + 1), 8), :] = jnp.zeros((8, HALF), F32)
+        keep[y, tail, :] = edge
+        send[y, tail, :] = edge.astype(BF16)
 
 
 def chip_kernel(mine, theirs, out):
-    out[...] = (mine[...] + theirs[...]).astype(BF16)
-
-
-def pick_kernel(nblocks, slots, listed, before, own, after, out):
-    groups = out.shape[0]
+    out[...] = (mine[...] + theirs[...].astype(F32)).astype(BF16)
+
+
+def pick_kernel(nblocks, slots, listed, before, own, after, out, near):
+    groups, length = out.shape[0], own.shape[0]
     step = HALF // groups
     base = (lax.axis_index("sep") - 1) * nblocks
     position = lax.broadcasted_iota(jnp.int32, (16, HALF), 0)
-    tail = pl.ds(nblocks * step, 16)
-    edges = [each[tail, :].astype(F32) for each in (before, own, after)]
+    for k, source in enumerate((before, own, after)):
+        near[pl.ds(k * length, length), :] = source[...]
     diagonals = jnp.zeros((16, HALF), F32)
     for s in range(slots):
         where = listed[0, s] - base
         side, b = where // nblocks, where % nblocks
-        at = pl.ds(pl.multiple_of(b * step, step), step)
-        for k, source in enumerate((before, own, after)):
-
-            @pl.when(side == k)
-            def _():
-                tile = source[at, :]
-                for y in range(groups):
-                    out[y, pl.ds(s * step, step), :] = tile
-
-        edge = jnp.where(side == 0, edges[0], jnp.where(side == 1, edges[1], edges[2]))
+        tile = near[pl.ds(pl.multiple_of(side * length + b * step, 16), step), :]
+        for y in range(groups):
+            out[y, pl.ds(s * step, step), :] = tile
+        edge = near[pl.ds(pl.multiple_of(side * length + nblocks * step, 16), 16), :].astype(F32)
         line = jnp.sum(jnp.where(position == b, edge, 0.0), axis=0, keepdims=True)
         diagonals = jnp.where(position == s, line, diagonals)
     for y in range(groups):
         out[y, pl.ds(slots * step, 16), :] = diagonals.astype(BF16)
 
 
-def group_kernel(parts, out):
-    total = parts[0].astype(F32)
-    for y in range(1, parts.shape[0]):
-        total = total + parts[y].astype(F32)
+def group_kernel(parts, keep, received, out):
+    me = lax.axis_index("yh")
+    total = keep[me] + received[me].astype(F32)
+    for y in range(parts.shape[0]):
+        total = total + jnp.where(me == y, 0.0, parts[y].astype(F32))
     out[...] = total.astype(BF16)
 
 
 def grid_kernel(slots, count, own, other, values, out):
     row, col = iotas()
+    upper, lower, middle = [
+        jnp.where(mask, 1.0, 0.0).astype(BF16) for mask in (col >= row, col < row, col == row)
+    ]
     first_core = lax.axis_index("core") == 0
     groups = own.shape[0]
     step = HALF // groups
@@ -127,17 +126,15 @@
     lines = own[0, pl.ds(slots * step, 16), :].astype(F32)
     for s in range(slots):
         at = pl.ds(s * step, step)
-        mine = jnp.concatenate([own[y, at, :] for y in range(groups)], axis=0).astype(F32)
-        theirs = jnp.concatenate([other[y, at, :] for y in range(groups)], axis=0).astype(F32)
+        mine = jnp.concatenate([own[y, at, :] for y in range(groups)], axis=0)
+        theirs = jnp.concatenate([other[y, at, :] for y in range(groups)], axis=0)
         first = jnp.where(first_core, mine, theirs)
         second = jnp.where(first_core, theirs, mine)
-        upper = jnp.where(col >= row, first, 0.0)
-        lower = jnp.where(col < row, first, jnp.where(col == row, lines[s : s + 1], 0.0))
-        top = jnp.concatenate([upper, second], axis=1)
-        bottom = jnp.concatenate([jnp.zeros_like(lower), lower], axis=1)
-        block = jnp.concatenate([top, bottom], axis=0).astype(BF16)
+        line = jnp.broadcast_to(lines[s : s + 1], (HALF, HALF)).astype(BF16)
+        top = jnp.concatenate([first * upper, second], axis=1)
+        bottom = jnp.concatenate([jnp.zeros_like(first), first * lower + line * middle], axis=1)
         v = values[s]
-        inner = dot(v, block)
+        inner = dot(v, jnp.concatenate([top, bottom], axis=0))
         total = total + jnp.where(s < count[0], v.astype(F32) * inner, 0.0)
     narrow = total[:, :HALF] + total[:, HALF:]
     for k in range(narrow.shape[0] // HALF):
@@ -191,7 +188,7 @@
     length = nblocks * step + 16
     keep, send = call(
         lambda *refs: term_kernel(nblocks, order, *refs),
-        (shape((groups, length, HALF), F32), shape((groups, length, HALF), F32)),
+        (shape((groups, length, HALF), F32), shape((groups, length, HALF), BF16)),
         [SMEM, SMEM] + [VMEM] * (3 + LEVELS),
         [pltpu.VMEM((LEVELS, 2, 256, 512), BF16)],
         flops=2_100_000_000,
@@ -201,7 +198,7 @@
     received = lax.ppermute(send, "core", swap)
     chip = call(chip_kernel, shape((groups, length, HALF), BF16), [VMEM] * 2, moved=1_400_000)(keep, received)
     parts = lax.all_to_all(chip, "yh", 0, 0, tiled=True)
-    held = call(group_kernel, shape((length, HALF), BF16), [VMEM], moved=350_000)(parts)
+    held = call(group_kernel, shape((length, HALF), BF16), [VMEM] * 3, moved=600_000)(parts, keep, received)
 
     before = lax.ppermute(held, "sep", [(i, i + 1) for i in range(nsep - 1)])
     after = lax.ppermute(held, "sep", [(i + 1, i) for i in range(nsep - 1)])
@@ -209,6 +206,7 @@
         lambda *refs: pick_kernel(nblocks, slots, *refs),
         shape((groups, slots * step + 16, HALF), BF16),
         [SMEM] + [VMEM] * 3,
+        [pltpu.VMEM((3 * length, HALF), BF16)],
         moved=500_000,
     )(tile_blocks, before, held, after)
     own = lax.all_to_all(picked, "yh", 0, 0, tiled=True)

time: 82.6 us -> 82 us (level)
  no operation moved by 1% of the time
where the time goes in v7:
time: 82 us; the launch traced here: 81.5 us
  blocking collectives  28.5 us (35%)
  starting transfers between devices  27.6 us (34%)
  waiting for transfers between devices  15.7 us (19%)
  Pallas kernels  6.54 us (8%)
  local copies, waits for them, and re-layouts  2.26 us (3%)
    all_to_all x1, blocking collectives, shards(): parts = lax.all_to_all(chip, 'yh', 0, 0, tiled=True)  16.6 us
    all_to_all x1, blocking collectives, shards(): own = lax.all_to_all(picked, 'yh', 0, 0, tiled=True)  11.9 us
    ppermute x4, starting transfers between devices, shards(): lax.ppermute(own_upper, 'sep', [(i, i ^ 1 << k) for i in range(nsep)])  9.16 us
    ppermute x4, waiting for transfers between devices, shards(): lax.ppermute(own_upper, 'sep', [(i, i ^ 1 << k) for i in range(nsep)])  7.7 us
    ppermute x1, starting transfers between devices, shards(): before = lax.ppermute(held, 'sep', [(i, i + 1) for i in range(nsep - 1)])  6.92 us
    ppermute x1, waiting for transfers between devices, shards(): after = lax.ppermute(held, 'sep', [(i + 1, i) for i in range(nsep - 1)])  6.43 us
    ppermute x1, starting transfers between devices, shards(): other = lax.ppermute(own, 'core', swap)  5.98 us
    ppermute x1, starting transfers between devices, shards(): received = lax.ppermute(send, 'core', swap)  3.66 us
  transfers between devices with their start and end apart: 8, of which 4 were waited for; matrix products, arithmetic and copies ran while one was open for 0% of the time, Pallas kernels for 1%

profile of v7, /device:TPU:199, one launch (start us, length us, event | category | flops | bytes accessed | tf_op | source)
XLA Modules:
  0.0 81.5 jit_solution(8784505800360074820)
XLA Ops:
  0.0 0.0 copy-start.3
  0.0 0.0 copy-start.6
  0.0 2.0 %collective-permute-start = (bf16[2,256,256]{2,1,0:T(8,128)(2,1)}, bf16[2,256,256]{2,1,0:T(8,128)(2,1)S(1)}, u32[]{:S(2)}, u32[]{:S(2)}) collective-permute-start(bf16[2,256,256]{2,1,0:T(8,128)(2,1)} %bitcast.7), channel_id=1, source_target_pairs={{0,4},{1,5},{2,6},{3,7},{4,0},{5,1},{6,2},{7,3},{8,12},{9,13},{10,... | collective-permute-start | bytes 786440 | tf_op jit(solution)/shard_map/ppermute | solution.py:178
  2.1 2.5 %collective-permute-start.1 = (bf16[2,256,256]{2,1,0:T(8,128)(2,1)}, bf16[2,256,256]{2,1,0:T(8,128)(2,1)S(1)}, u32[]{:S(2)}, u32[]{:S(2)}) collective-permute-start(bf16[2,256,256]{2,1,0:T(8,128)(2,1)} %bitcast.8), channel_id=1, source_target_pairs={{0,1},{1,0},{2,3},{3,2},{4,5},{5,4},{6,7},{7,6},{8,9},{9,8},{10,11... | collective-permute-start | bytes 786440 | tf_op jit(solution)/shard_map/ppermute | solution.py:178
  4.5 1.9 %collective-permute-start.2 = (bf16[2,256,256]{2,1,0:T(8,128)(2,1)}, bf16[2,256,256]{2,1,0:T(8,128)(2,1)S(1)}, u32[]{:S(2)}, u32[]{:S(2)}) collective-permute-start(bf16[2,256,256]{2,1,0:T(8,128)(2,1)} %bitcast.9), channel_id=1, source_target_pairs={{0,8},{1,9},{2,10},{3,11},{4,12},{5,13},{6,14},{7,15},{8,0},{9,1},... | collective-permute-start | bytes 786440 | tf_op jit(solution)/shard_map/ppermute | solution.py:178
  6.4 2.7 %collective-permute-start.3 = (bf16[2,256,256]{2,1,0:T(8,128)(2,1)}, bf16[2,256,256]{2,1,0:T(8,128)(2,1)S(1)}, u32[]{:S(2)}, u32[]{:S(2)}) collective-permute-start(bf16[2,256,256]{2,1,0:T(8,128)(2,1)} %bitcast.10), channel_id=1, source_target_pairs={{0,2},{1,3},{2,0},{3,1},{4,6},{5,7},{6,4},{7,5},{8,10},{9,11},{10,... | collective-permute-start | bytes 786440 | tf_op jit(solution)/shard_map/ppermute | solution.py:178
  9.2 0.0 copy-start
  9.2 1.6 %copy-done = bf16[1,8,2,256,256]{4,3,2,1,0:T(8,128)(2,1)S(1)} copy-done((bf16[1,8,2,256,256]{4,3,2,1,0:T(8,128)(2,1)S(1)}, bf16[1,8,2,256,256]{4,3,2,1,0:T(8,128)(2,1)}, u32[]{:S(2)}) %copy-start) | copy-done | bytes 2097176
  10.8 0.0 copy-start.2
  10.8 0.7 copy-done.2
  11.4 0.0 copy-start.5
  11.4 1.1 %shard_map.82 = (f32[8,2,128,128]{3,2,1,0:T(8,128)S(1)}, f32[8,128]{1,0:T(8,128)S(1)}) custom-call(f32[1,2]{1,0:T(1,128)S(1)} %copy-done.2, bf16[8,2,256,256]{3,2,1,0:T(8,128)(2,1)S(1)} %bitcast.4), custom_call_target="tpu_custom_call" | custom-call | flops 2000000 | bytes 3200000 | tf_op jit(solution)/shard_map/pallas_call | solution.py:179
  12.6 0.0 collective-permute-done.refs_5_
  12.6 0.0 collective-permute-done.1.refs_6_
  12.6 7.7 %collective-permute-done.2.refs_7_ = bf16[2,256,256]{2,1,0:T(8,128)(2,1)S(1)} collective-permute-done((bf16[2,256,256]{2,1,0:T(8,128)(2,1)}, bf16[2,256,256]{2,1,0:T(8,128)(2,1)S(1)}, u32[]{:S(2)}, u32[]{:S(2)}) %collective-permute-start.2) | collective-permute-done | bytes 262176 | tf_op jit(solution)/shard_map/ppermute | solution.py:178
  20.3 0.0 collective-permute-done.3.refs_8_
  20.3 0.0 copy-done.3
  20.3 0.0 copy-done.6
  20.3 0.0 copy-done.5
  20.3 3.6 %shard_map.83 = (f32[4,272,128]{2,1,0:T(8,128)S(1)}, bf16[4,272,128]{2,1,0:T(8,128)(2,1)S(1)}) custom-call(s32[8]{0:T(128)S(1)} %copy-done.6, f32[1,2]{1,0:T(1,128)S(1)} %copy-done.3, bf16[8,2,256,256]{3,2,1,0:T(8,128)(2,1)S(1)} %bitcast.6, f32[8,2,128,128]{3,2,1,0:T(8,128)S(1)} %get-tuple-element.9.refs_3_, f32[8,128]{1,0:T(8,128)S(1)} %get-tuple-element.10.refs_4_, ...), custom_call_target="tpu_custom_call" | custom-call | flops 2100000000 | bytes 5000000 | tf_op jit(solution)/shard_map/pallas_call | solution.py:189
  23.9 0.0 copy-start.4
  23.9 0.0 copy-start.1
  23.9 3.7 %collective-permute-start.4 = (bf16[4,272,128]{2,1,0:T(8,128)(2,1)S(1)}, bf16[4,272,128]{2,1,0:T(8,128)(2,1)S(1)}, u32[]{:S(2)}, u32[]{:S(2)}) collective-permute-start(bf16[4,272,128]{2,1,0:T(8,128)(2,1)S(1)} %get-tuple-element.12), channel_id=1, source_target_pairs={{0,64},{64,0},{1,65},{65,1},{2,66},{66,2},{3,67},{67,3},{4,68},{68... | collective-permute-start | bytes 835592 | tf_op jit(solution)/shard_map/ppermute | solution.py:198
  27.6 1.2 %collective-permute-done.4.theirs.received = bf16[4,272,128]{2,1,0:T(8,128)(2,1)S(1)} collective-permute-done((bf16[4,272,128]{2,1,0:T(8,128)(2,1)S(1)}, bf16[4,272,128]{2,1,0:T(8,128)(2,1)S(1)}, u32[]{:S(2)}, u32[]{:S(2)}) %collective-permute-start.4) | collective-permute-done | bytes 278560 | tf_op jit(solution)/shard_map/ppermute | solution.py:198
  28.8 0.1 shard_map.84
  28.8 16.6 %all_to_all.10.parts = bf16[4,272,128]{2,1,0:T(8,128)(2,1)S(1)} all-to-all(bf16[4,272,128]{2,1,0:T(8,128)(2,1)S(1)} %shard_map.84), channel_id=1, replica_groups=mesh['yh'=4,'core'=2,'sep'=64] {'yh'}, dimensions={0} | all-to-all | bytes 557056 | tf_op jit(solution)/shard_map/all_to_all | solution.py:200
  45.5 0.1 shard_map.85.refs_2_
  45.5 6.9 %collective-permute-start.5 = (bf16[272,128]{1,0:T(8,128)(2,1)S(1)}, bf16[272,128]{1,0:T(8,128)(2,1)S(1)}, u32[]{:S(2)}, u32[]{:S(2)}) collective-permute-start(bf16[272,128]{1,0:T(8,128)(2,1)S(1)} %shard_map.85.refs_2_), channel_id=1, source_target_pairs={{0,1},{1,2},{2,3},{3,4},{4,5},{5,6},{6,7},{7,8},{8,9},{9,10},{10,1... | collective-permute-start | bytes 208904 | tf_op jit(solution)/shard_map/ppermute | solution.py:203
  52.5 1.9 %collective-permute-start.6 = (bf16[272,128]{1,0:T(8,128)(2,1)S(1)}, bf16[272,128]{1,0:T(8,128)(2,1)S(1)}, u32[]{:S(2)}, u32[]{:S(2)}) collective-permute-start(bf16[272,128]{1,0:T(8,128)(2,1)S(1)} %shard_map.85.refs_2_), channel_id=1, source_target_pairs={{1,0},{2,1},{3,2},{4,3},{5,4},{6,5},{7,6},{8,7},{9,8},{10,9},{11,1... | collective-permute-start | bytes 208904 | tf_op jit(solution)/shard_map/ppermute | solution.py:204
  54.4 0.0 collective-permute-done.5.refs_1_
  54.4 6.4 %collective-permute-done.6.refs_3_ = bf16[272,128]{1,0:T(8,128)(2,1)S(1)} collective-permute-done((bf16[272,128]{1,0:T(8,128)(2,1)S(1)}, bf16[272,128]{1,0:T(8,128)(2,1)S(1)}, u32[]{:S(2)}, u32[]{:S(2)}) %collective-permute-start.6) | collective-permute-done | bytes 69664 | tf_op jit(solution)/shard_map/ppermute | solution.py:204
  60.8 0.0 copy-done.4
  60.8 0.6 shard_map.86
  61.5 11.9 %all_to_all.11.refs_1_ = bf16[4,208,128]{2,1,0:T(8,128)(2,1)S(1)} all-to-all(bf16[4,208,128]{2,1,0:T(8,128)(2,1)S(1)} %shard_map.86), channel_id=1, replica_groups=mesh['yh'=4,'core'=2,'sep'=64] {'yh'}, dimensions={0} | all-to-all | bytes 425984 | tf_op jit(solution)/shard_map/all_to_all | solution.py:212
  73.4 6.0 %collective-permute-start.7 = (bf16[4,208,128]{2,1,0:T(8,128)(2,1)S(1)}, bf16[4,208,128]{2,1,0:T(8,128)(2,1)S(1)}, u32[]{:S(2)}, u32[]{:S(2)}) collective-permute-start(bf16[4,208,128]{2,1,0:T(8,128)(2,1)S(1)} %all_to_all.11.refs_1_), channel_id=1, source_target_pairs={{0,64},{64,0},{1,65},{65,1},{2,66},{66,2},{3,67},{67,3},{4,68},{68... | collective-permute-start | bytes 638984 | tf_op jit(solution)/shard_map/ppermute | solution.py:213
  80.0 0.4 collective-permute-done.7.refs_2_
  80.5 0.0 copy-done.1
  80.5 1.0 %shard_map.87 = f32[1,256]{1,0:T(1,128)} custom-call(s32[1]{0:T(128)S(6)} %copy.9.refs_0_, bf16[4,208,128]{2,1,0:T(8,128)(2,1)S(1)} %all_to_all.11.refs_1_, bf16[4,208,128]{2,1,0:T(8,128)(2,1)S(1)} %collective-permute-done.7.refs_2_, bf16[6,256,256]{2,1,0:T(8,128)(2,1)S(1)} %bitcast.5), custom_call_target="tpu_custom_call" | custom-call | flops 200000000 | bytes 1300000 | tf_op jit(solution)/shard_map/pallas_call | solution.py:214
Async XLA Ops:
  0.0 20.3 %copy-start.3 = (f32[1,2]{1,0:T(1,128)S(1)}, f32[1,2]{1,0:T(1,128)}, u32[]{:S(2)}) copy-start(f32[1,2]{1,0:T(1,128)} %refs_1_.1) | copy-start | bytes 28
  0.0 20.3 %copy-start.6 = (s32[8]{0:T(128)S(1)}, s32[8]{0:T(128)}, u32[]{:S(2)}) copy-start(s32[8]{0:T(128)} %refs_0_.5) | copy-start | bytes 100
  0.0 12.6 %collective-permute-start = (bf16[2,256,256]{2,1,0:T(8,128)(2,1)}, bf16[2,256,256]{2,1,0:T(8,128)(2,1)S(1)}, u32[]{:S(2)}, u32[]{:S(2)}) collective-permute-start(bf16[2,256,256]{2,1,0:T(8,128)(2,1)} %bitcast.7), channel_id=1, source_target_pairs={{0,4},{1,5},{2,6},{3,7},{4,0},{5,1},{6,2},{7,3},{8,12},{9,13},{10,... | collective-permute-start | bytes 786440 | tf_op jit(solution)/shard_map/ppermute | solution.py:178
  2.1 10.5 %collective-permute-start.1 = (bf16[2,256,256]{2,1,0:T(8,128)(2,1)}, bf16[2,256,256]{2,1,0:T(8,128)(2,1)S(1)}, u32[]{:S(2)}, u32[]{:S(2)}) collective-permute-start(bf16[2,256,256]{2,1,0:T(8,128)(2,1)} %bitcast.8), channel_id=1, source_target_pairs={{0,1},{1,0},{2,3},{3,2},{4,5},{5,4},{6,7},{7,6},{8,9},{9,8},{10,11... | collective-permute-start | bytes 786440 | tf_op jit(solution)/shard_map/ppermute | solution.py:178
  4.5 15.8 %collective-permute-start.2 = (bf16[2,256,256]{2,1,0:T(8,128)(2,1)}, bf16[2,256,256]{2,1,0:T(8,128)(2,1)S(1)}, u32[]{:S(2)}, u32[]{:S(2)}) collective-permute-start(bf16[2,256,256]{2,1,0:T(8,128)(2,1)} %bitcast.9), channel_id=1, source_target_pairs={{0,8},{1,9},{2,10},{3,11},{4,12},{5,13},{6,14},{7,15},{8,0},{9,1},... | collective-permute-start | bytes 786440 | tf_op jit(solution)/shard_map/ppermute | solution.py:178
  6.4 13.8 %collective-permute-start.3 = (bf16[2,256,256]{2,1,0:T(8,128)(2,1)}, bf16[2,256,256]{2,1,0:T(8,128)(2,1)S(1)}, u32[]{:S(2)}, u32[]{:S(2)}) collective-permute-start(bf16[2,256,256]{2,1,0:T(8,128)(2,1)} %bitcast.10), channel_id=1, source_target_pairs={{0,2},{1,3},{2,0},{3,1},{4,6},{5,7},{6,4},{7,5},{8,10},{9,11},{10,... | collective-permute-start | bytes 786440 | tf_op jit(solution)/shard_map/ppermute | solution.py:178
  9.2 1.6 %copy-start = (bf16[1,8,2,256,256]{4,3,2,1,0:T(8,128)(2,1)S(1)}, bf16[1,8,2,256,256]{4,3,2,1,0:T(8,128)(2,1)}, u32[]{:S(2)}) copy-start(bf16[1,8,2,256,256]{4,3,2,1,0:T(8,128)(2,1)} %param.8) | copy-start | bytes 6291460
  10.8 0.7 copy-start.2
  11.4 8.9 %copy-start.5 = (bf16[1,8,2,256,256]{4,3,2,1,0:T(8,128)(2,1)S(1)}, bf16[1,8,2,256,256]{4,3,2,1,0:T(8,128)(2,1)}, u32[]{:S(2)}) copy-start(bf16[1,8,2,256,256]{4,3,2,1,0:T(8,128)(2,1)} %param.9) | copy-start | bytes 6291460
  23.9 36.9 %copy-start.4 = (s32[1,6]{1,0:T(1,128)S(1)}, s32[1,6]{1,0:T(1,128)}, u32[]{:S(2)}) copy-start(s32[1,6]{1,0:T(1,128)} %refs_0_.6) | copy-start | bytes 76
  23.9 56.5 %copy-start.1 = (bf16[1,6,256,256]{3,2,1,0:T(8,128)(2,1)S(1)}, bf16[1,6,256,256]{3,2,1,0:T(8,128)(2,1)}, u32[]{:S(2)}) copy-start(bf16[1,6,256,256]{3,2,1,0:T(8,128)(2,1)} %param.15) | copy-start | bytes 2359300
  23.9 4.8 %collective-permute-start.4 = (bf16[4,272,128]{2,1,0:T(8,128)(2,1)S(1)}, bf16[4,272,128]{2,1,0:T(8,128)(2,1)S(1)}, u32[]{:S(2)}, u32[]{:S(2)}) collective-permute-start(bf16[4,272,128]{2,1,0:T(8,128)(2,1)S(1)} %get-tuple-element.12), channel_id=1, source_target_pairs={{0,64},{64,0},{1,65},{65,1},{2,66},{66,2},{3,67},{67,3},{4,68},{68... | collective-permute-start | bytes 835592 | tf_op jit(solution)/shard_map/ppermute | solution.py:198
  45.5 8.9 %collective-permute-start.5 = (bf16[272,128]{1,0:T(8,128)(2,1)S(1)}, bf16[272,128]{1,0:T(8,128)(2,1)S(1)}, u32[]{:S(2)}, u32[]{:S(2)}) collective-permute-start(bf16[272,128]{1,0:T(8,128)(2,1)S(1)} %shard_map.85.refs_2_), channel_id=1, source_target_pairs={{0,1},{1,2},{2,3},{3,4},{4,5},{5,6},{6,7},{7,8},{8,9},{9,10},{10,1... | collective-permute-start | bytes 208904 | tf_op jit(solution)/shard_map/ppermute | solution.py:203
  52.5 8.4 %collective-permute-start.6 = (bf16[272,128]{1,0:T(8,128)(2,1)S(1)}, bf16[272,128]{1,0:T(8,128)(2,1)S(1)}, u32[]{:S(2)}, u32[]{:S(2)}) collective-permute-start(bf16[272,128]{1,0:T(8,128)(2,1)S(1)} %shard_map.85.refs_2_), channel_id=1, source_target_pairs={{1,0},{2,1},{3,2},{4,3},{5,4},{6,5},{7,6},{8,7},{9,8},{10,9},{11,1... | collective-permute-start | bytes 208904 | tf_op jit(solution)/shard_map/ppermute | solution.py:204
  73.4 7.1 %collective-permute-start.7 = (bf16[4,208,128]{2,1,0:T(8,128)(2,1)S(1)}, bf16[4,208,128]{2,1,0:T(8,128)(2,1)S(1)}, u32[]{:S(2)}, u32[]{:S(2)}) collective-permute-start(bf16[4,208,128]{2,1,0:T(8,128)(2,1)S(1)} %all_to_all.11.refs_1_), channel_id=1, source_target_pairs={{0,64},{64,0},{1,65},{65,1},{2,66},{66,2},{3,67},{67,3},{4,68},{68... | collective-permute-start | bytes 638984 | tf_op jit(solution)/shard_map/ppermute | solution.py:213

commit v8 on v7

--- a/solution.py
+++ b/solution.py
@@ -85,13 +85,15 @@
     out[...] = (mine[...] + theirs[...].astype(F32)).astype(BF16)
 
 
-def pick_kernel(nblocks, slots, listed, before, own, after, out, near):
+def pick_kernel(nblocks, slots, listed, across, own, within, out, near):
     groups, length = out.shape[0], own.shape[0]
     step = HALF // groups
     base = (lax.axis_index("sep") - 1) * nblocks
     position = lax.broadcasted_iota(jnp.int32, (16, HALF), 0)
-    for k, source in enumerate((before, own, after)):
-        near[pl.ds(k * length, length), :] = source[...]
+    odd = lax.axis_index("sep") % 2 == 1
+    near[pl.ds(0, length), :] = jnp.where(odd, within[...], across[...])
+    near[pl.ds(length, length), :] = own[...]
+    near[pl.ds(2 * length, length), :] = jnp.where(odd, across[...], within[...])
     diagonals = jnp.zeros((16, HALF), F32)
     for s in range(slots):
         where = listed[0, s] - base
@@ -200,15 +202,16 @@
     parts = lax.all_to_all(chip, "yh", 0, 0, tiled=True)
     held = call(group_kernel, shape((length, HALF), BF16), [VMEM] * 3, moved=600_000)(parts, keep, received)
 
-    before = lax.ppermute(held, "sep", [(i, i + 1) for i in range(nsep - 1)])
-    after = lax.ppermute(held, "sep", [(i + 1, i) for i in range(nsep - 1)])
+    odd = range(1, nsep - 1, 2)
+    across = lax.ppermute(held, "sep", [(i, i + 1) for i in odd] + [(i + 1, i) for i in odd])
+    within = lax.ppermute(held, "sep", [(i, i ^ 1) for i in range(nsep)])
     picked = call(
         lambda *refs: pick_kernel(nblocks, slots, *refs),
         shape((groups, slots * step + 16, HALF), BF16),
         [SMEM] + [VMEM] * 3,
         [pltpu.VMEM((3 * length, HALF), BF16)],
         moved=500_000,
-    )(tile_blocks, before, held, after)
+    )(tile_blocks, across, held, within)
     own = lax.all_to_all(picked, "yh", 0, 0, tiled=True)
     other = lax.ppermute(own, "core", swap)
     return call(

time: 82 us -> 84.1 us (1.026)
  the two profiles are of different devices: /device:TPU:199 before, /device:TPU:9 now
where the time goes in v8:
time: 84.1 us; the launch traced here: 83.6 us
  starting transfers between devices  38 us (45%)
  blocking collectives  27 us (32%)
  waiting for transfers between devices  8.96 us (11%)
  Pallas kernels  6.56 us (8%)
  local copies, waits for them, and re-layouts  2.26 us (3%)
    ppermute x4, starting transfers between devices, shards(): lax.ppermute(own_upper, 'sep', [(i, i ^ 1 << k) for i in range(nsep)])  17.4 us
    all_to_all x1, blocking collectives, shards(): parts = lax.all_to_all(chip, 'yh', 0, 0, tiled=True)  15.3 us
    all_to_all x1, blocking collectives, shards(): own = lax.all_to_all(picked, 'yh', 0, 0, tiled=True)  11.7 us
    ppermute x1, starting transfers between devices, shards(): lax.ppermute(held, 'sep', [(i, i + 1) for i in odd] + [(i + 1, i) for i i...  10.2 us
    ppermute x1, starting transfers between devices, shards(): other = lax.ppermute(own, 'core', swap)  5.58 us
    ppermute x4, waiting for transfers between devices, shards(): lax.ppermute(own_upper, 'sep', [(i, i ^ 1 << k) for i in range(nsep)])  4.26 us
    pallas_call x1, Pallas kernels, shards(): call(lambda *refs: term_kernel(nblocks, order, *refs), (shape((groups, le...  3.6 us
    ppermute x1, waiting for transfers between devices, shards(): within = lax.ppermute(held, 'sep', [(i, i ^ 1) for i in range(nsep)])  3.11 us
  transfers between devices with their start and end apart: 8, of which 4 were waited for; matrix products, arithmetic and copies ran while one was open for 0% of the time, Pallas kernels for 1%

profile of v8, /device:TPU:9, one launch (start us, length us, event | category | flops | bytes accessed | tf_op | source)
XLA Modules:
  0.0 83.6 jit_solution(3518900789134700810)
XLA Ops:
  0.0 0.0 copy-start.3
  0.0 0.0 copy-start.6
  0.0 4.1 %collective-permute-start = (bf16[2,256,256]{2,1,0:T(8,128)(2,1)}, bf16[2,256,256]{2,1,0:T(8,128)(2,1)S(1)}, u32[]{:S(2)}, u32[]{:S(2)}) collective-permute-start(bf16[2,256,256]{2,1,0:T(8,128)(2,1)} %bitcast.7), channel_id=1, source_target_pairs={{0,4},{1,5},{2,6},{3,7},{4,0},{5,1},{6,2},{7,3},{8,12},{9,13},{10,... | collective-permute-start | bytes 786440 | tf_op jit(solution)/shard_map/ppermute | solution.py:180
  4.1 3.1 %collective-permute-start.1 = (bf16[2,256,256]{2,1,0:T(8,128)(2,1)}, bf16[2,256,256]{2,1,0:T(8,128)(2,1)S(1)}, u32[]{:S(2)}, u32[]{:S(2)}) collective-permute-start(bf16[2,256,256]{2,1,0:T(8,128)(2,1)} %bitcast.8), channel_id=1, source_target_pairs={{0,1},{1,0},{2,3},{3,2},{4,5},{5,4},{6,7},{7,6},{8,9},{9,8},{10,11... | collective-permute-start | bytes 786440 | tf_op jit(solution)/shard_map/ppermute | solution.py:180
  7.3 5.8 %collective-permute-start.2 = (bf16[2,256,256]{2,1,0:T(8,128)(2,1)}, bf16[2,256,256]{2,1,0:T(8,128)(2,1)S(1)}, u32[]{:S(2)}, u32[]{:S(2)}) collective-permute-start(bf16[2,256,256]{2,1,0:T(8,128)(2,1)} %bitcast.9), channel_id=1, source_target_pairs={{0,8},{1,9},{2,10},{3,11},{4,12},{5,13},{6,14},{7,15},{8,0},{9,1},... | collective-permute-start | bytes 786440 | tf_op jit(solution)/shard_map/ppermute | solution.py:180
  13.1 4.4 %collective-permute-start.3 = (bf16[2,256,256]{2,1,0:T(8,128)(2,1)}, bf16[2,256,256]{2,1,0:T(8,128)(2,1)S(1)}, u32[]{:S(2)}, u32[]{:S(2)}) collective-permute-start(bf16[2,256,256]{2,1,0:T(8,128)(2,1)} %bitcast.10), channel_id=1, source_target_pairs={{0,2},{1,3},{2,0},{3,1},{4,6},{5,7},{6,4},{7,5},{8,10},{9,11},{10,... | collective-permute-start | bytes 786440 | tf_op jit(solution)/shard_map/ppermute | solution.py:180
  17.4 0.0 copy-start
  17.5 1.6 %copy-done = bf16[1,8,2,256,256]{4,3,2,1,0:T(8,128)(2,1)S(1)} copy-done((bf16[1,8,2,256,256]{4,3,2,1,0:T(8,128)(2,1)S(1)}, bf16[1,8,2,256,256]{4,3,2,1,0:T(8,128)(2,1)}, u32[]{:S(2)}) %copy-start) | copy-done | bytes 2097176
  19.0 0.0 copy-start.2
  19.0 0.7 copy-done.2
  19.7 0.0 copy-start.5
  19.7 1.1 %shard_map.82 = (f32[8,2,128,128]{3,2,1,0:T(8,128)S(1)}, f32[8,128]{1,0:T(8,128)S(1)}) custom-call(f32[1,2]{1,0:T(1,128)S(1)} %copy-done.2, bf16[8,2,256,256]{3,2,1,0:T(8,128)(2,1)S(1)} %bitcast.4), custom_call_target="tpu_custom_call" | custom-call | flops 2000000 | bytes 3200000 | tf_op jit(solution)/shard_map/pallas_call | solution.py:181
  20.8 0.0 collective-permute-done.refs_5_
  20.8 0.0 collective-permute-done.1.refs_6_
  20.8 4.2 %collective-permute-done.2.refs_7_ = bf16[2,256,256]{2,1,0:T(8,128)(2,1)S(1)} collective-permute-done((bf16[2,256,256]{2,1,0:T(8,128)(2,1)}, bf16[2,256,256]{2,1,0:T(8,128)(2,1)S(1)}, u32[]{:S(2)}, u32[]{:S(2)}) %collective-permute-start.2) | collective-permute-done | bytes 262176 | tf_op jit(solution)/shard_map/ppermute | solution.py:180
  25.1 0.0 collective-permute-done.3.refs_8_
  25.1 0.0 copy-done.3
  25.1 0.0 copy-done.6
  25.1 0.0 copy-done.5
  25.1 3.6 %shard_map.83 = (f32[4,272,128]{2,1,0:T(8,128)S(1)}, bf16[4,272,128]{2,1,0:T(8,128)(2,1)S(1)}) custom-call(s32[8]{0:T(128)S(1)} %copy-done.6, f32[1,2]{1,0:T(1,128)S(1)} %copy-done.3, bf16[8,2,256,256]{3,2,1,0:T(8,128)(2,1)S(1)} %bitcast.6, f32[8,2,128,128]{3,2,1,0:T(8,128)S(1)} %get-tuple-element.9.refs_3_, f32[8,128]{1,0:T(8,128)S(1)} %get-tuple-element.10.refs_4_, ...), custom_call_target="tpu_custom_call" | custom-call | flops 2100000000 | bytes 5000000 | tf_op jit(solution)/shard_map/pallas_call | solution.py:191
  28.7 0.0 copy-start.4
  28.7 0.0 copy-start.1
  28.7 3.0 %collective-permute-start.4 = (bf16[4,272,128]{2,1,0:T(8,128)(2,1)S(1)}, bf16[4,272,128]{2,1,0:T(8,128)(2,1)S(1)}, u32[]{:S(2)}, u32[]{:S(2)}) collective-permute-start(bf16[4,272,128]{2,1,0:T(8,128)(2,1)S(1)} %get-tuple-element.12), channel_id=1, source_target_pairs={{0,64},{64,0},{1,65},{65,1},{2,66},{66,2},{3,67},{67,3},{4,68},{68... | collective-permute-start | bytes 835592 | tf_op jit(solution)/shard_map/ppermute | solution.py:200
  31.7 1.2 %collective-permute-done.4.theirs.received = bf16[4,272,128]{2,1,0:T(8,128)(2,1)S(1)} collective-permute-done((bf16[4,272,128]{2,1,0:T(8,128)(2,1)S(1)}, bf16[4,272,128]{2,1,0:T(8,128)(2,1)S(1)}, u32[]{:S(2)}, u32[]{:S(2)}) %collective-permute-start.4) | collective-permute-done | bytes 278560 | tf_op jit(solution)/shard_map/ppermute | solution.py:200
  32.9 0.1 shard_map.84
  32.9 15.3 %all_to_all.10.parts = bf16[4,272,128]{2,1,0:T(8,128)(2,1)S(1)} all-to-all(bf16[4,272,128]{2,1,0:T(8,128)(2,1)S(1)} %shard_map.84), channel_id=1, replica_groups=mesh['yh'=4,'core'=2,'sep'=64] {'yh'}, dimensions={0} | all-to-all | bytes 557056 | tf_op jit(solution)/shard_map/all_to_all | solution.py:202
  48.2 0.1 shard_map.85.refs_2_
  48.3 10.2 %collective-permute-start.5 = (bf16[272,128]{1,0:T(8,128)(2,1)S(1)}, bf16[272,128]{1,0:T(8,128)(2,1)S(1)}, u32[]{:S(2)}, u32[]{:S(2)}) collective-permute-start(bf16[272,128]{1,0:T(8,128)(2,1)S(1)} %shard_map.85.refs_2_), channel_id=1, source_target_pairs={{1,2},{3,4},{5,6},{7,8},{9,10},{11,12},{13,14},{15,16},{17,18},{19... | collective-permute-start | bytes 208904 | tf_op jit(solution)/shard_map/ppermute | solution.py:206
  58.5 1.9 %collective-permute-start.6 = (bf16[272,128]{1,0:T(8,128)(2,1)S(1)}, bf16[272,128]{1,0:T(8,128)(2,1)S(1)}, u32[]{:S(2)}, u32[]{:S(2)}) collective-permute-start(bf16[272,128]{1,0:T(8,128)(2,1)S(1)} %shard_map.85.refs_2_), channel_id=1, source_target_pairs={{0,1},{1,0},{2,3},{3,2},{4,5},{5,4},{6,7},{7,6},{8,9},{9,8},{10,11... | collective-permute-start | bytes 208904 | tf_op jit(solution)/shard_map/ppermute | solution.py:207
  60.4 0.0 collective-permute-done.5.refs_1_
  60.4 3.1 %collective-permute-done.6.refs_3_ = bf16[272,128]{1,0:T(8,128)(2,1)S(1)} collective-permute-done((bf16[272,128]{1,0:T(8,128)(2,1)S(1)}, bf16[272,128]{1,0:T(8,128)(2,1)S(1)}, u32[]{:S(2)}, u32[]{:S(2)}) %collective-permute-start.6) | collective-permute-done | bytes 69664 | tf_op jit(solution)/shard_map/ppermute | solution.py:207
  63.6 0.0 copy-done.4
  63.6 0.6 shard_map.86
  64.2 11.7 %all_to_all.11.refs_1_ = bf16[4,208,128]{2,1,0:T(8,128)(2,1)S(1)} all-to-all(bf16[4,208,128]{2,1,0:T(8,128)(2,1)S(1)} %shard_map.86), channel_id=1, replica_groups=mesh['yh'=4,'core'=2,'sep'=64] {'yh'}, dimensions={0} | all-to-all | bytes 425984 | tf_op jit(solution)/shard_map/all_to_all | solution.py:215
  75.9 5.6 %collective-permute-start.7 = (bf16[4,208,128]{2,1,0:T(8,128)(2,1)S(1)}, bf16[4,208,128]{2,1,0:T(8,128)(2,1)S(1)}, u32[]{:S(2)}, u32[]{:S(2)}) collective-permute-start(bf16[4,208,128]{2,1,0:T(8,128)(2,1)S(1)} %all_to_all.11.refs_1_), channel_id=1, source_target_pairs={{0,64},{64,0},{1,65},{65,1},{2,66},{66,2},{3,67},{67,3},{4,68},{68... | collective-permute-start | bytes 638984 | tf_op jit(solution)/shard_map/ppermute | solution.py:216
  82.2 0.4 collective-permute-done.7.refs_2_
  82.6 0.0 copy-done.1
  82.6 1.0 %shard_map.87 = f32[1,256]{1,0:T(1,128)} custom-call(s32[1]{0:T(128)S(6)} %copy.9.refs_0_, bf16[4,208,128]{2,1,0:T(8,128)(2,1)S(1)} %all_to_all.11.refs_1_, bf16[4,208,128]{2,1,0:T(8,128)(2,1)S(1)} %collective-permute-done.7.refs_2_, bf16[6,256,256]{2,1,0:T(8,128)(2,1)S(1)} %bitcast.5), custom_call_target="tpu_custom_call" | custom-call | flops 200000000 | bytes 1300000 | tf_op jit(solution)/shard_map/pallas_call | solution.py:217
Async XLA Ops:
  0.0 25.1 %copy-start.3 = (f32[1,2]{1,0:T(1,128)S(1)}, f32[1,2]{1,0:T(1,128)}, u32[]{:S(2)}) copy-start(f32[1,2]{1,0:T(1,128)} %refs_1_.1) | copy-start | bytes 28
  0.0 25.1 %copy-start.6 = (s32[8]{0:T(128)S(1)}, s32[8]{0:T(128)}, u32[]{:S(2)}) copy-start(s32[8]{0:T(128)} %refs_0_.5) | copy-start | bytes 100
  0.0 20.8 %collective-permute-start = (bf16[2,256,256]{2,1,0:T(8,128)(2,1)}, bf16[2,256,256]{2,1,0:T(8,128)(2,1)S(1)}, u32[]{:S(2)}, u32[]{:S(2)}) collective-permute-start(bf16[2,256,256]{2,1,0:T(8,128)(2,1)} %bitcast.7), channel_id=1, source_target_pairs={{0,4},{1,5},{2,6},{3,7},{4,0},{5,1},{6,2},{7,3},{8,12},{9,13},{10,... | collective-permute-start | bytes 786440 | tf_op jit(solution)/shard_map/ppermute | solution.py:180
  4.1 16.7 %collective-permute-start.1 = (bf16[2,256,256]{2,1,0:T(8,128)(2,1)}, bf16[2,256,256]{2,1,0:T(8,128)(2,1)S(1)}, u32[]{:S(2)}, u32[]{:S(2)}) collective-permute-start(bf16[2,256,256]{2,1,0:T(8,128)(2,1)} %bitcast.8), channel_id=1, source_target_pairs={{0,1},{1,0},{2,3},{3,2},{4,5},{5,4},{6,7},{7,6},{8,9},{9,8},{10,11... | collective-permute-start | bytes 786440 | tf_op jit(solution)/shard_map/ppermute | solution.py:180
  7.3 17.8 %collective-permute-start.2 = (bf16[2,256,256]{2,1,0:T(8,128)(2,1)}, bf16[2,256,256]{2,1,0:T(8,128)(2,1)S(1)}, u32[]{:S(2)}, u32[]{:S(2)}) collective-permute-start(bf16[2,256,256]{2,1,0:T(8,128)(2,1)} %bitcast.9), channel_id=1, source_target_pairs={{0,8},{1,9},{2,10},{3,11},{4,12},{5,13},{6,14},{7,15},{8,0},{9,1},... | collective-permute-start | bytes 786440 | tf_op jit(solution)/shard_map/ppermute | solution.py:180
  13.1 12.0 %collective-permute-start.3 = (bf16[2,256,256]{2,1,0:T(8,128)(2,1)}, bf16[2,256,256]{2,1,0:T(8,128)(2,1)S(1)}, u32[]{:S(2)}, u32[]{:S(2)}) collective-permute-start(bf16[2,256,256]{2,1,0:T(8,128)(2,1)} %bitcast.10), channel_id=1, source_target_pairs={{0,2},{1,3},{2,0},{3,1},{4,6},{5,7},{6,4},{7,5},{8,10},{9,11},{10,... | collective-permute-start | bytes 786440 | tf_op jit(solution)/shard_map/ppermute | solution.py:180
  17.4 1.6 %copy-start = (bf16[1,8,2,256,256]{4,3,2,1,0:T(8,128)(2,1)S(1)}, bf16[1,8,2,256,256]{4,3,2,1,0:T(8,128)(2,1)}, u32[]{:S(2)}) copy-start(bf16[1,8,2,256,256]{4,3,2,1,0:T(8,128)(2,1)} %param.8) | copy-start | bytes 6291460
  19.0 0.7 copy-start.2
  19.7 5.4 %copy-start.5 = (bf16[1,8,2,256,256]{4,3,2,1,0:T(8,128)(2,1)S(1)}, bf16[1,8,2,256,256]{4,3,2,1,0:T(8,128)(2,1)}, u32[]{:S(2)}) copy-start(bf16[1,8,2,256,256]{4,3,2,1,0:T(8,128)(2,1)} %param.9) | copy-start | bytes 6291460
  28.7 34.8 %copy-start.4 = (s32[1,6]{1,0:T(1,128)S(1)}, s32[1,6]{1,0:T(1,128)}, u32[]{:S(2)}) copy-start(s32[1,6]{1,0:T(1,128)} %refs_0_.6) | copy-start | bytes 76
  28.7 53.9 %copy-start.1 = (bf16[1,6,256,256]{3,2,1,0:T(8,128)(2,1)S(1)}, bf16[1,6,256,256]{3,2,1,0:T(8,128)(2,1)}, u32[]{:S(2)}) copy-start(bf16[1,6,256,256]{3,2,1,0:T(8,128)(2,1)} %param.15) | copy-start | bytes 2359300
  28.7 4.1 %collective-permute-start.4 = (bf16[4,272,128]{2,1,0:T(8,128)(2,1)S(1)}, bf16[4,272,128]{2,1,0:T(8,128)(2,1)S(1)}, u32[]{:S(2)}, u32[]{:S(2)}) collective-permute-start(bf16[4,272,128]{2,1,0:T(8,128)(2,1)S(1)} %get-tuple-element.12), channel_id=1, source_target_pairs={{0,64},{64,0},{1,65},{65,1},{2,66},{66,2},{3,67},{67,3},{4,68},{68... | collective-permute-start | bytes 835592 | tf_op jit(solution)/shard_map/ppermute | solution.py:200
  48.3 12.1 %collective-permute-start.5 = (bf16[272,128]{1,0:T(8,128)(2,1)S(1)}, bf16[272,128]{1,0:T(8,128)(2,1)S(1)}, u32[]{:S(2)}, u32[]{:S(2)}) collective-permute-start(bf16[272,128]{1,0:T(8,128)(2,1)S(1)} %shard_map.85.refs_2_), channel_id=1, source_target_pairs={{1,2},{3,4},{5,6},{7,8},{9,10},{11,12},{13,14},{15,16},{17,18},{19... | collective-permute-start | bytes 208904 | tf_op jit(solution)/shard_map/ppermute | solution.py:206
  58.5 5.1 %collective-permute-start.6 = (bf16[272,128]{1,0:T(8,128)(2,1)S(1)}, bf16[272,128]{1,0:T(8,128)(2,1)S(1)}, u32[]{:S(2)}, u32[]{:S(2)}) collective-permute-start(bf16[272,128]{1,0:T(8,128)(2,1)S(1)} %shard_map.85.refs_2_), channel_id=1, source_target_pairs={{0,1},{1,0},{2,3},{3,2},{4,5},{5,4},{6,7},{7,6},{8,9},{9,8},{10,11... | collective-permute-start | bytes 208904 | tf_op jit(solution)/shard_map/ppermute | solution.py:207
  75.9 6.7 %collective-permute-start.7 = (bf16[4,208,128]{2,1,0:T(8,128)(2,1)S(1)}, bf16[4,208,128]{2,1,0:T(8,128)(2,1)S(1)}, u32[]{:S(2)}, u32[]{:S(2)}) collective-permute-start(bf16[4,208,128]{2,1,0:T(8,128)(2,1)S(1)} %all_to_all.11.refs_1_), channel_id=1, source_target_pairs={{0,64},{64,0},{1,65},{65,1},{2,66},{66,2},{3,67},{67,3},{4,68},{68... | collective-permute-start | bytes 638984 | tf_op jit(solution)/shard_map/ppermute | solution.py:216

commit v9 on v8

--- a/solution.py
+++ b/solution.py
@@ -85,7 +85,7 @@
     out[...] = (mine[...] + theirs[...].astype(F32)).astype(BF16)
 
 
-def pick_kernel(nblocks, slots, listed, across, own, within, out, near):
+def pick_kernel(nblocks, slots, listed, within, own, across, out, near):
     groups, length = out.shape[0], own.shape[0]
     step = HALF // groups
     base = (lax.axis_index("sep") - 1) * nblocks
@@ -203,15 +203,15 @@
     held = call(group_kernel, shape((length, HALF), BF16), [VMEM] * 3, moved=600_000)(parts, keep, received)
 
     odd = range(1, nsep - 1, 2)
+    within = lax.ppermute(held, "sep", [(i, i ^ 1) for i in range(nsep)])
     across = lax.ppermute(held, "sep", [(i, i + 1) for i in odd] + [(i + 1, i) for i in odd])
-    within = lax.ppermute(held, "sep", [(i, i ^ 1) for i in range(nsep)])
     picked = call(
         lambda *refs: pick_kernel(nblocks, slots, *refs),
         shape((groups, slots * step + 16, HALF), BF16),
         [SMEM] + [VMEM] * 3,
         [pltpu.VMEM((3 * length, HALF), BF16)],
         moved=500_000,
-    )(tile_blocks, across, held, within)
+    )(tile_blocks, within, held, across)
     own = lax.all_to_all(picked, "yh", 0, 0, tiled=True)
     other = lax.ppermute(own, "core", swap)
     return call(

time: 84.1 us -> 83.2 us (0.989)
  waiting for transfers between devices: 8.96 us -> 7.52 us
    ppermute x1, waiting for transfers between devices: 3.11 us -> 0.01 us  [shards(): within = lax.ppermute(held, 'sep', [(i, i ^ 1) for i in range(nsep)])]
    ppermute x1, waiting for transfers between devices: 0.01 us -> 1.67 us  [shards(): lax.ppermute(held, 'sep', [(i, i + 1) for i in odd] + [(i + 1, i) for i i...]
where the time goes in v9:
time: 83.2 us; the launch traced here: 82.8 us
  starting transfers between devices  38.7 us (47%)
  blocking collectives  27 us (32%)
  waiting for transfers between devices  7.52 us (9%)
  Pallas kernels  6.56 us (8%)
  local copies, waits for them, and re-layouts  2.26 us (3%)
    ppermute x4, starting transfers between devices, shards(): lax.ppermute(own_upper, 'sep', [(i, i ^ 1 << k) for i in range(nsep)])  17.4 us
    all_to_all x1, blocking collectives, shards(): parts = lax.all_to_all(chip, 'yh', 0, 0, tiled=True)  15.3 us
    all_to_all x1, blocking collectives, shards(): own = lax.all_to_all(picked, 'yh', 0, 0, tiled=True)  11.7 us
    ppermute x1, starting transfers between devices, shards(): lax.ppermute(held, 'sep', [(i, i + 1) for i in odd] + [(i + 1, i) for i i...  10.7 us
    ppermute x1, starting transfers between devices, shards(): other = lax.ppermute(own, 'core', swap)  5.3 us
    ppermute x4, waiting for transfers between devices, shards(): lax.ppermute(own_upper, 'sep', [(i, i ^ 1 << k) for i in range(nsep)])  4.26 us
    pallas_call x1, Pallas kernels, shards(): call(lambda *refs: term_kernel(nblocks, order, *refs), (shape((groups, le...  3.6 us
    ppermute x1, starting transfers between devices, shards(): received = lax.ppermute(send, 'core', swap)  2.96 us
  transfers between devices with their start and end apart: 8, of which 4 were waited for; matrix products, arithmetic and copies ran while one was open for 0% of the time, Pallas kernels for 1%

profile of v9, /device:TPU:9, one launch (start us, length us, event | category | flops | bytes accessed | tf_op | source)
XLA Modules:
  0.0 82.8 jit_solution(10913425931862035602)
XLA Ops:
  0.0 0.0 copy-start.3
  0.0 0.0 copy-start.6
  0.0 4.1 %collective-permute-start = (bf16[2,256,256]{2,1,0:T(8,128)(2,1)}, bf16[2,256,256]{2,1,0:T(8,128)(2,1)S(1)}, u32[]{:S(2)}, u32[]{:S(2)}) collective-permute-start(bf16[2,256,256]{2,1,0:T(8,128)(2,1)} %bitcast.7), channel_id=1, source_target_pairs={{0,4},{1,5},{2,6},{3,7},{4,0},{5,1},{6,2},{7,3},{8,12},{9,13},{10,... | collective-permute-start | bytes 786440 | tf_op jit(solution)/shard_map/ppermute | solution.py:180
  4.1 3.1 %collective-permute-start.1 = (bf16[2,256,256]{2,1,0:T(8,128)(2,1)}, bf16[2,256,256]{2,1,0:T(8,128)(2,1)S(1)}, u32[]{:S(2)}, u32[]{:S(2)}) collective-permute-start(bf16[2,256,256]{2,1,0:T(8,128)(2,1)} %bitcast.8), channel_id=1, source_target_pairs={{0,1},{1,0},{2,3},{3,2},{4,5},{5,4},{6,7},{7,6},{8,9},{9,8},{10,11... | collective-permute-start | bytes 786440 | tf_op jit(solution)/shard_map/ppermute | solution.py:180
  7.3 5.8 %collective-permute-start.2 = (bf16[2,256,256]{2,1,0:T(8,128)(2,1)}, bf16[2,256,256]{2,1,0:T(8,128)(2,1)S(1)}, u32[]{:S(2)}, u32[]{:S(2)}) collective-permute-start(bf16[2,256,256]{2,1,0:T(8,128)(2,1)} %bitcast.9), channel_id=1, source_target_pairs={{0,8},{1,9},{2,10},{3,11},{4,12},{5,13},{6,14},{7,15},{8,0},{9,1},... | collective-permute-start | bytes 786440 | tf_op jit(solution)/shard_map/ppermute | solution.py:180
  13.1 4.4 %collective-permute-start.3 = (bf16[2,256,256]{2,1,0:T(8,128)(2,1)}, bf16[2,256,256]{2,1,0:T(8,128)(2,1)S(1)}, u32[]{:S(2)}, u32[]{:S(2)}) collective-permute-start(bf16[2,256,256]{2,1,0:T(8,128)(2,1)} %bitcast.10), channel_id=1, source_target_pairs={{0,2},{1,3},{2,0},{3,1},{4,6},{5,7},{6,4},{7,5},{8,10},{9,11},{10,... | collective-permute-start | bytes 786440 | tf_op jit(solution)/shard_map/ppermute | solution.py:180
  17.4 0.0 copy-start
  17.5 1.6 %copy-done = bf16[1,8,2,256,256]{4,3,2,1,0:T(8,128)(2,1)S(1)} copy-done((bf16[1,8,2,256,256]{4,3,2,1,0:T(8,128)(2,1)S(1)}, bf16[1,8,2,256,256]{4,3,2,1,0:T(8,128)(2,1)}, u32[]{:S(2)}) %copy-start) | copy-done | bytes 2097176
  19.0 0.0 copy-start.2
  19.0 0.7 copy-done.2
  19.7 0.0 copy-start.5
  19.7 1.1 %shard_map.82 = (f32[8,2,128,128]{3,2,1,0:T(8,128)S(1)}, f32[8,128]{1,0:T(8,128)S(1)}) custom-call(f32[1,2]{1,0:T(1,128)S(1)} %copy-done.2, bf16[8,2,256,256]{3,2,1,0:T(8,128)(2,1)S(1)} %bitcast.4), custom_call_target="tpu_custom_call" | custom-call | flops 2000000 | bytes 3200000 | tf_op jit(solution)/shard_map/pallas_call | solution.py:181
  20.8 0.0 collective-permute-done.refs_5_
  20.8 0.0 collective-permute-done.1.refs_6_
  20.8 4.2 %collective-permute-done.2.refs_7_ = bf16[2,256,256]{2,1,0:T(8,128)(2,1)S(1)} collective-permute-done((bf16[2,256,256]{2,1,0:T(8,128)(2,1)}, bf16[2,256,256]{2,1,0:T(8,128)(2,1)S(1)}, u32[]{:S(2)}, u32[]{:S(2)}) %collective-permute-start.2) | collective-permute-done | bytes 262176 | tf_op jit(solution)/shard_map/ppermute | solution.py:180
  25.1 0.0 collective-permute-done.3.refs_8_
  25.1 0.0 copy-done.3
  25.1 0.0 copy-done.6
  25.1 0.0 copy-done.5
  25.1 3.6 %shard_map.83 = (f32[4,272,128]{2,1,0:T(8,128)S(1)}, bf16[4,272,128]{2,1,0:T(8,128)(2,1)S(1)}) custom-call(s32[8]{0:T(128)S(1)} %copy-done.6, f32[1,2]{1,0:T(1,128)S(1)} %copy-done.3, bf16[8,2,256,256]{3,2,1,0:T(8,128)(2,1)S(1)} %bitcast.6, f32[8,2,128,128]{3,2,1,0:T(8,128)S(1)} %get-tuple-element.9.refs_3_, f32[8,128]{1,0:T(8,128)S(1)} %get-tuple-element.10.refs_4_, ...), custom_call_target="tpu_custom_call" | custom-call | flops 2100000000 | bytes 5000000 | tf_op jit(solution)/shard_map/pallas_call | solution.py:191
  28.7 0.0 copy-start.4
  28.7 0.0 copy-start.1
  28.7 3.0 %collective-permute-start.4 = (bf16[4,272,128]{2,1,0:T(8,128)(2,1)S(1)}, bf16[4,272,128]{2,1,0:T(8,128)(2,1)S(1)}, u32[]{:S(2)}, u32[]{:S(2)}) collective-permute-start(bf16[4,272,128]{2,1,0:T(8,128)(2,1)S(1)} %get-tuple-element.12), channel_id=1, source_target_pairs={{0,64},{64,0},{1,65},{65,1},{2,66},{66,2},{3,67},{67,3},{4,68},{68... | collective-permute-start | bytes 835592 | tf_op jit(solution)/shard_map/ppermute | solution.py:200
  31.7 1.2 %collective-permute-done.4.theirs.received = bf16[4,272,128]{2,1,0:T(8,128)(2,1)S(1)} collective-permute-done((bf16[4,272,128]{2,1,0:T(8,128)(2,1)S(1)}, bf16[4,272,128]{2,1,0:T(8,128)(2,1)S(1)}, u32[]{:S(2)}, u32[]{:S(2)}) %collective-permute-start.4) | collective-permute-done | bytes 278560 | tf_op jit(solution)/shard_map/ppermute | solution.py:200
  32.9 0.1 shard_map.84
  32.9 15.3 %all_to_all.10.parts = bf16[4,272,128]{2,1,0:T(8,128)(2,1)S(1)} all-to-all(bf16[4,272,128]{2,1,0:T(8,128)(2,1)S(1)} %shard_map.84), channel_id=1, replica_groups=mesh['yh'=4,'core'=2,'sep'=64] {'yh'}, dimensions={0} | all-to-all | bytes 557056 | tf_op jit(solution)/shard_map/all_to_all | solution.py:202
  48.2 0.1 shard_map.85.refs_2_
  48.3 2.3 %collective-permute-start.5 = (bf16[272,128]{1,0:T(8,128)(2,1)S(1)}, bf16[272,128]{1,0:T(8,128)(2,1)S(1)}, u32[]{:S(2)}, u32[]{:S(2)}) collective-permute-start(bf16[272,128]{1,0:T(8,128)(2,1)S(1)} %shard_map.85.refs_2_), channel_id=1, source_target_pairs={{0,1},{1,0},{2,3},{3,2},{4,5},{5,4},{6,7},{7,6},{8,9},{9,8},{10,11... | collective-permute-start | bytes 208904 | tf_op jit(solution)/shard_map/ppermute | solution.py:206
  50.6 10.7 %collective-permute-start.6 = (bf16[272,128]{1,0:T(8,128)(2,1)S(1)}, bf16[272,128]{1,0:T(8,128)(2,1)S(1)}, u32[]{:S(2)}, u32[]{:S(2)}) collective-permute-start(bf16[272,128]{1,0:T(8,128)(2,1)S(1)} %shard_map.85.refs_2_), channel_id=1, source_target_pairs={{1,2},{3,4},{5,6},{7,8},{9,10},{11,12},{13,14},{15,16},{17,18},{19... | collective-permute-start | bytes 208904 | tf_op jit(solution)/shard_map/ppermute | solution.py:207
  61.3 0.0 collective-permute-done.5.refs_1_
  61.4 1.7 %collective-permute-done.6.refs_3_ = bf16[272,128]{1,0:T(8,128)(2,1)S(1)} collective-permute-done((bf16[272,128]{1,0:T(8,128)(2,1)S(1)}, bf16[272,128]{1,0:T(8,128)(2,1)S(1)}, u32[]{:S(2)}, u32[]{:S(2)}) %collective-permute-start.6) | collective-permute-done | bytes 69664 | tf_op jit(solution)/shard_map/ppermute | solution.py:207
  63.0 0.0 copy-done.4
  63.0 0.6 shard_map.86
  63.7 11.7 %all_to_all.11.refs_1_ = bf16[4,208,128]{2,1,0:T(8,128)(2,1)S(1)} all-to-all(bf16[4,208,128]{2,1,0:T(8,128)(2,1)S(1)} %shard_map.86), channel_id=1, replica_groups=mesh['yh'=4,'core'=2,'sep'=64] {'yh'}, dimensions={0} | all-to-all | bytes 425984 | tf_op jit(solution)/shard_map/all_to_all | solution.py:215
  75.4 5.3 %collective-permute-start.7 = (bf16[4,208,128]{2,1,0:T(8,128)(2,1)S(1)}, bf16[4,208,128]{2,1,0:T(8,128)(2,1)S(1)}, u32[]{:S(2)}, u32[]{:S(2)}) collective-permute-start(bf16[4,208,128]{2,1,0:T(8,128)(2,1)S(1)} %all_to_all.11.refs_1_), channel_id=1, source_target_pairs={{0,64},{64,0},{1,65},{65,1},{2,66},{66,2},{3,67},{67,3},{4,68},{68... | collective-permute-start | bytes 638984 | tf_op jit(solution)/shard_map/ppermute | solution.py:216
  81.4 0.4 collective-permute-done.7.refs_2_
  81.8 0.0 copy-done.1
  81.8 1.0 %shard_map.87 = f32[1,256]{1,0:T(1,128)} custom-call(s32[1]{0:T(128)S(6)} %copy.9.refs_0_, bf16[4,208,128]{2,1,0:T(8,128)(2,1)S(1)} %all_to_all.11.refs_1_, bf16[4,208,128]{2,1,0:T(8,128)(2,1)S(1)} %collective-permute-done.7.refs_2_, bf16[6,256,256]{2,1,0:T(8,128)(2,1)S(1)} %bitcast.5), custom_call_target="tpu_custom_call" | custom-call | flops 200000000 | bytes 1300000 | tf_op jit(solution)/shard_map/pallas_call | solution.py:217
Async XLA Ops:
  0.0 25.1 %copy-start.3 = (f32[1,2]{1,0:T(1,128)S(1)}, f32[1,2]{1,0:T(1,128)}, u32[]{:S(2)}) copy-start(f32[1,2]{1,0:T(1,128)} %refs_1_.1) | copy-start | bytes 28
  0.0 25.1 %copy-start.6 = (s32[8]{0:T(128)S(1)}, s32[8]{0:T(128)}, u32[]{:S(2)}) copy-start(s32[8]{0:T(128)} %refs_0_.5) | copy-start | bytes 100
  0.0 20.8 %collective-permute-start = (bf16[2,256,256]{2,1,0:T(8,128)(2,1)}, bf16[2,256,256]{2,1,0:T(8,128)(2,1)S(1)}, u32[]{:S(2)}, u32[]{:S(2)}) collective-permute-start(bf16[2,256,256]{2,1,0:T(8,128)(2,1)} %bitcast.7), channel_id=1, source_target_pairs={{0,4},{1,5},{2,6},{3,7},{4,0},{5,1},{6,2},{7,3},{8,12},{9,13},{10,... | collective-permute-start | bytes 786440 | tf_op jit(solution)/shard_map/ppermute | solution.py:180
  4.1 16.7 %collective-permute-start.1 = (bf16[2,256,256]{2,1,0:T(8,128)(2,1)}, bf16[2,256,256]{2,1,0:T(8,128)(2,1)S(1)}, u32[]{:S(2)}, u32[]{:S(2)}) collective-permute-start(bf16[2,256,256]{2,1,0:T(8,128)(2,1)} %bitcast.8), channel_id=1, source_target_pairs={{0,1},{1,0},{2,3},{3,2},{4,5},{5,4},{6,7},{7,6},{8,9},{9,8},{10,11... | collective-permute-start | bytes 786440 | tf_op jit(solution)/shard_map/ppermute | solution.py:180
  7.3 17.8 %collective-permute-start.2 = (bf16[2,256,256]{2,1,0:T(8,128)(2,1)}, bf16[2,256,256]{2,1,0:T(8,128)(2,1)S(1)}, u32[]{:S(2)}, u32[]{:S(2)}) collective-permute-start(bf16[2,256,256]{2,1,0:T(8,128)(2,1)} %bitcast.9), channel_id=1, source_target_pairs={{0,8},{1,9},{2,10},{3,11},{4,12},{5,13},{6,14},{7,15},{8,0},{9,1},... | collective-permute-start | bytes 786440 | tf_op jit(solution)/shard_map/ppermute | solution.py:180
  13.1 12.0 %collective-permute-start.3 = (bf16[2,256,256]{2,1,0:T(8,128)(2,1)}, bf16[2,256,256]{2,1,0:T(8,128)(2,1)S(1)}, u32[]{:S(2)}, u32[]{:S(2)}) collective-permute-start(bf16[2,256,256]{2,1,0:T(8,128)(2,1)} %bitcast.10), channel_id=1, source_target_pairs={{0,2},{1,3},{2,0},{3,1},{4,6},{5,7},{6,4},{7,5},{8,10},{9,11},{10,... | collective-permute-start | bytes 786440 | tf_op jit(solution)/shard_map/ppermute | solution.py:180
  17.4 1.6 %copy-start = (bf16[1,8,2,256,256]{4,3,2,1,0:T(8,128)(2,1)S(1)}, bf16[1,8,2,256,256]{4,3,2,1,0:T(8,128)(2,1)}, u32[]{:S(2)}) copy-start(bf16[1,8,2,256,256]{4,3,2,1,0:T(8,128)(2,1)} %param.8) | copy-start | bytes 6291460
  19.0 0.7 copy-start.2
  19.7 5.4 %copy-start.5 = (bf16[1,8,2,256,256]{4,3,2,1,0:T(8,128)(2,1)S(1)}, bf16[1,8,2,256,256]{4,3,2,1,0:T(8,128)(2,1)}, u32[]{:S(2)}) copy-start(bf16[1,8,2,256,256]{4,3,2,1,0:T(8,128)(2,1)} %param.9) | copy-start | bytes 6291460
  28.7 34.3 %copy-start.4 = (s32[1,6]{1,0:T(1,128)S(1)}, s32[1,6]{1,0:T(1,128)}, u32[]{:S(2)}) copy-start(s32[1,6]{1,0:T(1,128)} %refs_0_.6) | copy-start | bytes 76
  28.7 53.0 %copy-start.1 = (bf16[1,6,256,256]{3,2,1,0:T(8,128)(2,1)S(1)}, bf16[1,6,256,256]{3,2,1,0:T(8,128)(2,1)}, u32[]{:S(2)}) copy-start(bf16[1,6,256,256]{3,2,1,0:T(8,128)(2,1)} %param.15) | copy-start | bytes 2359300
  28.7 4.1 %collective-permute-start.4 = (bf16[4,272,128]{2,1,0:T(8,128)(2,1)S(1)}, bf16[4,272,128]{2,1,0:T(8,128)(2,1)S(1)}, u32[]{:S(2)}, u32[]{:S(2)}) collective-permute-start(bf16[4,272,128]{2,1,0:T(8,128)(2,1)S(1)} %get-tuple-element.12), channel_id=1, source_target_pairs={{0,64},{64,0},{1,65},{65,1},{2,66},{66,2},{3,67},{67,3},{4,68},{68... | collective-permute-start | bytes 835592 | tf_op jit(solution)/shard_map/ppermute | solution.py:200
  48.3 13.0 %collective-permute-start.5 = (bf16[272,128]{1,0:T(8,128)(2,1)S(1)}, bf16[272,128]{1,0:T(8,128)(2,1)S(1)}, u32[]{:S(2)}, u32[]{:S(2)}) collective-permute-start(bf16[272,128]{1,0:T(8,128)(2,1)S(1)} %shard_map.85.refs_2_), channel_id=1, source_target_pairs={{0,1},{1,0},{2,3},{3,2},{4,5},{5,4},{6,7},{7,6},{8,9},{9,8},{10,11... | collective-permute-start | bytes 208904 | tf_op jit(solution)/shard_map/ppermute | solution.py:206
  50.6 12.4 %collective-permute-start.6 = (bf16[272,128]{1,0:T(8,128)(2,1)S(1)}, bf16[272,128]{1,0:T(8,128)(2,1)S(1)}, u32[]{:S(2)}, u32[]{:S(2)}) collective-permute-start(bf16[272,128]{1,0:T(8,128)(2,1)S(1)} %shard_map.85.refs_2_), channel_id=1, source_target_pairs={{1,2},{3,4},{5,6},{7,8},{9,10},{11,12},{13,14},{15,16},{17,18},{19... | collective-permute-start | bytes 208904 | tf_op jit(solution)/shard_map/ppermute | solution.py:207
  75.4 6.4 %collective-permute-start.7 = (bf16[4,208,128]{2,1,0:T(8,128)(2,1)S(1)}, bf16[4,208,128]{2,1,0:T(8,128)(2,1)S(1)}, u32[]{:S(2)}, u32[]{:S(2)}) collective-permute-start(bf16[4,208,128]{2,1,0:T(8,128)(2,1)S(1)} %all_to_all.11.refs_1_), channel_id=1, source_target_pairs={{0,64},{64,0},{1,65},{65,1},{2,66},{66,2},{3,67},{67,3},{4,68},{68... | collective-permute-start | bytes 638984 | tf_op jit(solution)/shard_map/ppermute | solution.py:216

commit v10 on v7

--- a/solution.py
+++ b/solution.py
@@ -174,7 +174,7 @@
     nsep, groups = lax.axis_size("sep"), lax.axis_size("yh")
     swap = [(0, 1), (1, 0)]
 
-    order = (2, 0, 3, 1)
+    order = (3, 0, 2, 1)
     uppers = [lax.ppermute(own_upper, "sep", [(i, i ^ 1 << k) for i in range(nsep)]) for k in order]
     tiles, rows = call(
         lambda *refs: weigh_kernel(nblocks, *refs),

time: 82 us -> 81.1 us (0.989)
  waiting for transfers between devices: 15.7 us -> 14.5 us
    ppermute x4, waiting for transfers between devices: 7.7 us -> 6.49 us  [shards(): lax.ppermute(own_upper, 'sep', [(i, i ^ 1 << k) for i in range(nsep)])]
  transfers between devices with their start and end apart: 8 -> 8, of which waited for: 4 -> 5; matrix products, arithmetic and copies ran while one was open for 0% -> 0% of each run, Pallas kernels for 1% -> 1%
where the time goes in v10:
time: 81.1 us; the launch traced here: 80.6 us
  blocking collectives  28.6 us (35%)
  starting transfers between devices  27.9 us (34%)
  waiting for transfers between devices  14.5 us (18%)
  Pallas kernels  6.54 us (8%)
  local copies, waits for them, and re-layouts  2.26 us (3%)
    all_to_all x1, blocking collectives, shards(): parts = lax.all_to_all(chip, 'yh', 0, 0, tiled=True)  16.6 us
    all_to_all x1, blocking collectives, shards(): own = lax.all_to_all(picked, 'yh', 0, 0, tiled=True)  11.9 us
    ppermute x4, starting transfers between devices, shards(): lax.ppermute(own_upper, 'sep', [(i, i ^ 1 << k) for i in range(nsep)])  9.16 us
    ppermute x1, starting transfers between devices, shards(): before = lax.ppermute(held, 'sep', [(i, i + 1) for i in range(nsep - 1)])  7.04 us
    ppermute x4, waiting for transfers between devices, shards(): lax.ppermute(own_upper, 'sep', [(i, i ^ 1 << k) for i in range(nsep)])  6.49 us
    ppermute x1, waiting for transfers between devices, shards(): after = lax.ppermute(held, 'sep', [(i + 1, i) for i in range(nsep - 1)])  6.43 us
    ppermute x1, starting transfers between devices, shards(): other = lax.ppermute(own, 'core', swap)  5.98 us
    ppermute x1, starting transfers between devices, shards(): received = lax.ppermute(send, 'core', swap)  3.84 us
  transfers between devices with their start and end apart: 8, of which 5 were waited for; matrix products, arithmetic and copies ran while one was open for 0% of the time, Pallas kernels for 1%

profile of v10, /device:TPU:199, one launch (start us, length us, event | category | flops | bytes accessed | tf_op | source)
XLA Modules:
  0.0 80.6 jit_solution(16484323982960351407)
XLA Ops:
  0.0 0.0 copy-start.3
  0.0 0.0 copy-start.6
  0.0 2.0 %collective-permute-start = (bf16[2,256,256]{2,1,0:T(8,128)(2,1)}, bf16[2,256,256]{2,1,0:T(8,128)(2,1)S(1)}, u32[]{:S(2)}, u32[]{:S(2)}) collective-permute-start(bf16[2,256,256]{2,1,0:T(8,128)(2,1)} %bitcast.7), channel_id=1, source_target_pairs={{0,8},{1,9},{2,10},{3,11},{4,12},{5,13},{6,14},{7,15},{8,0},{9,1},... | collective-permute-start | bytes 786440 | tf_op jit(solution)/shard_map/ppermute | solution.py:178
  2.1 2.5 %collective-permute-start.1 = (bf16[2,256,256]{2,1,0:T(8,128)(2,1)}, bf16[2,256,256]{2,1,0:T(8,128)(2,1)S(1)}, u32[]{:S(2)}, u32[]{:S(2)}) collective-permute-start(bf16[2,256,256]{2,1,0:T(8,128)(2,1)} %bitcast.8), channel_id=1, source_target_pairs={{0,1},{1,0},{2,3},{3,2},{4,5},{5,4},{6,7},{7,6},{8,9},{9,8},{10,11... | collective-permute-start | bytes 786440 | tf_op jit(solution)/shard_map/ppermute | solution.py:178
  4.5 1.9 %collective-permute-start.2 = (bf16[2,256,256]{2,1,0:T(8,128)(2,1)}, bf16[2,256,256]{2,1,0:T(8,128)(2,1)S(1)}, u32[]{:S(2)}, u32[]{:S(2)}) collective-permute-start(bf16[2,256,256]{2,1,0:T(8,128)(2,1)} %bitcast.9), channel_id=1, source_target_pairs={{0,4},{1,5},{2,6},{3,7},{4,0},{5,1},{6,2},{7,3},{8,12},{9,13},{10,... | collective-permute-start | bytes 786440 | tf_op jit(solution)/shard_map/ppermute | solution.py:178
  6.4 2.7 %collective-permute-start.3 = (bf16[2,256,256]{2,1,0:T(8,128)(2,1)}, bf16[2,256,256]{2,1,0:T(8,128)(2,1)S(1)}, u32[]{:S(2)}, u32[]{:S(2)}) collective-permute-start(bf16[2,256,256]{2,1,0:T(8,128)(2,1)} %bitcast.10), channel_id=1, source_target_pairs={{0,2},{1,3},{2,0},{3,1},{4,6},{5,7},{6,4},{7,5},{8,10},{9,11},{10,... | collective-permute-start | bytes 786440 | tf_op jit(solution)/shard_map/ppermute | solution.py:178
  9.2 0.0 copy-start
  9.2 1.6 %copy-done = bf16[1,8,2,256,256]{4,3,2,1,0:T(8,128)(2,1)S(1)} copy-done((bf16[1,8,2,256,256]{4,3,2,1,0:T(8,128)(2,1)S(1)}, bf16[1,8,2,256,256]{4,3,2,1,0:T(8,128)(2,1)}, u32[]{:S(2)}) %copy-start) | copy-done | bytes 2097176
  10.8 0.0 copy-start.2
  10.8 0.7 copy-done.2
  11.4 0.0 copy-start.5
  11.4 1.1 %shard_map.82 = (f32[8,2,128,128]{3,2,1,0:T(8,128)S(1)}, f32[8,128]{1,0:T(8,128)S(1)}) custom-call(f32[1,2]{1,0:T(1,128)S(1)} %copy-done.2, bf16[8,2,256,256]{3,2,1,0:T(8,128)(2,1)S(1)} %bitcast.4), custom_call_target="tpu_custom_call" | custom-call | flops 2000000 | bytes 3200000 | tf_op jit(solution)/shard_map/pallas_call | solution.py:179
  12.6 3.5 %collective-permute-done.refs_5_ = bf16[2,256,256]{2,1,0:T(8,128)(2,1)S(1)} collective-permute-done((bf16[2,256,256]{2,1,0:T(8,128)(2,1)}, bf16[2,256,256]{2,1,0:T(8,128)(2,1)S(1)}, u32[]{:S(2)}, u32[]{:S(2)}) %collective-permute-start) | collective-permute-done | bytes 262176 | tf_op jit(solution)/shard_map/ppermute | solution.py:178
  16.1 0.0 collective-permute-done.1.refs_6_
  16.1 2.9 %collective-permute-done.2.refs_7_ = bf16[2,256,256]{2,1,0:T(8,128)(2,1)S(1)} collective-permute-done((bf16[2,256,256]{2,1,0:T(8,128)(2,1)}, bf16[2,256,256]{2,1,0:T(8,128)(2,1)S(1)}, u32[]{:S(2)}, u32[]{:S(2)}) %collective-permute-start.2) | collective-permute-done | bytes 262176 | tf_op jit(solution)/shard_map/ppermute | solution.py:178
  19.1 0.0 collective-permute-done.3.refs_8_
  19.1 0.0 copy-done.3
  19.1 0.0 copy-done.6
  19.1 0.0 copy-done.5
  19.1 3.6 %shard_map.83 = (f32[4,272,128]{2,1,0:T(8,128)S(1)}, bf16[4,272,128]{2,1,0:T(8,128)(2,1)S(1)}) custom-call(s32[8]{0:T(128)S(1)} %copy-done.6, f32[1,2]{1,0:T(1,128)S(1)} %copy-done.3, bf16[8,2,256,256]{3,2,1,0:T(8,128)(2,1)S(1)} %bitcast.6, f32[8,2,128,128]{3,2,1,0:T(8,128)S(1)} %get-tuple-element.9.refs_3_, f32[8,128]{1,0:T(8,128)S(1)} %get-tuple-element.10.refs_4_, ...), custom_call_target="tpu_custom_call" | custom-call | flops 2100000000 | bytes 5000000 | tf_op jit(solution)/shard_map/pallas_call | solution.py:189
  22.7 0.0 copy-start.4
  22.7 0.0 copy-start.1
  22.7 3.8 %collective-permute-start.4 = (bf16[4,272,128]{2,1,0:T(8,128)(2,1)S(1)}, bf16[4,272,128]{2,1,0:T(8,128)(2,1)S(1)}, u32[]{:S(2)}, u32[]{:S(2)}) collective-permute-start(bf16[4,272,128]{2,1,0:T(8,128)(2,1)S(1)} %get-tuple-element.12), channel_id=1, source_target_pairs={{0,64},{64,0},{1,65},{65,1},{2,66},{66,2},{3,67},{67,3},{4,68},{68... | collective-permute-start | bytes 835592 | tf_op jit(solution)/shard_map/ppermute | solution.py:198
  26.6 1.2 %collective-permute-done.4.theirs.received = bf16[4,272,128]{2,1,0:T(8,128)(2,1)S(1)} collective-permute-done((bf16[4,272,128]{2,1,0:T(8,128)(2,1)S(1)}, bf16[4,272,128]{2,1,0:T(8,128)(2,1)S(1)}, u32[]{:S(2)}, u32[]{:S(2)}) %collective-permute-start.4) | collective-permute-done | bytes 278560 | tf_op jit(solution)/shard_map/ppermute | solution.py:198
  27.7 0.1 shard_map.84
  27.8 16.6 %all_to_all.10.parts = bf16[4,272,128]{2,1,0:T(8,128)(2,1)S(1)} all-to-all(bf16[4,272,128]{2,1,0:T(8,128)(2,1)S(1)} %shard_map.84), channel_id=1, replica_groups=mesh['yh'=4,'core'=2,'sep'=64] {'yh'}, dimensions={0} | all-to-all | bytes 557056 | tf_op jit(solution)/shard_map/all_to_all | solution.py:200
  44.4 0.1 shard_map.85.refs_2_
  44.5 7.0 %collective-permute-start.5 = (bf16[272,128]{1,0:T(8,128)(2,1)S(1)}, bf16[272,128]{1,0:T(8,128)(2,1)S(1)}, u32[]{:S(2)}, u32[]{:S(2)}) collective-permute-start(bf16[272,128]{1,0:T(8,128)(2,1)S(1)} %shard_map.85.refs_2_), channel_id=1, source_target_pairs={{0,1},{1,2},{2,3},{3,4},{4,5},{5,6},{6,7},{7,8},{8,9},{9,10},{10,1... | collective-permute-start | bytes 208904 | tf_op jit(solution)/shard_map/ppermute | solution.py:203
  51.5 1.9 %collective-permute-start.6 = (bf16[272,128]{1,0:T(8,128)(2,1)S(1)}, bf16[272,128]{1,0:T(8,128)(2,1)S(1)}, u32[]{:S(2)}, u32[]{:S(2)}) collective-permute-start(bf16[272,128]{1,0:T(8,128)(2,1)S(1)} %shard_map.85.refs_2_), channel_id=1, source_target_pairs={{1,0},{2,1},{3,2},{4,3},{5,4},{6,5},{7,6},{8,7},{9,8},{10,9},{11,1... | collective-permute-start | bytes 208904 | tf_op jit(solution)/shard_map/ppermute | solution.py:204
  53.5 0.0 collective-permute-done.5.refs_1_
  53.5 6.4 %collective-permute-done.6.refs_3_ = bf16[272,128]{1,0:T(8,128)(2,1)S(1)} collective-permute-done((bf16[272,128]{1,0:T(8,128)(2,1)S(1)}, bf16[272,128]{1,0:T(8,128)(2,1)S(1)}, u32[]{:S(2)}, u32[]{:S(2)}) %collective-permute-start.6) | collective-permute-done | bytes 69664 | tf_op jit(solution)/shard_map/ppermute | solution.py:204
  59.9 0.0 copy-done.4
  59.9 0.6 shard_map.86
  60.5 11.9 %all_to_all.11.refs_1_ = bf16[4,208,128]{2,1,0:T(8,128)(2,1)S(1)} all-to-all(bf16[4,208,128]{2,1,0:T(8,128)(2,1)S(1)} %shard_map.86), channel_id=1, replica_groups=mesh['yh'=4,'core'=2,'sep'=64] {'yh'}, dimensions={0} | all-to-all | bytes 425984 | tf_op jit(solution)/shard_map/all_to_all | solution.py:212
  72.5 6.0 %collective-permute-start.7 = (bf16[4,208,128]{2,1,0:T(8,128)(2,1)S(1)}, bf16[4,208,128]{2,1,0:T(8,128)(2,1)S(1)}, u32[]{:S(2)}, u32[]{:S(2)}) collective-permute-start(bf16[4,208,128]{2,1,0:T(8,128)(2,1)S(1)} %all_to_all.11.refs_1_), channel_id=1, source_target_pairs={{0,64},{64,0},{1,65},{65,1},{2,66},{66,2},{3,67},{67,3},{4,68},{68... | collective-permute-start | bytes 638984 | tf_op jit(solution)/shard_map/ppermute | solution.py:213
  79.1 0.4 collective-permute-done.7.refs_2_
  79.5 0.0 copy-done.1
  79.5 1.0 %shard_map.87 = f32[1,256]{1,0:T(1,128)} custom-call(s32[1]{0:T(128)S(6)} %copy.9.refs_0_, bf16[4,208,128]{2,1,0:T(8,128)(2,1)S(1)} %all_to_all.11.refs_1_, bf16[4,208,128]{2,1,0:T(8,128)(2,1)S(1)} %collective-permute-done.7.refs_2_, bf16[6,256,256]{2,1,0:T(8,128)(2,1)S(1)} %bitcast.5), custom_call_target="tpu_custom_call" | custom-call | flops 200000000 | bytes 1300000 | tf_op jit(solution)/shard_map/pallas_call | solution.py:214
Async XLA Ops:
  0.0 19.1 %copy-start.3 = (f32[1,2]{1,0:T(1,128)S(1)}, f32[1,2]{1,0:T(1,128)}, u32[]{:S(2)}) copy-start(f32[1,2]{1,0:T(1,128)} %refs_1_.1) | copy-start | bytes 28
  0.0 19.1 %copy-start.6 = (s32[8]{0:T(128)S(1)}, s32[8]{0:T(128)}, u32[]{:S(2)}) copy-start(s32[8]{0:T(128)} %refs_0_.5) | copy-start | bytes 100
  0.0 16.1 %collective-permute-start = (bf16[2,256,256]{2,1,0:T(8,128)(2,1)}, bf16[2,256,256]{2,1,0:T(8,128)(2,1)S(1)}, u32[]{:S(2)}, u32[]{:S(2)}) collective-permute-start(bf16[2,256,256]{2,1,0:T(8,128)(2,1)} %bitcast.7), channel_id=1, source_target_pairs={{0,8},{1,9},{2,10},{3,11},{4,12},{5,13},{6,14},{7,15},{8,0},{9,1},... | collective-permute-start | bytes 786440 | tf_op jit(solution)/shard_map/ppermute | solution.py:178
  2.1 14.1 %collective-permute-start.1 = (bf16[2,256,256]{2,1,0:T(8,128)(2,1)}, bf16[2,256,256]{2,1,0:T(8,128)(2,1)S(1)}, u32[]{:S(2)}, u32[]{:S(2)}) collective-permute-start(bf16[2,256,256]{2,1,0:T(8,128)(2,1)} %bitcast.8), channel_id=1, source_target_pairs={{0,1},{1,0},{2,3},{3,2},{4,5},{5,4},{6,7},{7,6},{8,9},{9,8},{10,11... | collective-permute-start | bytes 786440 | tf_op jit(solution)/shard_map/ppermute | solution.py:178
  4.5 14.5 %collective-permute-start.2 = (bf16[2,256,256]{2,1,0:T(8,128)(2,1)}, bf16[2,256,256]{2,1,0:T(8,128)(2,1)S(1)}, u32[]{:S(2)}, u32[]{:S(2)}) collective-permute-start(bf16[2,256,256]{2,1,0:T(8,128)(2,1)} %bitcast.9), channel_id=1, source_target_pairs={{0,4},{1,5},{2,6},{3,7},{4,0},{5,1},{6,2},{7,3},{8,12},{9,13},{10,... | collective-permute-start | bytes 786440 | tf_op jit(solution)/shard_map/ppermute | solution.py:178
  6.4 12.6 %collective-permute-start.3 = (bf16[2,256,256]{2,1,0:T(8,128)(2,1)}, bf16[2,256,256]{2,1,0:T(8,128)(2,1)S(1)}, u32[]{:S(2)}, u32[]{:S(2)}) collective-permute-start(bf16[2,256,256]{2,1,0:T(8,128)(2,1)} %bitcast.10), channel_id=1, source_target_pairs={{0,2},{1,3},{2,0},{3,1},{4,6},{5,7},{6,4},{7,5},{8,10},{9,11},{10,... | collective-permute-start | bytes 786440 | tf_op jit(solution)/shard_map/ppermute | solution.py:178
  9.2 1.6 %copy-start = (bf16[1,8,2,256,256]{4,3,2,1,0:T(8,128)(2,1)S(1)}, bf16[1,8,2,256,256]{4,3,2,1,0:T(8,128)(2,1)}, u32[]{:S(2)}) copy-start(bf16[1,8,2,256,256]{4,3,2,1,0:T(8,128)(2,1)} %param.8) | copy-start | bytes 6291460
  10.8 0.7 copy-start.2
  11.4 7.6 %copy-start.5 = (bf16[1,8,2,256,256]{4,3,2,1,0:T(8,128)(2,1)S(1)}, bf16[1,8,2,256,256]{4,3,2,1,0:T(8,128)(2,1)}, u32[]{:S(2)}) copy-start(bf16[1,8,2,256,256]{4,3,2,1,0:T(8,128)(2,1)} %param.9) | copy-start | bytes 6291460
  22.7 37.2 %copy-start.4 = (s32[1,6]{1,0:T(1,128)S(1)}, s32[1,6]{1,0:T(1,128)}, u32[]{:S(2)}) copy-start(s32[1,6]{1,0:T(1,128)} %refs_0_.6) | copy-start | bytes 76
  22.7 56.8 %copy-start.1 = (bf16[1,6,256,256]{3,2,1,0:T(8,128)(2,1)S(1)}, bf16[1,6,256,256]{3,2,1,0:T(8,128)(2,1)}, u32[]{:S(2)}) copy-start(bf16[1,6,256,256]{3,2,1,0:T(8,128)(2,1)} %param.15) | copy-start | bytes 2359300
  22.7 5.0 %collective-permute-start.4 = (bf16[4,272,128]{2,1,0:T(8,128)(2,1)S(1)}, bf16[4,272,128]{2,1,0:T(8,128)(2,1)S(1)}, u32[]{:S(2)}, u32[]{:S(2)}) collective-permute-start(bf16[4,272,128]{2,1,0:T(8,128)(2,1)S(1)} %get-tuple-element.12), channel_id=1, source_target_pairs={{0,64},{64,0},{1,65},{65,1},{2,66},{66,2},{3,67},{67,3},{4,68},{68... | collective-permute-start | bytes 835592 | tf_op jit(solution)/shard_map/ppermute | solution.py:198
  44.5 9.0 %collective-permute-start.5 = (bf16[272,128]{1,0:T(8,128)(2,1)S(1)}, bf16[272,128]{1,0:T(8,128)(2,1)S(1)}, u32[]{:S(2)}, u32[]{:S(2)}) collective-permute-start(bf16[272,128]{1,0:T(8,128)(2,1)S(1)} %shard_map.85.refs_2_), channel_id=1, source_target_pairs={{0,1},{1,2},{2,3},{3,4},{4,5},{5,6},{6,7},{7,8},{8,9},{9,10},{10,1... | collective-permute-start | bytes 208904 | tf_op jit(solution)/shard_map/ppermute | solution.py:203
  51.5 8.4 %collective-permute-start.6 = (bf16[272,128]{1,0:T(8,128)(2,1)S(1)}, bf16[272,128]{1,0:T(8,128)(2,1)S(1)}, u32[]{:S(2)}, u32[]{:S(2)}) collective-permute-start(bf16[272,128]{1,0:T(8,128)(2,1)S(1)} %shard_map.85.refs_2_), channel_id=1, source_target_pairs={{1,0},{2,1},{3,2},{4,3},{5,4},{6,5},{7,6},{8,7},{9,8},{10,9},{11,1... | collective-permute-start | bytes 208904 | tf_op jit(solution)/shard_map/ppermute | solution.py:204
  72.5 7.1 %collective-permute-start.7 = (bf16[4,208,128]{2,1,0:T(8,128)(2,1)S(1)}, bf16[4,208,128]{2,1,0:T(8,128)(2,1)S(1)}, u32[]{:S(2)}, u32[]{:S(2)}) collective-permute-start(bf16[4,208,128]{2,1,0:T(8,128)(2,1)S(1)} %all_to_all.11.refs_1_), channel_id=1, source_target_pairs={{0,64},{64,0},{1,65},{65,1},{2,66},{66,2},{3,67},{67,3},{4,68},{68... | collective-permute-start | bytes 638984 | tf_op jit(solution)/shard_map/ppermute | solution.py:213
